TPU v7x, 512 devices: a whole 4x4x16 slice. The times are simulated.
512 devices in a mesh: cluster: 16 (over z), vector: 8 (over y, core), replica: 4 (over x).
Axes of the slice: x: 4, y: 4, z: 16, core: 2. Of those that a mesh axis runs over, the one named last changes fastest.
Arguments:
- samples: bfloat16 [128, 524288], P('vector', ('cluster', 'replica')), may hold values from -6 to 6
- leaf_basis_matrix: bfloat16 [32, 64, 8192], P(None, None, ('cluster', 'replica')), may hold values from -0.75 to 0.75
- transfer: bfloat16 [32, 32, 8192], P(None, None, ('cluster', 'replica')), may hold values from -0.75 to 0.75
- leaf_lists: int32 [4, 8192], P(None, ('cluster', 'replica')), may hold values from 0 to 8191, as said below
- leaf_coupling: bfloat16 [32, 32, 4, 8192], P(None, None, None, ('cluster', 'replica')), may hold values from -0.5 to 0.5
- parent_lists: int32 [4, 4096], P(None, ('cluster', 'replica')), may hold values from 0 to 4095, as said below
- parent_coupling: bfloat16 [32, 32, 4, 4096], P(None, None, None, ('cluster', 'replica')), may hold values from -0.5 to 0.5
- test_matrix: bfloat16 [128, 32], P('vector'), may hold values from -0.5 to 0.5
Outputs:
- product: bfloat16 [128, 524288], P('vector', ('cluster', 'replica'))
- new_basis: float32 [64, 32, 8192], P(None, None, ('cluster', 'replica'))
- fresh_transfer_sketch: float32 [32, 32, 8192], P(None, None, ('cluster', 'replica'))
Inputs may be any that keep to these rules, and one draw needn't show every extreme that they name: `leaf_lists`: every source leaf lies within 128 leaves of its target leaf, and some source lies exactly 128 leaves away. `parent_lists`: every source parent lies within half of 128 parents of its target parent, and some source lies exactly that far away.
All inputs are finite; a program needn't handle non-finite values.
Results may differ from a plain program's by a relative error of at most 0.0062.
Values may be sent and summed in bfloat16 or wider, within the bound.
No kernel may reach another device: no remote copies, remote signals or barrier semaphores. Data moves between devices by JAX's collectives and lax.ppermute only.
A program may use at most 64 MiB of HBM per device.

v0:
```python
import jax
import jax.numpy as jnp
from jax import lax
from jax.sharding import PartitionSpec as P


def extended_2(array, sides, width):
    edges = {}
    for axis, dim in sides:
        peers, length = (lax.axis_size(axis), array.shape[dim])
        up = [(i, (i + 1) % peers) for i in range(peers - 1)]
        last = lax.slice_in_dim(array, length - width, length, axis=dim)
        leading = lax.slice_in_dim(array, 0, width, axis=dim)
        edges[dim] = (
            lax.ppermute(last, axis, up),
            lax.ppermute(leading, axis, [(b, a) for a, b in up]),
        )
    done = []
    for _, dim in sides:
        low, high = edges[dim]
        around = [(width, width) if d in done else (0, 0) for d in range(array.ndim)]
        array = jnp.concatenate([jnp.pad(low, around), array, jnp.pad(high, around)], axis=dim)
        done.append(dim)
    return array


def in_order(parts, dim):
    parts = jnp.moveaxis(parts, 0, dim)
    shape = parts.shape
    return parts.reshape(*shape[:dim], shape[dim] * shape[dim + 1], *shape[dim + 2 :])


def sent_to_all(array, axis):
    peers = lax.axis_size(axis)
    return lax.all_to_all(
        jnp.broadcast_to(array[None], (peers, *array.shape)), axis, 0, 0, tiled=True
    )


def gathered_copies(array, axis, dim):
    return in_order(sent_to_all(array, axis), dim)


def in_one_piece(arrays, axis, dim, along):
    both = jnp.concatenate(arrays, axis=along)
    out, at, finished = (gathered_copies(both, axis, dim), 0, [])
    for a in arrays:
        finished.append(lax.slice_in_dim(out, at, at + a.shape[along], axis=along))
        at += a.shape[along]
    return tuple(finished)


def finish_basis(sketch, width):
    scale = lax.rsqrt(jnp.mean(sketch * sketch, axis=0, keepdims=True) + 1e-06)
    new_basis = sketch * scale
    fresh_transfer_sketch = (
        jnp.einsum("pal,pbl->abl", new_basis, sketch, precision=lax.Precision.HIGHEST) / width
    )
    return (new_basis, fresh_transfer_sketch)


def near_take(extended, lists, count):
    first = lax.axis_index(("cluster", "replica")) * count - count
    local_index = lists - first
    return jnp.take(extended, local_index, axis=2)


def shards(
    samples,
    leaf_basis_matrix,
    transfer,
    leaf_lists,
    leaf_coupling,
    parent_lists,
    parent_coupling,
    test_matrix,
):
    rank, width, leaves = leaf_basis_matrix.shape
    vec_local = samples.shape[0]
    each_leaf_amount = samples.reshape(vec_local, leaves, width)
    leaf_coeff = jnp.einsum(
        "rpl,vlp->rvl", leaf_basis_matrix, each_leaf_amount, preferred_element_type=jnp.float32
    ).astype(jnp.bfloat16)
    pairs = transfer.reshape(rank, rank, leaves // 2, 2)
    children = leaf_coeff.reshape(rank, vec_local, leaves // 2, 2)
    parent_coeff = jnp.einsum(
        "abqc,avqc->bvq", pairs, children, preferred_element_type=jnp.float32
    ).astype(jnp.bfloat16)
    leaf_ext = extended_2(leaf_coeff, ((("cluster", "replica"), 2),), leaves)
    leaf_src = near_take(leaf_ext, leaf_lists, leaves)
    parent_ext = extended_2(parent_coeff, ((("cluster", "replica"), 2),), leaves // 2)
    parent_src = near_take(parent_ext, parent_lists, leaves // 2)
    leaf_far = jnp.einsum(
        "rskt,svkt->rvt", leaf_coupling, leaf_src, preferred_element_type=jnp.float32
    )
    parent_far = jnp.einsum(
        "rskq,svkq->rvq", parent_coupling, parent_src, preferred_element_type=jnp.float32
    )
    descend = jnp.einsum(
        "abqc,bvq->avqc", pairs.astype(jnp.float32), parent_far, precision=lax.Precision.HIGHEST
    )
    leaf_count_total = (leaf_far + descend.reshape(rank, vec_local, leaves)).astype(jnp.bfloat16)
    product = jnp.einsum(
        "etw,ebw->bwt", leaf_basis_matrix, leaf_count_total, preferred_element_type=jnp.float32
    ).astype(jnp.bfloat16)
    moved = lax.all_to_all(product, "vector", split_axis=1, concat_axis=0, tiled=True)
    whole_test = gathered_copies(test_matrix, "vector", 0)
    sketch = jnp.einsum("vlp,vr->prl", moved, whole_test, preferred_element_type=jnp.float32)
    shared_basis_rows, shared_transfer_rows = finish_basis(sketch, width)
    new_basis, fresh_transfer_sketch = in_one_piece(
        (shared_basis_rows, shared_transfer_rows), "vector", 2, 0
    )
    return (product.reshape(vec_local, leaves * width), new_basis, fresh_transfer_sketch)


def solution(mesh):
    placed = (
        P("vector", ("cluster", "replica")),
        P(None, None, ("cluster", "replica")),
        P(None, None, ("cluster", "replica")),
        P(None, ("cluster", "replica")),
        P(None, None, None, ("cluster", "replica")),
        P(None, ("cluster", "replica")),
        P(None, None, None, ("cluster", "replica")),
        P("vector", None),
    )
    return jax.shard_map(
        shards,
        mesh=mesh,
        in_specs=placed,
        out_specs=(
            P("vector", ("cluster", "replica")),
            P(None, None, ("cluster", "replica")),
            P(None, None, ("cluster", "replica")),
        ),
        check_vma=False,
    )
```

profile of v0, /device:TPU:128, one launch (start us, length us, event | category | flops | bytes accessed | tf_op | source)
XLA Modules:
  0.0 124.2 jit_solution(8063657740272689346)
XLA Ops:
  0.6 0.0 copy-start.3
  0.6 2.5 %copy.69 = bf16[32,64,128]{1,0,2:T(8,128)(2,1)S(1)} copy(bf16[32,64,128]{2,1,0:T(8,128)(2,1)} %param.9) | data formatting | bytes 1048576 | tf_op args[1]
  3.1 1.5 %reshape.45 = bf16[16,128,64]{2,1,0:T(8,128)(2,1)S(1)} reshape(bf16[16,8192]{1,0:T(8,128)(2,1)} %param.8) | data formatting | bytes 524288 | tf_op jit(solution)/shard_map/reshape | solution.py:80
  4.6 0.0 copy-done.3
  4.6 1.4 %copy.71 = bf16[32,32,128]{1,0,2:T(8,128)(2,1)S(1)} copy(bf16[32,32,128]{2,1,0:T(8,128)(2,1)S(1)} %copy-done.3) | data formatting | bytes 524288 | tf_op args[2]
  6.1 0.0 copy-start.6
  6.1 0.0 copy-start.5
  6.1 0.0 copy-start.7
  6.1 0.7 convolution_convert_fusion.1
  6.8 0.5 fusion.18
  7.2 0.0 copy-start.2
  7.2 3.4 %collective-permute-start.2 = (bf16[32,16,64]{0,1,2:T(8,128)(2,1)S(1)}, bf16[32,16,64]{0,1,2:T(8,128)(2,1)S(1)}, u32[]{:S(2)}, u32[]{:S(2)}) collective-permute-start(bf16[32,16,64]{0,1,2:T(8,128)(2,1)S(1)} %fusion.18), channel_id=1, source_target_pairs={{0,1},{1,2},{2,3},{3,32},{32,33},{33,34},{34,35},{35,64},{64,65},{... | collective-permute-start | bytes 196616 | tf_op jit(solution)/shard_map/ppermute | solution.py:15
  10.7 5.8 %collective-permute-start.3 = (bf16[32,16,64]{0,1,2:T(8,128)(2,1)S(1)}, bf16[32,16,64]{0,1,2:T(8,128)(2,1)}, u32[]{:S(2)}, u32[]{:S(2)}) collective-permute-start(bf16[32,16,64]{0,1,2:T(8,128)(2,1)S(1)} %fusion.18), channel_id=1, source_target_pairs={{1,0},{2,1},{3,2},{32,3},{33,32},{34,33},{35,34},{64,35},{65,64},{... | collective-permute-start | bytes 196616 | tf_op jit(solution)/shard_map/ppermute | solution.py:16
  16.4 1.9 %collective-permute-start = (bf16[32,16,128]{0,1,2:T(8,128)(2,1)S(1)}, bf16[32,16,128]{0,1,2:T(8,128)(2,1)}, u32[]{:S(2)}, u32[]{:S(2)}) collective-permute-start(bf16[32,16,128]{0,1,2:T(8,128)(2,1)S(1)} %bitcast.94), channel_id=1, source_target_pairs={{0,1},{1,2},{2,3},{3,32},{32,33},{33,34},{34,35},{35,64},{64,65},{... | collective-permute-start | bytes 393224 | tf_op jit(solution)/shard_map/ppermute | solution.py:15
  18.4 7.2 %collective-permute-start.1 = (bf16[32,16,128]{0,1,2:T(8,128)(2,1)S(1)}, bf16[32,16,128]{0,1,2:T(8,128)(2,1)}, u32[]{:S(2)}, u32[]{:S(2)}) collective-permute-start(bf16[32,16,128]{0,1,2:T(8,128)(2,1)S(1)} %bitcast.95), channel_id=1, source_target_pairs={{1,0},{2,1},{3,2},{32,3},{33,32},{34,33},{35,34},{64,35},{65,64},{... | collective-permute-start | bytes 393224 | tf_op jit(solution)/shard_map/ppermute | solution.py:16
  25.6 0.0 copy-done.6
  25.6 0.7 reshape.78
  26.3 4.5 %all-to-all-start.1 = ((bf16[8,2,256]{2,1,0:T(2,128)(2,1)}), bf16[8,2,256]{2,1,0:T(2,128)(2,1)S(1)}, u32[]{:S(2)}, u32[]{:S(2)}) async-start(bf16[8,2,256]{2,1,0:T(2,128)(2,1)} %reshape.78), calls=%async_computation.1 | async-start | bytes 16384 | tf_op jit(solution)/shard_map/all_to_all | solution.py:35
  30.8 0.0 copy-done.5
  30.8 0.0 copy-done.7
  30.9 0.1 reshape.60
  30.9 4.4 %copy.72 = bf16[32,32,4,64]{1,0,3,2:T(8,128)(2,1)} copy(bf16[32,32,4,64]{3,2,1,0:T(4,128)(2,1)} %param.14) | data formatting | bytes 1048576 | tf_op args[6]
  35.4 5.4 %copy.70 = bf16[32,32,4,128]{1,0,3,2:T(8,128)(2,1)} copy(bf16[32,32,4,128]{3,2,1,0:T(4,128)(2,1)} %param.12) | data formatting | bytes 2097152 | tf_op args[4]
  40.8 0.0 copy-done.2
  40.8 0.0 collective-permute-done.2
  40.8 0.0 copy-start.4
  40.8 0.7 copy-done.4
  41.5 0.0 collective-permute-done.3
  41.5 1.3 %pad_maximum_fusion.1 = bf16[32,16,192]{0,1,2:T(8,128)(2,1)S(1)} fusion(bf16[32,16,64]{0,1,2:T(8,128)(2,1)} %collective-permute-done.3, bf16[32,16,64]{0,1,2:T(8,128)(2,1)} %copy-done.2, bf16[32,16,64]{0,1,2:T(8,128)(2,1)} %copy-done.4), kind=kLoop, calls=%fused_computation.24 | loop fusion | flops 196608 | bytes 393216 | tf_op jit(solution)/shard_map/concatenate | solution.py:22
  42.8 1.8 %gather_fusion.1 = bf16[256,32,16]{1,2,0:T(8,128)(2,1)} fusion(bf16[32,16,192]{0,1,2:T(8,128)(2,1)S(1)} %pad_maximum_fusion.1, s32[1024]{0:T(1024)S(1)} %pad_clamp_fusion), kind=kCustom, calls=%fused_computation.1 | custom fusion | bytes 525312 | tf_op jit(solution)/shard_map/jit(_take)/gather | solution.py:65
  44.5 2.6 %convolution_bitcast_fusion = f32[32,16,64,1]{0,1,3,2:T(8,128)S(1)} fusion(bf16[32,32,4,64]{1,0,3,2:T(8,128)(2,1)} %copy.72, bf16[4,64,32,16]{2,3,1,0:T(8,128)(2,1)} %bitcast.99, pred[4,64]{1,0:T(4,128)(4,1)S(1)} %get-tuple-element.15), kind=kOutput, calls=%fused_computation.13 | convolution fusion | flops 8519680 | bytes 917760 | tf_op jit(solution)/shard_map/rskq,svkq->rvq/dot_general | solution.py:96
  47.2 5.2 %fusion.31 = f32[64,16,32,2]{2,1,3,0:T(8,128)} fusion(f32[32,16,64,1]{0,1,3,2:T(8,128)S(1)} %convolution_bitcast_fusion, bf16[32,32,64,2]{1,0,3,2:T(8,128)(2,1)S(1)} %bitcast.89), kind=kOutput, calls=%fused_computation.41 | convolution fusion | flops 25165824 | bytes 655360 | tf_op jit(solution)/shard_map/abqc,bvq->avqc/dot_general | solution.py:99
  52.3 0.0 collective-permute-done
  52.3 0.0 collective-permute-done.1
  52.3 2.7 %pad_maximum_fusion = bf16[32,16,384]{0,1,2:T(8,128)(2,1)} fusion(bf16[32,16,128]{0,1,2:T(8,128)(2,1)} %collective-permute-done.1, bf16[32,16,128]{0,1,2:T(8,128)(2,1)S(1)} %bitcast.96, bf16[32,16,128]{0,1,2:T(8,128)(2,1)} %collective-permute-done), kind=kLoop, calls=%fused_computation.6 | loop fusion | flops 393216 | bytes 786432 | tf_op jit(solution)/shard_map/concatenate | solution.py:22
  55.0 3.8 %gather_fusion = bf16[512,32,16]{1,2,0:T(8,128)(2,1)} fusion(bf16[32,16,384]{0,1,2:T(8,128)(2,1)} %pad_maximum_fusion, s32[1024]{0:T(1024)S(1)} %pad_clamp_fusion.1), kind=kCustom, calls=%fused_computation | custom fusion | bytes 1050624 | tf_op jit(solution)/shard_map/jit(_take)/gather | solution.py:65
  58.8 4.0 %fusion.13 = bf16[16,128,64]{2,0,1:T(8,128)(2,1)S(1)} fusion(bf16[32,64,128]{1,0,2:T(8,128)(2,1)S(1)} %copy.69, f32[32,16,128]{0,1,2:T(8,128)} %bitcast.97, bf16[32,32,4,128]{1,0,3,2:T(8,128)(2,1)} %copy.70, bf16[4,128,32,16]{2,3,1,0:T(8,128)(2,1)} %bitcast.98, pred[4,128]{1,0:T(4,128)(4,1)S(1)} %compare_and_fusion.1), kind=kOutput, calls=%fused_computation.12 | convolution fusion | flops 25690112 | bytes 2621952 | tf_op jit(solution)/shard_map/etw,ebw->bwt/dot_general | solution.py:103
  62.8 0.0 copy-start
  62.8 1.1 reshape.76
  63.9 0.0 all-to-all-done.1
  63.9 4.8 %all-to-all-start = ((bf16[8,2,8192]{2,1,0:T(2,128)(2,1)}), bf16[8,2,8192]{2,1,0:T(2,128)(2,1)S(1)}, u32[]{:S(2)}, u32[]{:S(2)}) async-start(bf16[8,2,8192]{2,1,0:T(2,128)(2,1)} %reshape.76), calls=%async_computation | async-start | bytes 524288 | tf_op jit(solution)/shard_map/all_to_all | solution.py:106
  68.7 0.1 reshape.79
  68.8 7.4 %all-to-all-done = bf16[8,2,8192]{2,1,0:T(2,128)(2,1)S(1)} async-done(((bf16[8,2,8192]{2,1,0:T(2,128)(2,1)}), bf16[8,2,8192]{2,1,0:T(2,128)(2,1)S(1)}, u32[]{:S(2)}, u32[]{:S(2)}) %all-to-all-start) | async-done | bytes 262176 | tf_op jit(solution)/shard_map/all_to_all | solution.py:106
  76.2 0.3 reshape.77
  76.5 0.4 multiply_reduce_fusion
  76.9 0.1 broadcast_multiply_fusion
  77.1 0.6 fusion.17
  77.7 0.0 copy-done
  77.7 0.1 pad_maximum_fusion.2
  77.8 0.2 copy.75
  78.0 1.5 %broadcast_in_dim.44 = f32[8,96,32,16]{1,3,2,0:T(8,128)} broadcast(f32[96,32,16]{0,2,1:T(8,128)S(1)} %copy.75), dimensions={1,2,3} | broadcast | bytes 1769472 | tf_op jit(solution)/shard_map/broadcast_in_dim | solution.py:36
  79.5 0.0 copy-start.1
  79.5 3.7 %all-to-all-start.2 = ((f32[8,96,32,16]{1,3,2,0:T(8,128)}), f32[8,96,32,16]{1,3,2,0:T(8,128)S(1)}, u32[]{:S(2)}, u32[]{:S(2)}) async-start(f32[8,96,32,16]{1,3,2,0:T(8,128)} %broadcast_in_dim.44), calls=%async_computation.2 | async-start | bytes 4194304 | tf_op jit(solution)/shard_map/all_to_all | solution.py:35
  83.3 0.0 copy-done.1
  83.3 0.1 copy.74
  83.4 1.2 reshape.49
  84.6 25.8 %all-to-all-done.2 = f32[8,96,32,16]{1,3,2,0:T(8,128)S(1)} async-done(((f32[8,96,32,16]{1,3,2,0:T(8,128)}), f32[8,96,32,16]{1,3,2,0:T(8,128)S(1)}, u32[]{:S(2)}, u32[]{:S(2)}) %all-to-all-start.2) | async-done | bytes 1572896 | tf_op jit(solution)/shard_map/all_to_all | solution.py:35
  110.4 2.0 %slice.21 = f32[32,32,8,16]{0,3,1,2:T(8,128)} slice(f32[96,32,8,16]{0,3,1,2:T(8,128)S(1)} %bitcast.86), slice={[64:96], [0:32], [0:8], [0:16]} | slice | bytes 1048576 | tf_op jit(solution)/shard_map/slice | solution.py:48
  112.3 3.9 %copy.77 = f32[32,32,8,16]{1,3,2,0:T(8,128)} copy(f32[32,32,8,16]{0,3,1,2:T(8,128)} %slice.21) | data formatting | bytes 1048576 | tf_op jit(solution)/shard_map/slice | solution.py:48
  116.2 3.0 %copy.79 = f32[32,32,128]{2,1,0:T(8,128)} copy(f32[32,32,128]{1,2,0:T(8,128)} %bitcast.90) | data formatting | bytes 1048576
  119.2 1.6 %copy.76 = f32[64,32,8,16]{0,3,2,1:T(8,128)} copy(f32[64,32,8,16]{0,3,1,2:T(8,128)S(1)} %bitcast.87) | data formatting | bytes 2097152 | tf_op jit(solution)/shard_map/slice | solution.py:48
  120.8 3.4 %copy.78 = f32[64,32,128]{2,1,0:T(8,128)} copy(f32[64,32,128]{0,2,1:T(8,128)} %bitcast.91) | data formatting | bytes 2097152
  (7 shorter events, 0.1 us)
Async XLA Ops:
  0.6 4.0 %copy-start.3 = (bf16[32,32,128]{2,1,0:T(8,128)(2,1)S(1)}, bf16[32,32,128]{2,1,0:T(8,128)(2,1)}, u32[]{:S(2)}) copy-start(bf16[32,32,128]{2,1,0:T(8,128)(2,1)} %param.10) | copy-start | bytes 786436
  6.1 19.5 %copy-start.6 = (bf16[16,32]{1,0:T(8,128)(2,1)S(1)}, bf16[16,32]{1,0:T(8,128)(2,1)}, u32[]{:S(2)}) copy-start(bf16[16,32]{1,0:T(8,128)(2,1)} %param.15) | copy-start | bytes 3076
  6.1 24.7 %copy-start.5 = (s32[4,128]{1,0:T(4,128)S(1)}, s32[4,128]{1,0:T(4,128)}, u32[]{:S(2)}) copy-start(s32[4,128]{1,0:T(4,128)} %param.11) | copy-start | bytes 6148
  6.1 24.7 %copy-start.7 = (s32[4,64]{1,0:T(4,128)S(1)}, s32[4,64]{1,0:T(4,128)}, u32[]{:S(2)}) copy-start(s32[4,64]{1,0:T(4,128)} %param.13) | copy-start | bytes 3076
  7.2 33.5 %copy-start.2 = (bf16[32,16,64]{0,1,2:T(8,128)(2,1)}, bf16[32,16,64]{0,1,2:T(8,128)(2,1)S(1)}, u32[]{:S(2)}) copy-start(bf16[32,16,64]{0,1,2:T(8,128)(2,1)S(1)} %fusion.18) | copy-start | bytes 196612
  7.2 33.5 %collective-permute-start.2 = (bf16[32,16,64]{0,1,2:T(8,128)(2,1)S(1)}, bf16[32,16,64]{0,1,2:T(8,128)(2,1)S(1)}, u32[]{:S(2)}, u32[]{:S(2)}) collective-permute-start(bf16[32,16,64]{0,1,2:T(8,128)(2,1)S(1)} %fusion.18), channel_id=1, source_target_pairs={{0,1},{1,2},{2,3},{3,32},{32,33},{33,34},{34,35},{35,64},{64,65},{... | collective-permute-start | bytes 196616 | tf_op jit(solution)/shard_map/ppermute | solution.py:15
  10.7 30.8 %collective-permute-start.3 = (bf16[32,16,64]{0,1,2:T(8,128)(2,1)S(1)}, bf16[32,16,64]{0,1,2:T(8,128)(2,1)}, u32[]{:S(2)}, u32[]{:S(2)}) collective-permute-start(bf16[32,16,64]{0,1,2:T(8,128)(2,1)S(1)} %fusion.18), channel_id=1, source_target_pairs={{1,0},{2,1},{3,2},{32,3},{33,32},{34,33},{35,34},{64,35},{65,64},{... | collective-permute-start | bytes 196616 | tf_op jit(solution)/shard_map/ppermute | solution.py:16
  16.4 35.9 %collective-permute-start = (bf16[32,16,128]{0,1,2:T(8,128)(2,1)S(1)}, bf16[32,16,128]{0,1,2:T(8,128)(2,1)}, u32[]{:S(2)}, u32[]{:S(2)}) collective-permute-start(bf16[32,16,128]{0,1,2:T(8,128)(2,1)S(1)} %bitcast.94), channel_id=1, source_target_pairs={{0,1},{1,2},{2,3},{3,32},{32,33},{33,34},{34,35},{35,64},{64,65},{... | collective-permute-start | bytes 393224 | tf_op jit(solution)/shard_map/ppermute | solution.py:15
  18.4 34.0 %collective-permute-start.1 = (bf16[32,16,128]{0,1,2:T(8,128)(2,1)S(1)}, bf16[32,16,128]{0,1,2:T(8,128)(2,1)}, u32[]{:S(2)}, u32[]{:S(2)}) collective-permute-start(bf16[32,16,128]{0,1,2:T(8,128)(2,1)S(1)} %bitcast.95), channel_id=1, source_target_pairs={{1,0},{2,1},{3,2},{32,3},{33,32},{34,33},{35,34},{64,35},{65,64},{... | collective-permute-start | bytes 393224 | tf_op jit(solution)/shard_map/ppermute | solution.py:16
  26.3 37.6 %all-to-all-start.1 = ((bf16[8,2,256]{2,1,0:T(2,128)(2,1)}), bf16[8,2,256]{2,1,0:T(2,128)(2,1)S(1)}, u32[]{:S(2)}, u32[]{:S(2)}) async-start(bf16[8,2,256]{2,1,0:T(2,128)(2,1)} %reshape.78), calls=%async_computation.1 | async-start | bytes 16384 | tf_op jit(solution)/shard_map/all_to_all | solution.py:35
  40.8 0.7 copy-start.4
  62.8 14.9 %copy-start = (bf16[16,128,64]{2,0,1:T(8,128)(2,1)}, bf16[16,128,64]{2,0,1:T(8,128)(2,1)S(1)}, u32[]{:S(2)}) copy-start(bf16[16,128,64]{2,0,1:T(8,128)(2,1)S(1)} %fusion.13) | copy-start | bytes 786436
  63.9 12.3 %all-to-all-start = ((bf16[8,2,8192]{2,1,0:T(2,128)(2,1)}), bf16[8,2,8192]{2,1,0:T(2,128)(2,1)S(1)}, u32[]{:S(2)}, u32[]{:S(2)}) async-start(bf16[8,2,8192]{2,1,0:T(2,128)(2,1)} %reshape.76), calls=%async_computation | async-start | bytes 524288 | tf_op jit(solution)/shard_map/all_to_all | solution.py:106
  79.5 3.7 %copy-start.1 = (bf16[16,128,64]{2,0,1:T(8,128)(2,1)S(1)}, bf16[16,128,64]{2,0,1:T(8,128)(2,1)}, u32[]{:S(2)}) copy-start(bf16[16,128,64]{2,0,1:T(8,128)(2,1)} %copy-done) | copy-start | bytes 786436
  79.5 30.8 %all-to-all-start.2 = ((f32[8,96,32,16]{1,3,2,0:T(8,128)}), f32[8,96,32,16]{1,3,2,0:T(8,128)S(1)}, u32[]{:S(2)}, u32[]{:S(2)}) async-start(f32[8,96,32,16]{1,3,2,0:T(8,128)} %broadcast_in_dim.44), calls=%async_computation.2 | async-start | bytes 4194304 | tf_op jit(solution)/shard_map/all_to_all | solution.py:35
where the time goes:
time: 125 us; the launch traced here: 124 us
  local copies, waits for them, and re-layouts  40.6 us (32%)
  waiting for transfers between devices  33.2 us (27%)
  starting transfers between devices  31.3 us (25%)
  matrix products  13.8 us (11%)
  other arithmetic  4.28 us (3%)
    all_to_all x2, waiting for transfers between devices, sent_to_all(): lax.all_to_all(jnp.broadcast_to(array[None], (peers, *array.shape)), axis...  25.8 us
    unnamed x26, local copies, waits for them, and re-layouts  23 us
    ppermute x2, starting transfers between devices, extended_2(): lax.ppermute(leading, axis, [(b, a) for a, b in up])  13 us
    all_to_all x2, starting transfers between devices, sent_to_all(): lax.all_to_all(jnp.broadcast_to(array[None], (peers, *array.shape)), axis...  8.2 us
    slice x3, local copies, waits for them, and re-layouts, in_one_piece(): finished.append(lax.slice_in_dim(out, at, at + a.shape[along], axis=along))  7.48 us
    all_to_all x1, waiting for transfers between devices, shards(): lax.all_to_all(product, 'vector', split_axis=1, concat_axis=0, tiled=True)  7.41 us
    gather x2, local copies, waits for them, and re-layouts, near_take(): return jnp.take(extended, local_index, axis=2)  5.56 us
    ppermute x2, starting transfers between devices, extended_2(): lax.ppermute(last, axis, up)  5.32 us
  transfers between devices with their start and end apart: 7, of which 2 were waited for; matrix products, arithmetic and copies ran while one was open for 28% of the time, Pallas kernels for 0%

commit v1 on v0

v1 whole, which is shorter than its diff:
```python
import functools

import jax
import jax.numpy as jnp
from jax import lax
from jax.experimental import pallas as pl
from jax.experimental.pallas import tpu as pltpu
from jax.sharding import PartitionSpec as P

F32, BF16 = jnp.float32, jnp.bfloat16
HOPS = ("cluster", "replica")


def iota(shape, dim):
    return lax.broadcasted_iota(jnp.int32, shape, dim)


def picked(mask):
    return jnp.where(mask, 1.0, 0.0).astype(BF16)


def dot(a, b, contract=((1,), (0,))):
    return lax.dot_general(a, b, (contract, ((), ())), preferred_element_type=F32)


def widen(src, dst, step):
    tiles = step // 8

    def body(i, _):
        rows = src[pl.ds(pl.multiple_of(i * step, step), step), :].astype(F32)
        dst[pl.ds(i * tiles, tiles)] = rows.reshape(tiles, 8, rows.shape[-1])
        return 0

    lax.fori_loop(0, src.shape[0] // step, body, 0)


def lane_product(out, left, right, blocks, block, chunks, tile_of, right_of, start=None):
    wide = right.shape[-1]

    def outer(blk, _):
        first = [blk * block + i for i in range(block)]

        def inner(chunk, acc):
            acc = list(acc)
            tiles = [tile_of(o, chunk) for o in first]
            for c in range(8):
                term = right_of(chunk, c)
                for i in range(block):
                    acc[i] = acc[i] + left[tiles[i], c : c + 1, :] * term
            return tuple(acc)

        rows = out.shape[1]
        init = tuple(
            jnp.zeros((rows, wide), F32) if start is None else start[o] for o in first
        )
        acc = lax.fori_loop(0, chunks, inner, init)
        for i, o in enumerate(first):
            out[o] = acc[i]
        return 0

    lax.fori_loop(0, blocks, outer, 0)


def coeff_kernel(samples, basis, transfer, out, basis_w, transfer_w, xj, points, leaf, parent):
    vecs = samples.shape[0]
    widen(basis, basis_w, 64)
    widen(transfer, transfer_w, 64)
    for j in range(64):
        xj[pl.ds(j * vecs, vecs), :] = samples[:, 128 * j : 128 * (j + 1)].astype(F32)
    even = picked(iota((64, 128), 1) == 2 * iota((64, 128), 0))
    odd = picked(iota((64, 128), 1) == 2 * iota((64, 128), 0) + 1)
    for v in range(vecs):
        turned = xj[pl.ds(v, 64, stride=vecs), :].T
        both = dot(turned[:64].astype(BF16), even) + dot(turned[64:].astype(BF16), odd)
        points[:, v, :] = both
    lane_product(
        leaf, basis_w, points, 4, 8, 8,
        lambda r, chunk: r * 8 + chunk,
        lambda chunk, c: points[chunk * 8 + c],
    )
    rounded = leaf[...].astype(BF16)
    out[0:512, :] = rounded.reshape(512, 128)
    leaf[...] = rounded.astype(F32)

    def outer(blk, _):
        def inner(a, acc):
            src = leaf[a]
            return tuple(
                acc[i] + transfer_w[a * 4 + blk, i : i + 1, :] * src for i in range(8)
            )

        acc = lax.fori_loop(0, 32, inner, tuple(jnp.zeros((vecs, 128), F32) for _ in range(8)))
        for i in range(8):
            parent[blk * 8 + i] = acc[i] + pltpu.roll(acc[i], 127, 1)
        return 0

    lax.fori_loop(0, 4, outer, 0)
    low = picked(iota((128, 128), 0) == 2 * iota((128, 128), 1))
    high = picked(iota((128, 128), 0) == 2 * iota((128, 128), 1) - 128)
    sums = parent[...].reshape(512, 128).astype(BF16)
    out[512:768, :] = (dot(sums[0:256], low) + dot(sums[256:512], high)).astype(BF16)


def far_kernel(
    own, before, after, leaf_lists, parent_lists, transfer, test, leaf_coupling, parent_coupling,
    out, leaf_b, parent_b, coupling_w, parent_w, transfer_w, source, far, pfar, wide, sem,
):
    copies = [
        pltpu.make_async_copy(leaf_coupling, leaf_b, sem.at[0]),
        pltpu.make_async_copy(parent_coupling, parent_b, sem.at[1]),
    ]
    for copy in copies:
        copy.start()
    place = lax.axis_index("cluster") * lax.axis_size("replica") + lax.axis_index("replica")
    widen(transfer, transfer_w, 64)

    first = place * 64 - 64
    half = iota((128, 128), 0) // 64
    row = iota((128, 128), 0) % 64
    twice = picked(iota((64, 128), 0) == iota((64, 128), 1) % 64)
    packed = jnp.concatenate([before[512:768], own[512:768], after[512:768]], axis=1)
    for k in range(4):
        index = jnp.broadcast_to(parent_lists[k : k + 1, :] - first, (64, 64))
        cols = []
        for h in range(2):
            parts = []
            for m in range(3):
                hit = dot(picked(iota((64, 64), 0) + 64 * m == index), twice).astype(BF16)
                none = jnp.zeros((64, 128), BF16)
                parts += [hit, none] if h == 0 else [none, hit]
            cols.append(jnp.concatenate(parts, axis=0))
        for h in range(2):
            got = dot(packed, cols[h])
            source[k, 16 * h : 16 * (h + 1)] = got.reshape(16, 16, 128)

    copies[1].wait()

    def pack(i, _):
        low = parent_b[pl.ds(pl.multiple_of(i * 64, 64), 64), :].astype(F32)
        high = parent_b[pl.ds(pl.multiple_of(2048 + i * 64, 64), 64), :].astype(F32)
        both = jnp.concatenate([low, high], axis=1)
        parent_w[pl.ds(i * 8, 8)] = both.reshape(8, 8, 128)
        return 0

    lax.fori_loop(0, 32, pack, 0)
    lane_product(
        pfar, parent_w, source, 2, 8, 16,
        lambda r, chunk: r * 16 + chunk,
        lambda chunk, c: source[c % 4, chunk * 2 + c // 4],
    )
    lane = iota((256, 128), 1) // 2
    flat = pfar[...].reshape(256, 128)
    wide[0:16] = jnp.take_along_axis(flat, lane, axis=1).reshape(16, 16, 128)
    wide[16:32] = jnp.take_along_axis(flat, lane + 64, axis=1).reshape(16, 16, 128)

    first = place * 128 - 128
    rows = jnp.concatenate([before[0:512], own[0:512], after[0:512]], axis=1)
    for k in range(4):
        index = jnp.broadcast_to(leaf_lists[k : k + 1, :] - first, (384, 128))
        source[k] = dot(rows, picked(iota((384, 128), 0) == index)).reshape(32, 16, 128)
    copies[0].wait()
    widen(leaf_b, coupling_w, 64)
    lane_product(
        far, coupling_w, source, 4, 8, 16,
        lambda r, chunk: r * 16 + chunk,
        lambda chunk, c: source[c % 4, chunk * 2 + c // 4],
    )
    lane_product(
        far, transfer_w, wide, 4, 8, 4,
        lambda a, chunk: a * 4 + chunk,
        lambda chunk, c: wide[chunk * 8 + c],
        start=far,
    )
    out[0:512, :] = far[...].reshape(512, 128).astype(BF16)
    pad = jnp.zeros((16, 128 - 32), BF16)
    out[512:528, :] = jnp.concatenate([test[...], pad], axis=1)


def product_kernel(total, basis, out, basis_w, total_w, grid, turned):
    widen(basis, basis_w, 64)
    total_w[...] = total[0:512, :].astype(F32).reshape(32, 16, 128)

    def outer(blk, _):
        def inner(a, acc):
            src = total_w[a]
            return tuple(acc[i] + basis_w[a * 8 + blk, i : i + 1, :] * src for i in range(8))

        acc = lax.fori_loop(0, 32, inner, tuple(jnp.zeros((16, 128), F32) for _ in range(8)))
        for i in range(8):
            grid[blk * 8 + i] = acc[i]
        return 0

    lax.fori_loop(0, 8, outer, 0)
    even = picked(iota((64, 128), 1) == 2 * iota((64, 128), 0))
    odd = picked(iota((64, 128), 1) == 2 * iota((64, 128), 0) + 1)
    none = jnp.zeros((64, 128), BF16)
    for v in range(16):
        mine = grid[:, v, :].astype(BF16)
        turned[:, v, :] = dot(even, jnp.concatenate([mine, none], axis=0), ((1,), (1,))) + dot(
            odd, jnp.concatenate([none, mine], axis=0), ((1,), (1,))
        )
    for j in range(64):
        out[:, 128 * j : 128 * (j + 1)] = turned[j].astype(BF16)


def basis_kernel(totals, basis, new_basis, fresh, basis_w, compressed, sketch, scale_w):
    groups = totals.shape[0]
    widen(basis, basis_w, 64)
    tests = jnp.concatenate([totals[g, 512:528, :] for g in range(groups)], axis=0)
    across = tests.astype(F32).T[0:32].astype(BF16)
    for a in range(32):
        rows = jnp.concatenate([totals[g, 16 * a : 16 * (a + 1), :] for g in range(groups)], axis=0)
        compressed[a] = dot(across, rows)

    def outer(blk, square):
        def inner(a, acc):
            src = compressed[a]
            return tuple(acc[i] + basis_w[a * 8 + blk, i : i + 1, :] * src for i in range(8))

        acc = lax.fori_loop(0, 32, inner, tuple(jnp.zeros((32, 128), F32) for _ in range(8)))
        for i in range(8):
            sketch[blk * 8 + i] = acc[i]
            square = square + acc[i] * acc[i]
        return square

    square = lax.fori_loop(0, 8, outer, jnp.zeros((32, 128), F32))
    scale = lax.rsqrt(square / 64 + 1e-06)
    scale_w[...] = scale

    def scaled(p, _):
        new_basis[p] = sketch[p] * scale_w[...]
        return 0

    lax.fori_loop(0, 64, scaled, 0)

    def gram(blk, _):
        base = pl.multiple_of(blk * 8, 8)

        def inner(p, acc):
            src = sketch[p]
            mine = new_basis.at[p]
            return tuple(acc[i] + mine[pl.ds(base + i, 1), :] * src for i in range(8))

        acc = lax.fori_loop(0, 64, inner, tuple(jnp.zeros((32, 128), F32) for _ in range(8)))
        for i in range(8):
            fresh[blk * 8 + i] = acc[i] * (1.0 / 64)
        return 0

    lax.fori_loop(0, 4, gram, 0)


def shards(
    samples, leaf_basis_matrix, transfer, leaf_lists, leaf_coupling, parent_lists,
    parent_coupling, test_matrix,
):
    basis = leaf_basis_matrix.reshape(2048, 128)
    moves = transfer.reshape(1024, 128)
    near = leaf_coupling.reshape(4096, 128)
    above = parent_coupling.reshape(4096, 64)
    vmem = pl.BlockSpec(memory_space=pltpu.VMEM)
    anywhere = pl.BlockSpec(memory_space=pl.ANY)

    coeff = pl.pallas_call(
        coeff_kernel,
        out_shape=jax.ShapeDtypeStruct((768, 128), BF16),
        in_specs=[vmem] * 3,
        out_specs=vmem,
        scratch_shapes=[
            pltpu.VMEM((256, 8, 128), F32),
            pltpu.VMEM((128, 8, 128), F32),
            pltpu.VMEM((1024, 128), F32),
            pltpu.VMEM((64, 16, 128), F32),
            pltpu.VMEM((32, 16, 128), F32),
            pltpu.VMEM((32, 16, 128), F32),
        ],
        name="coeff",
    )(samples, basis, moves)

    peers = lax.axis_size("cluster") * lax.axis_size("replica")
    up = [(i, (i + 1) % peers) for i in range(peers)]
    before = lax.ppermute(coeff, HOPS, up)
    after = lax.ppermute(coeff, HOPS, [(b, a) for a, b in up])

    total = pl.pallas_call(
        far_kernel,
        out_shape=jax.ShapeDtypeStruct((528, 128), BF16),
        in_specs=[vmem] * 7 + [anywhere] * 2,
        out_specs=vmem,
        scratch_shapes=[
            pltpu.VMEM((4096, 128), BF16),
            pltpu.VMEM((4096, 64), BF16),
            pltpu.VMEM((512, 8, 128), F32),
            pltpu.VMEM((256, 8, 128), F32),
            pltpu.VMEM((128, 8, 128), F32),
            pltpu.VMEM((4, 32, 16, 128), F32),
            pltpu.VMEM((32, 16, 128), F32),
            pltpu.VMEM((16, 16, 128), F32),
            pltpu.VMEM((32, 16, 128), F32),
            pltpu.SemaphoreType.DMA((2,)),
        ],
        name="far",
    )(coeff, before, after, leaf_lists, parent_lists, moves, test_matrix, near, above)

    groups = lax.axis_size("vector")
    totals = lax.all_to_all(
        jnp.broadcast_to(total[None], (groups, *total.shape)), "vector", 0, 0, tiled=True
    )

    product = pl.pallas_call(
        product_kernel,
        out_shape=jax.ShapeDtypeStruct((16, 8192), BF16),
        in_specs=[vmem] * 2,
        out_specs=vmem,
        scratch_shapes=[
            pltpu.VMEM((256, 8, 128), F32),
            pltpu.VMEM((32, 16, 128), F32),
            pltpu.VMEM((64, 16, 128), F32),
            pltpu.VMEM((64, 16, 128), F32),
        ],
        cost_estimate=pl.CostEstimate(flops=10**7, bytes_accessed=10**6, transcendentals=0),
        name="product",
    )(total, basis)

    new_basis, fresh = pl.pallas_call(
        basis_kernel,
        out_shape=(
            jax.ShapeDtypeStruct((64, 32, 128), F32),
            jax.ShapeDtypeStruct((32, 32, 128), F32),
        ),
        in_specs=[vmem] * 2,
        out_specs=(vmem, vmem),
        scratch_shapes=[
            pltpu.VMEM((256, 8, 128), F32),
            pltpu.VMEM((32, 32, 128), F32),
            pltpu.VMEM((64, 32, 128), F32),
            pltpu.VMEM((32, 128), F32),
        ],
        name="basis",
    )(totals, basis)
    return product, new_basis, fresh


def solution(mesh):
    placed = (
        P("vector", HOPS),
        P(None, None, HOPS),
        P(None, None, HOPS),
        P(None, HOPS),
        P(None, None, None, HOPS),
        P(None, HOPS),
        P(None, None, None, HOPS),
        P("vector", None),
    )
    return jax.shard_map(
        shards,
        mesh=mesh,
        in_specs=placed,
        out_specs=(P("vector", HOPS), P(None, None, HOPS), P(None, None, HOPS)),
        check_vma=False,
    )
```

time: 125 us -> 76.8 us (0.61)
  the two profiles are of different devices: /device:TPU:128 before, /device:TPU:1 now
where the time goes in v1:
time: 76.8 us; the launch traced here: 76.5 us
  Pallas kernels  36.3 us (47%)
  starting transfers between devices  22 us (29%)
  waiting for transfers between devices  13.9 us (18%)
  local copies, waits for them, and re-layouts  3.67 us (5%)
    pallas_call x1, Pallas kernels, shards(): pl.pallas_call(basis_kernel, out_shape=(jax.ShapeDtypeStruct((64, 32, 128...  13.7 us
    ppermute x1, starting transfers between devices, shards(): after = lax.ppermute(coeff, HOPS, [(b, a) for a, b in up])  12.1 us
    pallas_call x1, Pallas kernels, shards(): pl.pallas_call(far_kernel, out_shape=jax.ShapeDtypeStruct((528, 128), BF1...  11.3 us
    all_to_all x1, waiting for transfers between devices, shards(): lax.all_to_all(jnp.broadcast_to(total[None], (groups, *total.shape)), 've...  9.97 us
    all_to_all x1, starting transfers between devices, shards(): lax.all_to_all(jnp.broadcast_to(total[None], (groups, *total.shape)), 've...  6 us
    pallas_call x1, Pallas kernels, shards(): pl.pallas_call(coeff_kernel, out_shape=jax.ShapeDtypeStruct((768, 128), B...  5.94 us
    pallas_call x1, Pallas kernels, shards(): pl.pallas_call(product_kernel, out_shape=jax.ShapeDtypeStruct((16, 8192),...  5.34 us
    ppermute x1, starting transfers between devices, shards(): before = lax.ppermute(coeff, HOPS, up)  3.92 us
  transfers between devices with their start and end apart: 3, of which 3 were waited for; matrix products, arithmetic and copies ran while one was open for 0% of the time, Pallas kernels for 7%

profile of v1, /device:TPU:1, one launch (start us, length us, event | category | flops | bytes accessed | tf_op | source)
XLA Modules:
  0.0 76.5 jit_solution(839448010860035041)
XLA Ops:
  0.6 5.9 %coeff.1.own = bf16[768,128]{1,0:T(8,128)(2,1)} custom-call(bf16[16,8192]{1,0:T(8,128)(2,1)} %samples.1, bf16[2048,128]{1,0:T(8,128)(2,1)} %bitcast.4, bf16[1024,128]{1,0:T(8,128)(2,1)} %bitcast.7), custom_call_target="tpu_custom_call" | custom-call | tf_op jit(solution)/shard_map/coeff/pallas_call | solution.py:263
  6.6 3.9 %collective-permute-start = (bf16[768,128]{1,0:T(8,128)(2,1)}, bf16[768,128]{1,0:T(8,128)(2,1)S(1)}, u32[]{:S(2)}, u32[]{:S(2)}) collective-permute-start(bf16[768,128]{1,0:T(8,128)(2,1)} %coeff.1.own), channel_id=1, source_target_pairs={{0,1},{1,2},{2,3},{3,32},{32,33},{33,34},{34,35},{35,64},{64,65},{... | collective-permute-start | bytes 589832 | tf_op jit(solution)/shard_map/ppermute | solution.py:281
  10.5 12.1 %collective-permute-start.1 = (bf16[768,128]{1,0:T(8,128)(2,1)}, bf16[768,128]{1,0:T(8,128)(2,1)S(1)}, u32[]{:S(2)}, u32[]{:S(2)}) collective-permute-start(bf16[768,128]{1,0:T(8,128)(2,1)} %coeff.1.own), channel_id=1, source_target_pairs={{1,0},{2,1},{3,2},{32,3},{33,32},{34,33},{35,34},{64,35},{65,64},{... | collective-permute-start | bytes 589832 | tf_op jit(solution)/shard_map/ppermute | solution.py:282
  22.6 2.9 %collective-permute-done.before = bf16[768,128]{1,0:T(8,128)(2,1)S(1)} collective-permute-done((bf16[768,128]{1,0:T(8,128)(2,1)}, bf16[768,128]{1,0:T(8,128)(2,1)S(1)}, u32[]{:S(2)}, u32[]{:S(2)}) %collective-permute-start) | collective-permute-done | bytes 196640 | tf_op jit(solution)/shard_map/ppermute | solution.py:281
  25.5 0.0 copy-start.1
  25.5 1.0 %collective-permute-done.1.after = bf16[768,128]{1,0:T(8,128)(2,1)S(1)} collective-permute-done((bf16[768,128]{1,0:T(8,128)(2,1)}, bf16[768,128]{1,0:T(8,128)(2,1)S(1)}, u32[]{:S(2)}, u32[]{:S(2)}) %collective-permute-start.1) | collective-permute-done | bytes 196640 | tf_op jit(solution)/shard_map/ppermute | solution.py:282
  26.5 0.0 copy-start.2
  26.5 0.0 copy-done.1
  26.5 0.7 copy-done.2
  27.2 11.3 %far.1.total = bf16[528,128]{1,0:T(8,128)(2,1)} custom-call(bf16[768,128]{1,0:T(8,128)(2,1)} %coeff.1.own, bf16[768,128]{1,0:T(8,128)(2,1)} %copy-done.1, bf16[768,128]{1,0:T(8,128)(2,1)} %copy-done.2, s32[4,128]{1,0:T(4,128)} %leaf_lists.1, s32[4,64]{1,0:T(4,128)} %parent_lists.1, bf16[1024,128]{1,0:T(8,128)(2,1)} %bitcast.8, bf16[16,32]{1,0:T(8,128)(2,1)} %test.1, ...), custom_call_target="tpu_custom_call" | custom-call | tf_op jit(solution)/shard_map/far/pallas_call | solution.py:284
  38.5 2.0 %broadcast_in_dim.2 = bf16[8,528,128]{2,1,0:T(8,128)(2,1)} broadcast(bf16[528,128]{1,0:T(8,128)(2,1)} %far.1.total), dimensions={1,2} | broadcast | bytes 1216512 | tf_op jit(solution)/shard_map/broadcast_in_dim | solution.py:306
  40.5 6.0 %all-to-all-start = ((bf16[8,528,128]{2,1,0:T(8,128)(2,1)}), bf16[8,528,128]{2,1,0:T(8,128)(2,1)S(1)}, u32[]{:S(2)}, u32[]{:S(2)}) async-start(bf16[8,528,128]{2,1,0:T(8,128)(2,1)} %broadcast_in_dim.2), calls=%async_computation | async-start | bytes 2162688 | tf_op jit(solution)/shard_map/all_to_all | solution.py:305
  46.5 5.3 %product.1 = bf16[16,8192]{1,0:T(8,128)(2,1)} custom-call(bf16[528,128]{1,0:T(8,128)(2,1)} %far.1.total, bf16[2048,128]{1,0:T(8,128)(2,1)} %bitcast.5), custom_call_target="tpu_custom_call" | custom-call | flops 10000000 | bytes 1000000 | tf_op jit(solution)/shard_map/product/pallas_call | solution.py:309
  51.9 10.0 %all-to-all-done.totals = bf16[8,528,128]{2,1,0:T(8,128)(2,1)S(1)} async-done(((bf16[8,528,128]{2,1,0:T(8,128)(2,1)}), bf16[8,528,128]{2,1,0:T(8,128)(2,1)S(1)}, u32[]{:S(2)}, u32[]{:S(2)}) %all-to-all-start) | async-done | bytes 1081376 | tf_op jit(solution)/shard_map/all_to_all | solution.py:305
  61.8 0.0 copy-start
  61.8 1.0 %copy-done = bf16[8,528,128]{2,1,0:T(8,128)(2,1)} copy-done((bf16[8,528,128]{2,1,0:T(8,128)(2,1)}, bf16[8,528,128]{2,1,0:T(8,128)(2,1)S(1)}, u32[]{:S(2)}) %copy-start) | copy-done | bytes 1081368
  62.8 13.7 %basis.1 = (f32[64,32,128]{2,1,0:T(8,128)}, f32[32,32,128]{2,1,0:T(8,128)}) custom-call(bf16[8,528,128]{2,1,0:T(8,128)(2,1)} %copy-done, bf16[2048,128]{1,0:T(8,128)(2,1)} %bitcast.6), custom_call_target="tpu_custom_call" | custom-call | tf_op jit(solution)/shard_map/basis/pallas_call | solution.py:324
Async XLA Ops:
  6.6 18.9 %collective-permute-start = (bf16[768,128]{1,0:T(8,128)(2,1)}, bf16[768,128]{1,0:T(8,128)(2,1)S(1)}, u32[]{:S(2)}, u32[]{:S(2)}) collective-permute-start(bf16[768,128]{1,0:T(8,128)(2,1)} %coeff.1.own), channel_id=1, source_target_pairs={{0,1},{1,2},{2,3},{3,32},{32,33},{33,34},{34,35},{35,64},{64,65},{... | collective-permute-start | bytes 589832 | tf_op jit(solution)/shard_map/ppermute | solution.py:281
  10.5 16.0 %collective-permute-start.1 = (bf16[768,128]{1,0:T(8,128)(2,1)}, bf16[768,128]{1,0:T(8,128)(2,1)S(1)}, u32[]{:S(2)}, u32[]{:S(2)}) collective-permute-start(bf16[768,128]{1,0:T(8,128)(2,1)} %coeff.1.own), channel_id=1, source_target_pairs={{1,0},{2,1},{3,2},{32,3},{33,32},{34,33},{35,34},{64,35},{65,64},{... | collective-permute-start | bytes 589832 | tf_op jit(solution)/shard_map/ppermute | solution.py:282
  25.5 1.0 %copy-start.1 = (bf16[768,128]{1,0:T(8,128)(2,1)}, bf16[768,128]{1,0:T(8,128)(2,1)S(1)}, u32[]{:S(2)}) copy-start(bf16[768,128]{1,0:T(8,128)(2,1)S(1)} %collective-permute-done.before) | copy-start | bytes 589828
  26.5 0.7 copy-start.2
  40.5 21.3 %all-to-all-start = ((bf16[8,528,128]{2,1,0:T(8,128)(2,1)}), bf16[8,528,128]{2,1,0:T(8,128)(2,1)S(1)}, u32[]{:S(2)}, u32[]{:S(2)}) async-start(bf16[8,528,128]{2,1,0:T(8,128)(2,1)} %broadcast_in_dim.2), calls=%async_computation | async-start | bytes 2162688 | tf_op jit(solution)/shard_map/all_to_all | solution.py:305
  61.8 1.0 %copy-start = (bf16[8,528,128]{2,1,0:T(8,128)(2,1)}, bf16[8,528,128]{2,1,0:T(8,128)(2,1)S(1)}, u32[]{:S(2)}) copy-start(bf16[8,528,128]{2,1,0:T(8,128)(2,1)S(1)} %all-to-all-done.totals) | copy-start | bytes 3244036

commit v2 on v1

v2 whole, which is shorter than its diff:
```python
import jax
import jax.numpy as jnp
from jax import lax
from jax.experimental import pallas as pl
from jax.experimental.pallas import tpu as pltpu
from jax.sharding import PartitionSpec as P

F32, BF16 = jnp.float32, jnp.bfloat16
HOPS = ("cluster", "replica")


def iota(shape, dim):
    return lax.broadcasted_iota(jnp.int32, shape, dim)


def picked(mask):
    return jnp.where(mask, 1.0, 0.0).astype(BF16)


def dot(a, b, contract=((1,), (0,))):
    return lax.dot_general(a, b, (contract, ((), ())), preferred_element_type=F32)


def widen(src, dst, step=128):
    tiles = step // 8

    def body(i, _):
        rows = src[pl.ds(pl.multiple_of(i * step, step), step), :].astype(F32)
        dst[pl.ds(i * tiles, tiles)] = rows.reshape(tiles, 8, rows.shape[-1])
        return 0

    lax.fori_loop(0, src.shape[0] // step, body, 0)


def weighted(block, steps, unroll, weight, term, init):
    def body(group, acc):
        acc = list(acc)
        for u in range(unroll):
            src = term(group, u)
            for i in range(block):
                acc[i] = acc[i] + weight(i, group, u) * src
        return tuple(acc)

    return lax.fori_loop(0, steps // unroll, body, tuple(init))


def lane_product(out, left, right_of, blocks, chunks, per, tile_of, start=None, block=8):
    rows, wide = out.shape[1:]

    def outer(blk, _):
        first = [blk * block + i for i in range(block)]
        init = [jnp.zeros((rows, wide), F32) if start is None else start[o] for o in first]

        def weight(i, group, u):
            c = u % 8
            return left[tile_of(first[i], group * per + u // 8), c : c + 1, :]

        acc = weighted(
            block, chunks * 8, per * 8, weight,
            lambda group, u: right_of(group * per + u // 8, u % 8), init,
        )
        for i, o in enumerate(first):
            out[o] = acc[i]
        return 0

    lax.fori_loop(0, blocks, outer, 0)


def fetched(pairs, sem):
    copies = [pltpu.make_async_copy(a, b, sem.at[i]) for i, (a, b) in enumerate(pairs)]
    for copy in copies:
        copy.start()
    return copies


def coeff_kernel(
    samples_at, basis_at, transfer_at, out,
    samples, basis, transfer, basis_w, transfer_w, xj, points, leaf, parent, sem,
):
    copies = fetched(
        [(samples_at, samples), (basis_at, basis), (transfer_at, transfer)], sem
    )
    vecs = samples.shape[0]
    even = picked(iota((64, 128), 1) == 2 * iota((64, 128), 0))
    odd = picked(iota((64, 128), 1) == 2 * iota((64, 128), 0) + 1)
    copies[0].wait()
    for j in range(64):
        xj[pl.ds(j * vecs, vecs), :] = samples[:, 128 * j : 128 * (j + 1)].astype(F32)
    for v in range(vecs):
        turned = xj[pl.ds(v, 64, stride=vecs), :].T
        both = dot(turned[:64].astype(BF16), even) + dot(turned[64:].astype(BF16), odd)
        points[:, v, :] = both
    copies[1].wait()
    widen(basis, basis_w)
    lane_product(
        leaf, basis_w, lambda chunk, c: points[chunk * 8 + c], 4, 8, 4,
        lambda r, chunk: r * 8 + chunk,
    )
    rounded = leaf[...].astype(BF16)
    out[0:512, :] = rounded.reshape(512, 128)
    leaf[...] = rounded.astype(F32)
    copies[2].wait()
    widen(transfer, transfer_w)

    def outer(blk, _):
        acc = weighted(
            8, 32, 16,
            lambda i, group, u: transfer_w[(group * 16 + u) * 4 + blk, i : i + 1, :],
            lambda group, u: leaf[group * 16 + u],
            [jnp.zeros((vecs, 128), F32)] * 8,
        )
        for i in range(8):
            parent[blk * 8 + i] = acc[i] + pltpu.roll(acc[i], 127, 1)
        return 0

    lax.fori_loop(0, 4, outer, 0)
    low = picked(iota((128, 128), 0) == 2 * iota((128, 128), 1))
    high = picked(iota((128, 128), 0) == 2 * iota((128, 128), 1) - 128)
    sums = parent[...].reshape(512, 128).astype(BF16)
    out[512:768, :] = (dot(sums[0:256], low) + dot(sums[256:512], high)).astype(BF16)


def far_kernel(
    own_at, before_at, after_at, transfer_at, leaf_at, parent_at, leaf_lists, parent_lists, test,
    out, own, before, after, transfer, leaf_b, parent_b,
    coupling_w, parent_w, transfer_w, source, far, pfar, wide, payload, sem, sent,
):
    copies = fetched(
        [
            (own_at, own), (before_at, before), (after_at, after),
            (parent_at, parent_b), (leaf_at, leaf_b), (transfer_at, transfer),
        ],
        sem,
    )
    place = lax.axis_index("cluster") * lax.axis_size("replica") + lax.axis_index("replica")

    first = place * 64 - 64
    twice = picked(iota((64, 128), 0) == iota((64, 128), 1) % 64)
    none = jnp.zeros((64, 128), BF16)
    for copy in copies[:3]:
        copy.wait()
    packed = jnp.concatenate([before[512:768], own[512:768], after[512:768]], axis=1)
    for k in range(4):
        index = jnp.broadcast_to(parent_lists[k : k + 1, :] - first, (64, 64))
        hits = [
            dot(picked(iota((64, 64), 0) + 64 * m == index), twice).astype(BF16) for m in range(3)
        ]
        for h in range(2):
            parts = [part for hit in hits for part in ((hit, none) if h == 0 else (none, hit))]
            got = dot(packed, jnp.concatenate(parts, axis=0))
            source[k, 16 * h : 16 * (h + 1)] = got.reshape(16, 16, 128)

    copies[3].wait()

    def pack(i, _):
        low = parent_b[pl.ds(pl.multiple_of(i * 128, 128), 128), :].astype(F32)
        high = parent_b[pl.ds(pl.multiple_of(2048 + i * 128, 128), 128), :].astype(F32)
        both = jnp.concatenate([low, high], axis=1)
        parent_w[pl.ds(i * 16, 16)] = both.reshape(16, 8, 128)
        return 0

    lax.fori_loop(0, 16, pack, 0)
    lane_product(
        pfar, parent_w, lambda chunk, c: source[c % 4, chunk * 2 + c // 4], 2, 16, 4,
        lambda r, chunk: r * 16 + chunk,
    )
    lane = iota((256, 128), 1) // 2
    flat = pfar[...].reshape(256, 128)
    wide[0:16] = jnp.take_along_axis(flat, lane, axis=1).reshape(16, 16, 128)
    wide[16:32] = jnp.take_along_axis(flat, lane + 64, axis=1).reshape(16, 16, 128)

    first = place * 128 - 128
    rows = jnp.concatenate([before[0:512], own[0:512], after[0:512]], axis=1)
    for k in range(4):
        index = jnp.broadcast_to(leaf_lists[k : k + 1, :] - first, (384, 128))
        source[k] = dot(rows, picked(iota((384, 128), 0) == index)).reshape(32, 16, 128)
    copies[4].wait()
    widen(leaf_b, coupling_w)
    lane_product(
        far, coupling_w, lambda chunk, c: source[c % 4, chunk * 2 + c // 4], 4, 16, 4,
        lambda r, chunk: r * 16 + chunk,
    )
    copies[5].wait()
    widen(transfer, transfer_w)
    lane_product(
        far, transfer_w, lambda chunk, c: wide[chunk * 8 + c], 4, 4, 4,
        lambda a, chunk: a * 4 + chunk, start=far,
    )
    payload[0:512, :] = far[...].reshape(512, 128).astype(BF16)
    pad = jnp.zeros((16, 128 - 32), BF16)
    payload[512:528, :] = jnp.concatenate([test[...], pad], axis=1)
    for copy in fetched([(payload, out.at[i]) for i in range(out.shape[0])], sent):
        copy.wait()


def product_kernel(total_at, basis_at, out, total, basis, basis_w, total_w, grid, turned, sem):
    copies = fetched([(total_at.at[0], total), (basis_at, basis)], sem)
    for copy in copies:
        copy.wait()
    widen(basis, basis_w)
    total_w[...] = total[0:512, :].astype(F32).reshape(32, 16, 128)

    def outer(blk, _):
        acc = weighted(
            8, 32, 16,
            lambda i, group, u: basis_w[(group * 16 + u) * 8 + blk, i : i + 1, :],
            lambda group, u: total_w[group * 16 + u],
            [jnp.zeros((16, 128), F32)] * 8,
        )
        for i in range(8):
            grid[blk * 8 + i] = acc[i]
        return 0

    lax.fori_loop(0, 8, outer, 0)
    even = picked(iota((64, 128), 1) == 2 * iota((64, 128), 0))
    odd = picked(iota((64, 128), 1) == 2 * iota((64, 128), 0) + 1)
    none = jnp.zeros((64, 128), BF16)
    for v in range(16):
        mine = grid[:, v, :].astype(BF16)
        turned[:, v, :] = dot(even, jnp.concatenate([mine, none], axis=0), ((1,), (1,))) + dot(
            odd, jnp.concatenate([none, mine], axis=0), ((1,), (1,))
        )
    for j in range(64):
        out[:, 128 * j : 128 * (j + 1)] = turned[j].astype(BF16)


def basis_kernel(
    mine_at, theirs_at, basis_at, new_at, fresh_at,
    totals, basis, basis_w, compressed, sketch, scale_w, gram, new_basis, fresh, sem, sent,
):
    groups = totals.shape[0]
    half = mine_at.shape[0]
    copies = fetched(
        [(basis_at, basis), (mine_at, totals.at[0:half]), (theirs_at, totals.at[half:groups])], sem
    )
    copies[0].wait()
    widen(basis, basis_w)
    for copy in copies[1:]:
        copy.wait()
    tests = jnp.concatenate([totals[g, 512:528, :] for g in range(groups)], axis=0)
    across = tests.astype(F32).T[0:32].astype(BF16)
    for a in range(32):
        rows = jnp.concatenate([totals[g, 16 * a : 16 * (a + 1), :] for g in range(groups)], axis=0)
        compressed[a] = dot(across, rows)

    scale_w[...] = jnp.zeros((32, 128), F32)

    def outer(blk, _):
        acc = weighted(
            8, 32, 16,
            lambda i, group, u: basis_w[(group * 16 + u) * 8 + blk, i : i + 1, :],
            lambda group, u: compressed[group * 16 + u],
            [jnp.zeros((32, 128), F32)] * 8,
        )
        square = scale_w[...]
        for i in range(8):
            sketch[blk * 8 + i] = acc[i]
            square = square + acc[i] * acc[i]
        scale_w[...] = square
        return 0

    lax.fori_loop(0, 8, outer, 0)
    scale_w[...] = lax.rsqrt(scale_w[...] / 64 + 1e-06)

    def scaled(group, _):
        scale = scale_w[...]
        for u in range(8):
            new_basis[group * 8 + u] = sketch[group * 8 + u] * scale
        return 0

    lax.fori_loop(0, 8, scaled, 0)
    first = fetched([(new_basis, new_at)], sent)

    for tile in range(4):
        low = 8 * tile
        acc = weighted(
            8, 64, 16,
            lambda i, group, u: sketch[group * 16 + u, low + i : low + i + 1, :],
            lambda group, u: sketch[group * 16 + u, low:32, :],
            [jnp.zeros((32 - low, 128), F32)] * 8,
        )
        for i in range(8):
            gram[(low + i) * 32 + low : (low + i) * 32 + 32, :] = acc[i]
    for a in range(32):
        row = scale_w[a : a + 1, :] * (1.0 / 64)
        low = a // 8 * 8
        fresh[a, low:32, :] = gram[a * 32 + low : a * 32 + 32, :] * row
        for b in range(0, low, 8):
            fresh[a, b : b + 8, :] = gram[pl.ds(b * 32 + a, 8, stride=32), :] * row
    second = pltpu.make_async_copy(fresh, fresh_at, sent.at[1])
    second.start()
    first[0].wait()
    second.wait()


def shards(
    samples, leaf_basis_matrix, transfer, leaf_lists, leaf_coupling, parent_lists,
    parent_coupling, test_matrix,
):
    basis = leaf_basis_matrix.reshape(2048, 128)
    moves = transfer.reshape(1024, 128)
    near = leaf_coupling.reshape(4096, 128)
    above = parent_coupling.reshape(4096, 64)
    vmem = pl.BlockSpec(memory_space=pltpu.VMEM)
    anywhere = pl.BlockSpec(memory_space=pl.ANY)

    coeff = pl.pallas_call(
        coeff_kernel,
        out_shape=jax.ShapeDtypeStruct((768, 128), BF16),
        in_specs=[anywhere] * 3,
        out_specs=vmem,
        scratch_shapes=[
            pltpu.VMEM((16, 8192), BF16),
            pltpu.VMEM((2048, 128), BF16),
            pltpu.VMEM((1024, 128), BF16),
            pltpu.VMEM((256, 8, 128), F32),
            pltpu.VMEM((128, 8, 128), F32),
            pltpu.VMEM((1024, 128), F32),
            pltpu.VMEM((64, 16, 128), F32),
            pltpu.VMEM((32, 16, 128), F32),
            pltpu.VMEM((32, 16, 128), F32),
            pltpu.SemaphoreType.DMA((3,)),
        ],
        name="coeff",
    )(samples, basis, moves)

    peers = lax.axis_size("cluster") * lax.axis_size("replica")
    up = [(i, i + 1) for i in range(peers - 1)]
    before = lax.ppermute(coeff, HOPS, up)
    after = lax.ppermute(coeff, HOPS, [(b, a) for a, b in up])

    groups = lax.axis_size("vector")
    half = groups // 2
    total = pl.pallas_call(
        far_kernel,
        out_shape=jax.ShapeDtypeStruct((half, 528, 128), BF16),
        in_specs=[anywhere] * 6 + [vmem] * 3,
        out_specs=anywhere,
        scratch_shapes=[
            pltpu.VMEM((768, 128), BF16),
            pltpu.VMEM((768, 128), BF16),
            pltpu.VMEM((768, 128), BF16),
            pltpu.VMEM((1024, 128), BF16),
            pltpu.VMEM((4096, 128), BF16),
            pltpu.VMEM((4096, 64), BF16),
            pltpu.VMEM((512, 8, 128), F32),
            pltpu.VMEM((256, 8, 128), F32),
            pltpu.VMEM((128, 8, 128), F32),
            pltpu.VMEM((4, 32, 16, 128), F32),
            pltpu.VMEM((32, 16, 128), F32),
            pltpu.VMEM((16, 16, 128), F32),
            pltpu.VMEM((32, 16, 128), F32),
            pltpu.VMEM((528, 128), BF16),
            pltpu.SemaphoreType.DMA((6,)),
            pltpu.SemaphoreType.DMA((half,)),
        ],
        name="far",
    )(coeff, before, after, moves, near, above, leaf_lists, parent_lists, test_matrix)

    cores = [[2 * y + core for y in range(half)] for core in range(2)]
    mine = lax.all_to_all(total, "vector", 0, 0, tiled=True, axis_index_groups=cores)
    theirs = lax.ppermute(mine, "vector", [(i, i ^ 1) for i in range(groups)])

    product = pl.pallas_call(
        product_kernel,
        out_shape=jax.ShapeDtypeStruct((16, 8192), BF16),
        in_specs=[anywhere] * 2,
        out_specs=vmem,
        scratch_shapes=[
            pltpu.VMEM((528, 128), BF16),
            pltpu.VMEM((2048, 128), BF16),
            pltpu.VMEM((256, 8, 128), F32),
            pltpu.VMEM((32, 16, 128), F32),
            pltpu.VMEM((64, 16, 128), F32),
            pltpu.VMEM((64, 16, 128), F32),
            pltpu.SemaphoreType.DMA((2,)),
        ],
        cost_estimate=pl.CostEstimate(flops=10**7, bytes_accessed=10**6, transcendentals=0),
        name="product",
    )(total, basis)

    new_basis, fresh = pl.pallas_call(
        basis_kernel,
        out_shape=(
            jax.ShapeDtypeStruct((64, 32, 128), F32),
            jax.ShapeDtypeStruct((32, 32, 128), F32),
        ),
        in_specs=[anywhere] * 3,
        out_specs=(anywhere, anywhere),
        scratch_shapes=[
            pltpu.VMEM((groups, 528, 128), BF16),
            pltpu.VMEM((2048, 128), BF16),
            pltpu.VMEM((256, 8, 128), F32),
            pltpu.VMEM((32, 32, 128), F32),
            pltpu.VMEM((64, 32, 128), F32),
            pltpu.VMEM((32, 128), F32),
            pltpu.VMEM((1024, 128), F32),
            pltpu.VMEM((64, 32, 128), F32),
            pltpu.VMEM((32, 32, 128), F32),
            pltpu.SemaphoreType.DMA((3,)),
            pltpu.SemaphoreType.DMA((2,)),
        ],
        name="basis",
    )(mine, theirs, basis)
    return product, new_basis, fresh


def solution(mesh):
    placed = (
        P("vector", HOPS),
        P(None, None, HOPS),
        P(None, None, HOPS),
        P(None, HOPS),
        P(None, None, None, HOPS),
        P(None, HOPS),
        P(None, None, None, HOPS),
        P("vector", None),
    )
    return jax.shard_map(
        shards,
        mesh=mesh,
        in_specs=placed,
        out_specs=(P("vector", HOPS), P(None, None, HOPS), P(None, None, HOPS)),
        check_vma=False,
    )
```

time: 76.8 us -> 62 us (0.81)
  the two profiles are of different devices: /device:TPU:1 before, /device:TPU:385 now
where the time goes in v2:
time: 62 us; the launch traced here: 61.6 us
  Pallas kernels  25.8 us (42%)
  starting transfers between devices  13.1 us (21%)
  blocking collectives  11.6 us (19%)
  waiting for transfers between devices  9 us (15%)
  local copies, waits for them, and re-layouts  1.47 us (2%)
  between operations  0.71 us (1%)
    all_to_all x1, blocking collectives, shards(): lax.all_to_all(total, 'vector', 0, 0, tiled=True, axis_index_groups=cores)  11.6 us
    pallas_call x1, Pallas kernels, shards(): pl.pallas_call(far_kernel, out_shape=jax.ShapeDtypeStruct((half, 528, 128...  10.1 us
    ppermute x1, waiting for transfers between devices, shards(): before = lax.ppermute(coeff, HOPS, up)  7.05 us
    pallas_call x1, Pallas kernels, shards(): pl.pallas_call(basis_kernel, out_shape=(jax.ShapeDtypeStruct((64, 32, 128...  6.81 us
    ppermute x1, starting transfers between devices, shards(): after = lax.ppermute(coeff, HOPS, [(b, a) for a, b in up])  6.04 us
    ppermute x1, starting transfers between devices, shards(): theirs = lax.ppermute(mine, 'vector', [(i, i ^ 1) for i in range(groups)])  5.13 us
    pallas_call x1, Pallas kernels, shards(): pl.pallas_call(coeff_kernel, out_shape=jax.ShapeDtypeStruct((768, 128), B...  4.69 us
    pallas_call x1, Pallas kernels, shards(): pl.pallas_call(product_kernel, out_shape=jax.ShapeDtypeStruct((16, 8192),...  4.16 us
  transfers between devices with their start and end apart: 3, of which 2 were waited for; matrix products, arithmetic and copies ran while one was open for 0% of the time, Pallas kernels for 7%

profile of v2, /device:TPU:385, one launch (start us, length us, event | category | flops | bytes accessed | tf_op | source)
XLA Modules:
  0.0 61.6 jit_solution(13260800301975872767)
XLA Ops:
  0.6 4.7 %coeff.1.own_at = bf16[768,128]{1,0:T(8,128)(2,1)} custom-call(bf16[16,8192]{1,0:T(8,128)(2,1)} %samples_at.1, bf16[2048,128]{1,0:T(8,128)(2,1)} %bitcast.4, bf16[1024,128]{1,0:T(8,128)(2,1)} %bitcast.9), custom_call_target="tpu_custom_call" | custom-call | tf_op jit(solution)/shard_map/coeff/pallas_call | solution.py:307
  5.3 6.0 %collective-permute-start.1 = (bf16[768,128]{1,0:T(8,128)(2,1)}, bf16[768,128]{1,0:T(8,128)(2,1)S(1)}, u32[]{:S(2)}, u32[]{:S(2)}) collective-permute-start(bf16[768,128]{1,0:T(8,128)(2,1)} %coeff.1.own_at), channel_id=1, source_target_pairs={{1,0},{2,1},{3,2},{32,3},{33,32},{34,33},{35,34},{64,35},{65,64},{... | collective-permute-start | bytes 589832 | tf_op jit(solution)/shard_map/ppermute | solution.py:330
  11.4 1.9 %collective-permute-start = (bf16[768,128]{1,0:T(8,128)(2,1)}, bf16[768,128]{1,0:T(8,128)(2,1)S(1)}, u32[]{:S(2)}, u32[]{:S(2)}) collective-permute-start(bf16[768,128]{1,0:T(8,128)(2,1)} %coeff.1.own_at), channel_id=1, source_target_pairs={{0,1},{1,2},{2,3},{3,32},{32,33},{33,34},{34,35},{35,64},{64,65},{... | collective-permute-start | bytes 589832 | tf_op jit(solution)/shard_map/ppermute | solution.py:329
  13.3 1.9 %collective-permute-done.1.after_at = bf16[768,128]{1,0:T(8,128)(2,1)S(1)} collective-permute-done((bf16[768,128]{1,0:T(8,128)(2,1)}, bf16[768,128]{1,0:T(8,128)(2,1)S(1)}, u32[]{:S(2)}, u32[]{:S(2)}) %collective-permute-start.1) | collective-permute-done | bytes 196640 | tf_op jit(solution)/shard_map/ppermute | solution.py:330
  15.2 0.0 copy-start.2
  15.3 7.0 %collective-permute-done.before_at = bf16[768,128]{1,0:T(8,128)(2,1)S(1)} collective-permute-done((bf16[768,128]{1,0:T(8,128)(2,1)}, bf16[768,128]{1,0:T(8,128)(2,1)S(1)}, u32[]{:S(2)}, u32[]{:S(2)}) %collective-permute-start) | collective-permute-done | bytes 196640 | tf_op jit(solution)/shard_map/ppermute | solution.py:329
  22.3 0.0 copy-start.3
  22.3 0.0 copy-done.2
  22.3 0.7 %copy-done.3 = bf16[768,128]{1,0:T(8,128)(2,1)} copy-done((bf16[768,128]{1,0:T(8,128)(2,1)}, bf16[768,128]{1,0:T(8,128)(2,1)S(1)}, u32[]{:S(2)}) %copy-start.3) | copy-done | bytes 196632
  23.0 10.1 %far.1.total_at = bf16[4,528,128]{2,1,0:T(8,128)(2,1)} custom-call(bf16[768,128]{1,0:T(8,128)(2,1)} %coeff.1.own_at, bf16[768,128]{1,0:T(8,128)(2,1)} %copy-done.3, bf16[768,128]{1,0:T(8,128)(2,1)} %copy-done.2, bf16[1024,128]{1,0:T(8,128)(2,1)} %bitcast.10, bf16[4096,128]{1,0:T(8,128)(2,1)} %bitcast.7, bf16[4096,64]{1,0:T(8,128)(2,1)} %bitcast.8, ...), custom_call_target="tpu_custom_call" | custom-call | tf_op jit(solution)/shard_map/far/pallas_call | solution.py:334
  33.1 11.6 %all_to_all.5.mine_at = bf16[4,528,128]{2,1,0:T(8,128)(2,1)S(1)} all-to-all(bf16[4,528,128]{2,1,0:T(8,128)(2,1)} %far.1.total_at), channel_id=1, replica_groups={{0,8,16,24},{4,12,20,28},{1,9,17,25},{5,13,21,29},{2,10,18,26},{6,14,22..., dimensions={0} | all-to-all | bytes 1081344 | tf_op jit(solution)/shard_map/all_to_all | solution.py:361
  44.7 0.0 copy-start
  44.7 5.1 %collective-permute-start.2 = (bf16[4,528,128]{2,1,0:T(8,128)(2,1)S(1)}, bf16[4,528,128]{2,1,0:T(8,128)(2,1)S(1)}, u32[]{:S(2)}, u32[]{:S(2)}) collective-permute-start(bf16[4,528,128]{2,1,0:T(8,128)(2,1)S(1)} %all_to_all.5.mine_at), channel_id=1, source_target_pairs={{0,4},{4,0},{8,12},{12,8},{16,20},{20,16},{24,28},{28,24},{1,5},{5... | collective-permute-start | bytes 1622024 | tf_op jit(solution)/shard_map/ppermute | solution.py:362
  49.8 4.2 %product.1 = bf16[16,8192]{1,0:T(8,128)(2,1)} custom-call(bf16[4,528,128]{2,1,0:T(8,128)(2,1)} %far.1.total_at, bf16[2048,128]{1,0:T(8,128)(2,1)} %bitcast.5), custom_call_target="tpu_custom_call" | custom-call | flops 10000000 | bytes 1000000 | tf_op jit(solution)/shard_map/product/pallas_call | solution.py:364
  54.0 0.0 copy-done
  54.0 0.0 collective-permute-done.2.theirs_at
  54.0 0.0 copy-start.1
  54.0 0.8 %copy-done.1 = bf16[4,528,128]{2,1,0:T(8,128)(2,1)} copy-done((bf16[4,528,128]{2,1,0:T(8,128)(2,1)}, bf16[4,528,128]{2,1,0:T(8,128)(2,1)S(1)}, u32[]{:S(2)}) %copy-start.1) | copy-done | bytes 540696
  54.8 6.8 %basis.1 = (f32[64,32,128]{2,1,0:T(8,128)}, f32[32,32,128]{2,1,0:T(8,128)}) custom-call(bf16[4,528,128]{2,1,0:T(8,128)(2,1)} %copy-done, bf16[4,528,128]{2,1,0:T(8,128)(2,1)} %copy-done.1, bf16[2048,128]{1,0:T(8,128)(2,1)} %bitcast.6), custom_call_target="tpu_custom_call" | custom-call | tf_op jit(solution)/shard_map/basis/pallas_call | solution.py:382
Async XLA Ops:
  5.3 9.9 %collective-permute-start.1 = (bf16[768,128]{1,0:T(8,128)(2,1)}, bf16[768,128]{1,0:T(8,128)(2,1)S(1)}, u32[]{:S(2)}, u32[]{:S(2)}) collective-permute-start(bf16[768,128]{1,0:T(8,128)(2,1)} %coeff.1.own_at), channel_id=1, source_target_pairs={{1,0},{2,1},{3,2},{32,3},{33,32},{34,33},{35,34},{64,35},{65,64},{... | collective-permute-start | bytes 589832 | tf_op jit(solution)/shard_map/ppermute | solution.py:330
  11.4 10.9 %collective-permute-start = (bf16[768,128]{1,0:T(8,128)(2,1)}, bf16[768,128]{1,0:T(8,128)(2,1)S(1)}, u32[]{:S(2)}, u32[]{:S(2)}) collective-permute-start(bf16[768,128]{1,0:T(8,128)(2,1)} %coeff.1.own_at), channel_id=1, source_target_pairs={{0,1},{1,2},{2,3},{3,32},{32,33},{33,34},{34,35},{35,64},{64,65},{... | collective-permute-start | bytes 589832 | tf_op jit(solution)/shard_map/ppermute | solution.py:329
  15.2 7.1 %copy-start.2 = (bf16[768,128]{1,0:T(8,128)(2,1)}, bf16[768,128]{1,0:T(8,128)(2,1)S(1)}, u32[]{:S(2)}) copy-start(bf16[768,128]{1,0:T(8,128)(2,1)S(1)} %collective-permute-done.1.after_at) | copy-start | bytes 589828
  22.3 0.7 %copy-start.3 = (bf16[768,128]{1,0:T(8,128)(2,1)}, bf16[768,128]{1,0:T(8,128)(2,1)S(1)}, u32[]{:S(2)}) copy-start(bf16[768,128]{1,0:T(8,128)(2,1)S(1)} %collective-permute-done.before_at) | copy-start | bytes 589828
  44.7 9.3 %copy-start = (bf16[4,528,128]{2,1,0:T(8,128)(2,1)}, bf16[4,528,128]{2,1,0:T(8,128)(2,1)S(1)}, u32[]{:S(2)}) copy-start(bf16[4,528,128]{2,1,0:T(8,128)(2,1)S(1)} %all_to_all.5.mine_at) | copy-start | bytes 1622020
  44.7 9.3 %collective-permute-start.2 = (bf16[4,528,128]{2,1,0:T(8,128)(2,1)S(1)}, bf16[4,528,128]{2,1,0:T(8,128)(2,1)S(1)}, u32[]{:S(2)}, u32[]{:S(2)}) collective-permute-start(bf16[4,528,128]{2,1,0:T(8,128)(2,1)S(1)} %all_to_all.5.mine_at), channel_id=1, source_target_pairs={{0,4},{4,0},{8,12},{12,8},{16,20},{20,16},{24,28},{28,24},{1,5},{5... | collective-permute-start | bytes 1622024 | tf_op jit(solution)/shard_map/ppermute | solution.py:362
  54.0 0.8 %copy-start.1 = (bf16[4,528,128]{2,1,0:T(8,128)(2,1)}, bf16[4,528,128]{2,1,0:T(8,128)(2,1)S(1)}, u32[]{:S(2)}) copy-start(bf16[4,528,128]{2,1,0:T(8,128)(2,1)S(1)} %collective-permute-done.2.theirs_at) | copy-start | bytes 1622020

commit v3 on v2

--- a/solution.py
+++ b/solution.py
@@ -186,9 +186,11 @@
         far, transfer_w, lambda chunk, c: wide[chunk * 8 + c], 4, 4, 4,
         lambda a, chunk: a * 4 + chunk, start=far,
     )
-    payload[0:512, :] = far[...].reshape(512, 128).astype(BF16)
-    pad = jnp.zeros((16, 128 - 32), BF16)
-    payload[512:528, :] = jnp.concatenate([test[...], pad], axis=1)
+    total = far[...].reshape(512, 128).astype(BF16)
+    rows = jnp.concatenate([test[...].astype(F32), jnp.zeros((16, 128 - 32), F32)], axis=1)
+    for h in range(2):
+        payload[264 * h : 264 * h + 256, :] = total[256 * h : 256 * (h + 1)]
+        payload[264 * h + 256 : 264 * h + 264, :] = rows[8 * h : 8 * (h + 1)].astype(BF16)
     for copy in fetched([(payload, out.at[i]) for i in range(out.shape[0])], sent):
         copy.wait()
 
@@ -198,7 +200,9 @@
     for copy in copies:
         copy.wait()
     widen(basis, basis_w)
-    total_w[...] = total[0:512, :].astype(F32).reshape(32, 16, 128)
+    for h in range(2):
+        rows = total[264 * h : 264 * h + 256, :].astype(F32)
+        total_w[16 * h : 16 * (h + 1)] = rows.reshape(16, 16, 128)
 
     def outer(blk, _):
         acc = weighted(
@@ -228,19 +232,21 @@
     mine_at, theirs_at, basis_at, new_at, fresh_at,
     totals, basis, basis_w, compressed, sketch, scale_w, gram, new_basis, fresh, sem, sent,
 ):
-    groups = totals.shape[0]
-    half = mine_at.shape[0]
+    groups = totals.shape[1]
+    core = lax.rem(lax.axis_index("vector"), 2)
     copies = fetched(
-        [(basis_at, basis), (mine_at, totals.at[0:half]), (theirs_at, totals.at[half:groups])], sem
+        [(basis_at, basis), (mine_at, totals.at[core]), (theirs_at, totals.at[1 - core])], sem
     )
     copies[0].wait()
     widen(basis, basis_w)
     for copy in copies[1:]:
         copy.wait()
-    tests = jnp.concatenate([totals[g, 512:528, :] for g in range(groups)], axis=0)
-    across = tests.astype(F32).T[0:32].astype(BF16)
+    pairs = [(g, h) for g in range(groups) for h in range(2)]
+    tests = jnp.concatenate([totals[h, g, 256:264, :].astype(F32) for g, h in pairs], axis=0)
+    across = tests.T[0:32].astype(BF16)
     for a in range(32):
-        rows = jnp.concatenate([totals[g, 16 * a : 16 * (a + 1), :] for g in range(groups)], axis=0)
+        at = 16 * (a % 16)
+        rows = jnp.concatenate([totals[a // 16, g, at : at + 16, :] for g in range(groups)], axis=0)
         compressed[a] = dot(across, rows)
 
     scale_w[...] = jnp.zeros((32, 128), F32)
@@ -303,11 +309,12 @@
     above = parent_coupling.reshape(4096, 64)
     vmem = pl.BlockSpec(memory_space=pltpu.VMEM)
     anywhere = pl.BlockSpec(memory_space=pl.ANY)
+    stored = pl.BlockSpec(memory_space=pltpu.HBM)
 
     coeff = pl.pallas_call(
         coeff_kernel,
         out_shape=jax.ShapeDtypeStruct((768, 128), BF16),
-        in_specs=[anywhere] * 3,
+        in_specs=[stored] * 3,
         out_specs=vmem,
         scratch_shapes=[
             pltpu.VMEM((16, 8192), BF16),
@@ -321,6 +328,7 @@
             pltpu.VMEM((32, 16, 128), F32),
             pltpu.SemaphoreType.DMA((3,)),
         ],
+        compiler_params=pltpu.CompilerParams(vmem_limit_bytes=24 << 20),
         name="coeff",
     )(samples, basis, moves)
 
@@ -334,7 +342,7 @@
     total = pl.pallas_call(
         far_kernel,
         out_shape=jax.ShapeDtypeStruct((half, 528, 128), BF16),
-        in_specs=[anywhere] * 6 + [vmem] * 3,
+        in_specs=[anywhere] * 3 + [stored] * 3 + [vmem] * 3,
         out_specs=anywhere,
         scratch_shapes=[
             pltpu.VMEM((768, 128), BF16),
@@ -354,13 +362,11 @@
             pltpu.SemaphoreType.DMA((6,)),
             pltpu.SemaphoreType.DMA((half,)),
         ],
+        compiler_params=pltpu.CompilerParams(vmem_limit_bytes=24 << 20),
         name="far",
     )(coeff, before, after, moves, near, above, leaf_lists, parent_lists, test_matrix)
 
-    cores = [[2 * y + core for y in range(half)] for core in range(2)]
-    mine = lax.all_to_all(total, "vector", 0, 0, tiled=True, axis_index_groups=cores)
-    theirs = lax.ppermute(mine, "vector", [(i, i ^ 1) for i in range(groups)])
-
+    mine = lax.all_to_all(total.reshape(groups, 264, 128), "vector", 0, 0, tiled=True)
     product = pl.pallas_call(
         product_kernel,
         out_shape=jax.ShapeDtypeStruct((16, 8192), BF16),
@@ -376,8 +382,12 @@
             pltpu.SemaphoreType.DMA((2,)),
         ],
         cost_estimate=pl.CostEstimate(flops=10**7, bytes_accessed=10**6, transcendentals=0),
+        compiler_params=pltpu.CompilerParams(vmem_limit_bytes=24 << 20),
         name="product",
     )(total, basis)
+
+    mine, product = lax.optimization_barrier((mine, product))
+    theirs = lax.ppermute(mine, "vector", [(i, i ^ 1) for i in range(groups)])
 
     new_basis, fresh = pl.pallas_call(
         basis_kernel,
@@ -388,7 +398,7 @@
         in_specs=[anywhere] * 3,
         out_specs=(anywhere, anywhere),
         scratch_shapes=[
-            pltpu.VMEM((groups, 528, 128), BF16),
+            pltpu.VMEM((2, groups, 264, 128), BF16),
             pltpu.VMEM((2048, 128), BF16),
             pltpu.VMEM((256, 8, 128), F32),
             pltpu.VMEM((32, 32, 128), F32),
@@ -400,6 +410,7 @@
             pltpu.SemaphoreType.DMA((3,)),
             pltpu.SemaphoreType.DMA((2,)),
         ],
+        compiler_params=pltpu.CompilerParams(vmem_limit_bytes=24 << 20),
         name="basis",
     )(mine, theirs, basis)
     return product, new_basis, fresh

time: 62 us -> 61.4 us (level)
  blocking collectives: 11.6 us -> 0 us
  waiting for transfers between devices: 9 us -> 15.9 us
  starting transfers between devices: 13.1 us -> 17.3 us
  Pallas kernels: 25.8 us -> 22 us
  local copies, waits for them, and re-layouts: 1.47 us -> 5.13 us
    all_to_all x1 -> x0, blocking collectives: 11.6 us -> none  [shards(): lax.all_to_all(total, 'vector', 0, 0, tiled=True, axis_index_groups=cores)]
    all_to_all x0 -> x1, starting transfers between devices: none -> 6.42 us  [shards(): lax.all_to_all(total.reshape(groups, 264, 128), 'vector', 0, 0, tiled=True)]
    all_to_all x0 -> x1, waiting for transfers between devices: none -> 5.56 us  [shards(): lax.all_to_all(total.reshape(groups, 264, 128), 'vector', 0, 0, tiled=True)]
    unnamed x8 -> x20, local copies, waits for them, and re-layouts: 1.47 us -> 5.13 us
    ppermute x1, starting transfers between devices: 5.13 us -> 2.87 us  [shards(): theirs = lax.ppermute(mine, 'vector', [(i, i ^ 1) for i in range(groups)])]
    pallas_call x1, Pallas kernels: 4.69 us -> 3.15 us  [shards(): pl.pallas_call(coeff_kernel, out_shape=jax.ShapeDtypeStruct((768, 128), B...]
    ppermute x1, waiting for transfers between devices: 0.01 us -> 1.54 us  [shards(): theirs = lax.ppermute(mine, 'vector', [(i, i ^ 1) for i in range(groups)])]
    pallas_call x1, Pallas kernels: 6.81 us -> 5.72 us  [shards(): pl.pallas_call(basis_kernel, out_shape=(jax.ShapeDtypeStruct((64, 32, 128...]
  transfers between devices with their start and end apart: 3 -> 4, of which waited for: 2 -> 4; matrix products, arithmetic and copies ran while one was open for 0% -> 0% of each run, Pallas kernels for 7% -> 6%
where the time goes in v3:
time: 61.4 us; the launch traced here: 61 us
  Pallas kernels  22 us (36%)
  starting transfers between devices  17.3 us (28%)
  waiting for transfers between devices  15.9 us (26%)
  local copies, waits for them, and re-layouts  5.13 us (8%)
  between operations  0.73 us (1%)
    pallas_call x1, Pallas kernels, shards(): pl.pallas_call(far_kernel, out_shape=jax.ShapeDtypeStruct((half, 528, 128...  9.17 us
    ppermute x1, waiting for transfers between devices, shards(): before = lax.ppermute(coeff, HOPS, up)  7.16 us
    all_to_all x1, starting transfers between devices, shards(): lax.all_to_all(total.reshape(groups, 264, 128), 'vector', 0, 0, tiled=True)  6.42 us
    ppermute x1, starting transfers between devices, shards(): after = lax.ppermute(coeff, HOPS, [(b, a) for a, b in up])  6.04 us
    pallas_call x1, Pallas kernels, shards(): pl.pallas_call(basis_kernel, out_shape=(jax.ShapeDtypeStruct((64, 32, 128...  5.72 us
    all_to_all x1, waiting for transfers between devices, shards(): lax.all_to_all(total.reshape(groups, 264, 128), 'vector', 0, 0, tiled=True)  5.56 us
    unnamed x20, local copies, waits for them, and re-layouts  5.13 us
    pallas_call x1, Pallas kernels, shards(): pl.pallas_call(product_kernel, out_shape=jax.ShapeDtypeStruct((16, 8192),...  3.95 us
  transfers between devices with their start and end apart: 4, of which 4 were waited for; matrix products, arithmetic and copies ran while one was open for 0% of the time, Pallas kernels for 6%

profile of v3, /device:TPU:385, one launch (start us, length us, event | category | flops | bytes accessed | tf_op | source)
XLA Modules:
  0.0 61.0 jit_solution(12300439516657715234)
XLA Ops:
  0.6 0.0 copy-start
  0.6 1.0 %copy-done = bf16[32,64,128]{2,1,0:T(8,128)(2,1)S(1)} copy-done((bf16[32,64,128]{2,1,0:T(8,128)(2,1)S(1)}, bf16[32,64,128]{2,1,0:T(8,128)(2,1)}, u32[]{:S(2)}) %copy-start) | copy-done | bytes 524312
  1.7 0.0 copy-start.4
  1.7 0.9 %copy-done.4 = bf16[32,32,128]{2,1,0:T(8,128)(2,1)S(1)} copy-done((bf16[32,32,128]{2,1,0:T(8,128)(2,1)S(1)}, bf16[32,32,128]{2,1,0:T(8,128)(2,1)}, u32[]{:S(2)}) %copy-start.4) | copy-done | bytes 262168
  2.6 0.0 copy-start.6
  2.6 0.9 %copy-done.6 = bf16[16,8192]{1,0:T(8,128)(2,1)S(1)} copy-done((bf16[16,8192]{1,0:T(8,128)(2,1)S(1)}, bf16[16,8192]{1,0:T(8,128)(2,1)}, u32[]{:S(2)}) %copy-start.6) | copy-done | bytes 262168
  3.6 0.0 copy-start.2
  3.6 0.0 copy-start.7
  3.6 0.0 copy-start.9
  3.6 3.1 %coeff.1.own_at = bf16[768,128]{1,0:T(8,128)(2,1)S(1)} custom-call(bf16[16,8192]{1,0:T(8,128)(2,1)S(1)} %copy-done.6, bf16[2048,128]{1,0:T(8,128)(2,1)S(1)} %bitcast.5, bf16[1024,128]{1,0:T(8,128)(2,1)S(1)} %bitcast.10), custom_call_target="tpu_custom_call" | custom-call | tf_op jit(solution)/shard_map/coeff/pallas_call | solution.py:314
  6.7 0.0 copy-start.8
  6.8 6.0 %collective-permute-start.1 = (bf16[768,128]{1,0:T(8,128)(2,1)S(1)}, bf16[768,128]{1,0:T(8,128)(2,1)S(1)}, u32[]{:S(2)}, u32[]{:S(2)}) collective-permute-start(bf16[768,128]{1,0:T(8,128)(2,1)S(1)} %coeff.1.own_at), channel_id=1, source_target_pairs={{1,0},{2,1},{3,2},{32,3},{33,32},{34,33},{35,34},{64,35},{65,64},{... | collective-permute-start | bytes 589832 | tf_op jit(solution)/shard_map/ppermute | solution.py:338
  12.8 1.9 %collective-permute-start = (bf16[768,128]{1,0:T(8,128)(2,1)S(1)}, bf16[768,128]{1,0:T(8,128)(2,1)S(1)}, u32[]{:S(2)}, u32[]{:S(2)}) collective-permute-start(bf16[768,128]{1,0:T(8,128)(2,1)S(1)} %coeff.1.own_at), channel_id=1, source_target_pairs={{0,1},{1,2},{2,3},{3,32},{32,33},{33,34},{34,35},{35,64},{64,65},{... | collective-permute-start | bytes 589832 | tf_op jit(solution)/shard_map/ppermute | solution.py:337
  14.7 1.6 %collective-permute-done.1.after_at = bf16[768,128]{1,0:T(8,128)(2,1)S(1)} collective-permute-done((bf16[768,128]{1,0:T(8,128)(2,1)S(1)}, bf16[768,128]{1,0:T(8,128)(2,1)S(1)}, u32[]{:S(2)}, u32[]{:S(2)}) %collective-permute-start.1) | collective-permute-done | bytes 196640 | tf_op jit(solution)/shard_map/ppermute | solution.py:338
  16.4 7.2 %collective-permute-done.before_at = bf16[768,128]{1,0:T(8,128)(2,1)S(1)} collective-permute-done((bf16[768,128]{1,0:T(8,128)(2,1)S(1)}, bf16[768,128]{1,0:T(8,128)(2,1)S(1)}, u32[]{:S(2)}, u32[]{:S(2)}) %collective-permute-start) | collective-permute-done | bytes 196640 | tf_op jit(solution)/shard_map/ppermute | solution.py:337
  23.5 0.0 copy-done.2
  23.5 0.0 copy-done.7
  23.5 0.0 copy-done.9
  23.5 0.0 copy-done.8
  23.5 0.0 copy-start.3
  23.5 1.2 %copy-done.3 = bf16[32,32,4,64]{3,2,1,0:T(4,128)(2,1)S(1)} copy-done((bf16[32,32,4,64]{3,2,1,0:T(4,128)(2,1)S(1)}, bf16[32,32,4,64]{3,2,1,0:T(4,128)(2,1)}, u32[]{:S(2)}) %copy-start.3) | copy-done | bytes 524312
  24.8 0.0 copy-start.5
  24.8 0.9 %copy-done.5 = bf16[32,32,128]{2,1,0:T(8,128)(2,1)S(1)} copy-done((bf16[32,32,128]{2,1,0:T(8,128)(2,1)S(1)}, bf16[32,32,128]{2,1,0:T(8,128)(2,1)}, u32[]{:S(2)}) %copy-start.5) | copy-done | bytes 262168
  25.7 9.2 %far.1.total_at = bf16[4,528,128]{2,1,0:T(8,128)(2,1)} custom-call(bf16[768,128]{1,0:T(8,128)(2,1)S(1)} %coeff.1.own_at, bf16[768,128]{1,0:T(8,128)(2,1)S(1)} %collective-permute-done.before_at, bf16[768,128]{1,0:T(8,128)(2,1)S(1)} %collective-permute-done.1.after_at, bf16[1024,128]{1,0:T(8,128)(2,1)S(1)} %bitcast.11, bf16[4096,128]{1,0:T(8,128)(2,1)S(1)} %bitcast.8, ...), custom_call_target="tpu_custom_call" | custom-call | tf_op jit(solution)/shard_map/far/pallas_call | solution.py:342
  34.9 0.0 copy-start.1
  34.9 6.4 %all-to-all-start = ((bf16[8,264,128]{2,1,0:T(8,128)(2,1)}), bf16[8,264,128]{2,1,0:T(8,128)(2,1)S(1)}, u32[]{:S(2)}, u32[]{:S(2)}) async-start(bf16[8,264,128]{2,1,0:T(8,128)(2,1)} %bitcast.4), calls=%async_computation | async-start | bytes 1081344 | tf_op jit(solution)/shard_map/all_to_all | solution.py:369
  41.3 0.0 copy-done.1
  41.3 4.0 %product.1 = bf16[16,8192]{1,0:T(8,128)(2,1)} custom-call(bf16[4,528,128]{2,1,0:T(8,128)(2,1)} %far.1.total_at, bf16[2048,128]{1,0:T(8,128)(2,1)S(1)} %bitcast.6), custom_call_target="tpu_custom_call" | custom-call | flops 10000000 | bytes 1000000 | tf_op jit(solution)/shard_map/product/pallas_call | solution.py:370
  45.3 5.6 %all-to-all-done.mine_at = bf16[8,264,128]{2,1,0:T(8,128)(2,1)S(1)} async-done(((bf16[8,264,128]{2,1,0:T(8,128)(2,1)}), bf16[8,264,128]{2,1,0:T(8,128)(2,1)S(1)}, u32[]{:S(2)}, u32[]{:S(2)}) %all-to-all-start) | async-done | bytes 540704 | tf_op jit(solution)/shard_map/all_to_all | solution.py:369
  50.8 2.9 %collective-permute-start.2 = (bf16[8,264,128]{2,1,0:T(8,128)(2,1)S(1)}, bf16[8,264,128]{2,1,0:T(8,128)(2,1)S(1)}, u32[]{:S(2)}, u32[]{:S(2)}) collective-permute-start(bf16[8,264,128]{2,1,0:T(8,128)(2,1)S(1)} %all-to-all-done.mine_at), channel_id=1, source_target_pairs={{0,4},{4,0},{8,12},{12,8},{16,20},{20,16},{24,28},{28,24},{1,5},{5... | collective-permute-start | bytes 1622024 | tf_op jit(solution)/shard_map/ppermute | solution.py:390
  53.7 1.5 %collective-permute-done.2.theirs_at = bf16[8,264,128]{2,1,0:T(8,128)(2,1)S(1)} collective-permute-done((bf16[8,264,128]{2,1,0:T(8,128)(2,1)S(1)}, bf16[8,264,128]{2,1,0:T(8,128)(2,1)S(1)}, u32[]{:S(2)}, u32[]{:S(2)}) %collective-permute-start.2) | collective-permute-done | bytes 540704 | tf_op jit(solution)/shard_map/ppermute | solution.py:390
  55.3 5.7 %basis.1 = (f32[64,32,128]{2,1,0:T(8,128)}, f32[32,32,128]{2,1,0:T(8,128)}) custom-call(bf16[8,264,128]{2,1,0:T(8,128)(2,1)S(1)} %all-to-all-done.mine_at, bf16[8,264,128]{2,1,0:T(8,128)(2,1)S(1)} %collective-permute-done.2.theirs_at, bf16[2048,128]{1,0:T(8,128)(2,1)S(1)} %bitcast.7), custom_call_target="tpu_custom_call" | custom-call | tf_op jit(solution)/shard_map/basis/pallas_call | solution.py:392
Async XLA Ops:
  0.6 1.0 %copy-start = (bf16[32,64,128]{2,1,0:T(8,128)(2,1)S(1)}, bf16[32,64,128]{2,1,0:T(8,128)(2,1)}, u32[]{:S(2)}) copy-start(bf16[32,64,128]{2,1,0:T(8,128)(2,1)} %param.9) | copy-start | bytes 1572868
  1.7 0.9 %copy-start.4 = (bf16[32,32,128]{2,1,0:T(8,128)(2,1)S(1)}, bf16[32,32,128]{2,1,0:T(8,128)(2,1)}, u32[]{:S(2)}) copy-start(bf16[32,32,128]{2,1,0:T(8,128)(2,1)} %param.10) | copy-start | bytes 786436
  2.6 0.9 %copy-start.6 = (bf16[16,8192]{1,0:T(8,128)(2,1)S(1)}, bf16[16,8192]{1,0:T(8,128)(2,1)}, u32[]{:S(2)}) copy-start(bf16[16,8192]{1,0:T(8,128)(2,1)} %samples_at.1) | copy-start | bytes 786436
  3.6 19.9 %copy-start.2 = (bf16[32,32,4,128]{3,2,1,0:T(4,128)(2,1)S(1)}, bf16[32,32,4,128]{3,2,1,0:T(4,128)(2,1)}, u32[]{:S(2)}) copy-start(bf16[32,32,4,128]{3,2,1,0:T(4,128)(2,1)} %param.12) | copy-start | bytes 3145732
  3.6 19.9 %copy-start.7 = (bf16[16,32]{1,0:T(8,128)(2,1)S(1)}, bf16[16,32]{1,0:T(8,128)(2,1)}, u32[]{:S(2)}) copy-start(bf16[16,32]{1,0:T(8,128)(2,1)} %test.1) | copy-start | bytes 3076
  3.6 19.9 %copy-start.9 = (s32[4,64]{1,0:T(4,128)S(1)}, s32[4,64]{1,0:T(4,128)}, u32[]{:S(2)}) copy-start(s32[4,64]{1,0:T(4,128)} %parent_lists.1) | copy-start | bytes 3076
  6.7 16.8 %copy-start.8 = (s32[4,128]{1,0:T(4,128)S(1)}, s32[4,128]{1,0:T(4,128)}, u32[]{:S(2)}) copy-start(s32[4,128]{1,0:T(4,128)} %leaf_lists.1) | copy-start | bytes 6148
  6.8 9.6 %collective-permute-start.1 = (bf16[768,128]{1,0:T(8,128)(2,1)S(1)}, bf16[768,128]{1,0:T(8,128)(2,1)S(1)}, u32[]{:S(2)}, u32[]{:S(2)}) collective-permute-start(bf16[768,128]{1,0:T(8,128)(2,1)S(1)} %coeff.1.own_at), channel_id=1, source_target_pairs={{1,0},{2,1},{3,2},{32,3},{33,32},{34,33},{35,34},{64,35},{65,64},{... | collective-permute-start | bytes 589832 | tf_op jit(solution)/shard_map/ppermute | solution.py:338
  12.8 10.7 %collective-permute-start = (bf16[768,128]{1,0:T(8,128)(2,1)S(1)}, bf16[768,128]{1,0:T(8,128)(2,1)S(1)}, u32[]{:S(2)}, u32[]{:S(2)}) collective-permute-start(bf16[768,128]{1,0:T(8,128)(2,1)S(1)} %coeff.1.own_at), channel_id=1, source_target_pairs={{0,1},{1,2},{2,3},{3,32},{32,33},{33,34},{34,35},{35,64},{64,65},{... | collective-permute-start | bytes 589832 | tf_op jit(solution)/shard_map/ppermute | solution.py:337
  23.5 1.2 %copy-start.3 = (bf16[32,32,4,64]{3,2,1,0:T(4,128)(2,1)S(1)}, bf16[32,32,4,64]{3,2,1,0:T(4,128)(2,1)}, u32[]{:S(2)}) copy-start(bf16[32,32,4,64]{3,2,1,0:T(4,128)(2,1)} %param.14) | copy-start | bytes 1572868
  24.8 0.9 %copy-start.5 = (bf16[32,32,128]{2,1,0:T(8,128)(2,1)S(1)}, bf16[32,32,128]{2,1,0:T(8,128)(2,1)}, u32[]{:S(2)}) copy-start(bf16[32,32,128]{2,1,0:T(8,128)(2,1)} %param.10) | copy-start | bytes 786436
  34.9 6.4 %copy-start.1 = (bf16[32,64,128]{2,1,0:T(8,128)(2,1)S(1)}, bf16[32,64,128]{2,1,0:T(8,128)(2,1)}, u32[]{:S(2)}) copy-start(bf16[32,64,128]{2,1,0:T(8,128)(2,1)} %param.9) | copy-start | bytes 1572868
  34.9 15.9 %all-to-all-start = ((bf16[8,264,128]{2,1,0:T(8,128)(2,1)}), bf16[8,264,128]{2,1,0:T(8,128)(2,1)S(1)}, u32[]{:S(2)}, u32[]{:S(2)}) async-start(bf16[8,264,128]{2,1,0:T(8,128)(2,1)} %bitcast.4), calls=%async_computation | async-start | bytes 1081344 | tf_op jit(solution)/shard_map/all_to_all | solution.py:369
  50.8 4.4 %collective-permute-start.2 = (bf16[8,264,128]{2,1,0:T(8,128)(2,1)S(1)}, bf16[8,264,128]{2,1,0:T(8,128)(2,1)S(1)}, u32[]{:S(2)}, u32[]{:S(2)}) collective-permute-start(bf16[8,264,128]{2,1,0:T(8,128)(2,1)S(1)} %all-to-all-done.mine_at), channel_id=1, source_target_pairs={{0,4},{4,0},{8,12},{12,8},{16,20},{20,16},{24,28},{28,24},{1,5},{5... | collective-permute-start | bytes 1622024 | tf_op jit(solution)/shard_map/ppermute | solution.py:390

commit v4 on v3

--- a/solution.py
+++ b/solution.py
@@ -64,6 +64,10 @@
         return 0
 
     lax.fori_loop(0, blocks, outer, 0)
+
+
+def swaps(firsts):
+    return [pair for i in firsts for pair in ((i, i + 1), (i + 1, i))]
 
 
 def fetched(pairs, sem):
@@ -121,18 +125,20 @@
 
 
 def far_kernel(
-    own_at, before_at, after_at, transfer_at, leaf_at, parent_at, leaf_lists, parent_lists, test,
-    out, own, before, after, transfer, leaf_b, parent_b,
+    own_at, inner_at, outer_at, transfer_at, leaf_at, parent_at, leaf_lists, parent_lists, test,
+    out, own, sides, transfer, leaf_b, parent_b,
     coupling_w, parent_w, transfer_w, source, far, pfar, wide, payload, sem, sent,
 ):
+    place = lax.axis_index("cluster") * lax.axis_size("replica") + lax.axis_index("replica")
+    odd = lax.rem(place, 2)
+    before, after = sides.at[0], sides.at[1]
     copies = fetched(
         [
-            (own_at, own), (before_at, before), (after_at, after),
+            (own_at, own), (inner_at, sides.at[1 - odd]), (outer_at, sides.at[odd]),
             (parent_at, parent_b), (leaf_at, leaf_b), (transfer_at, transfer),
         ],
         sem,
     )
-    place = lax.axis_index("cluster") * lax.axis_size("replica") + lax.axis_index("replica")
 
     first = place * 64 - 64
     twice = picked(iota((64, 128), 0) == iota((64, 128), 1) % 64)
@@ -309,12 +315,11 @@
     above = parent_coupling.reshape(4096, 64)
     vmem = pl.BlockSpec(memory_space=pltpu.VMEM)
     anywhere = pl.BlockSpec(memory_space=pl.ANY)
-    stored = pl.BlockSpec(memory_space=pltpu.HBM)
 
     coeff = pl.pallas_call(
         coeff_kernel,
         out_shape=jax.ShapeDtypeStruct((768, 128), BF16),
-        in_specs=[stored] * 3,
+        in_specs=[anywhere] * 3,
         out_specs=vmem,
         scratch_shapes=[
             pltpu.VMEM((16, 8192), BF16),
@@ -328,26 +333,24 @@
             pltpu.VMEM((32, 16, 128), F32),
             pltpu.SemaphoreType.DMA((3,)),
         ],
-        compiler_params=pltpu.CompilerParams(vmem_limit_bytes=24 << 20),
+        compiler_params=pltpu.CompilerParams(vmem_limit_bytes=62 << 20),
         name="coeff",
     )(samples, basis, moves)
 
     peers = lax.axis_size("cluster") * lax.axis_size("replica")
-    up = [(i, i + 1) for i in range(peers - 1)]
-    before = lax.ppermute(coeff, HOPS, up)
-    after = lax.ppermute(coeff, HOPS, [(b, a) for a, b in up])
+    outer = lax.ppermute(coeff, HOPS, swaps(range(1, peers - 1, 2)))
+    inner = lax.ppermute(coeff, HOPS, swaps(range(0, peers - 1, 2)))
 
     groups = lax.axis_size("vector")
     half = groups // 2
     total = pl.pallas_call(
         far_kernel,
         out_shape=jax.ShapeDtypeStruct((half, 528, 128), BF16),
-        in_specs=[anywhere] * 3 + [stored] * 3 + [vmem] * 3,
+        in_specs=[anywhere] * 3 + [anywhere] * 3 + [vmem] * 3,
         out_specs=anywhere,
         scratch_shapes=[
             pltpu.VMEM((768, 128), BF16),
-            pltpu.VMEM((768, 128), BF16),
-            pltpu.VMEM((768, 128), BF16),
+            pltpu.VMEM((2, 768, 128), BF16),
             pltpu.VMEM((1024, 128), BF16),
             pltpu.VMEM((4096, 128), BF16),
             pltpu.VMEM((4096, 64), BF16),
@@ -362,9 +365,9 @@
             pltpu.SemaphoreType.DMA((6,)),
             pltpu.SemaphoreType.DMA((half,)),
         ],
-        compiler_params=pltpu.CompilerParams(vmem_limit_bytes=24 << 20),
+        compiler_params=pltpu.CompilerParams(vmem_limit_bytes=62 << 20),
         name="far",
-    )(coeff, before, after, moves, near, above, leaf_lists, parent_lists, test_matrix)
+    )(coeff, inner, outer, moves, near, above, leaf_lists, parent_lists, test_matrix)
 
     mine = lax.all_to_all(total.reshape(groups, 264, 128), "vector", 0, 0, tiled=True)
     product = pl.pallas_call(

time: 61.4 us -> 56.2 us (0.915)
  local copies, waits for them, and re-layouts: 5.13 us -> 0.69 us
  waiting for transfers between devices: 15.9 us -> 13.5 us
  Pallas kernels: 22 us -> 23.8 us
    unnamed x20 -> x8, local copies, waits for them, and re-layouts: 5.13 us -> 0.69 us
    ppermute x2, waiting for transfers between devices: 8.79 us -> 5.67 us  [the longest x1 3.23 us: shards(): outer = lax.ppermute(coeff, HOPS, swaps(range(1, peers - 1, 2)))]
    pallas_call x1, Pallas kernels: 3.15 us -> 4.69 us  [shards(): pl.pallas_call(coeff_kernel, out_shape=jax.ShapeDtypeStruct((768, 128), B...]
    pallas_call x1, Pallas kernels: 9.17 us -> 10.1 us  [shards(): pl.pallas_call(far_kernel, out_shape=jax.ShapeDtypeStruct((half, 528, 128...]
    pallas_call x1, Pallas kernels: 3.95 us -> 3.27 us  [shards(): pl.pallas_call(product_kernel, out_shape=jax.ShapeDtypeStruct((16, 8192),...]
    all_to_all x1, waiting for transfers between devices: 5.56 us -> 6.24 us  [shards(): lax.all_to_all(total.reshape(groups, 264, 128), 'vector', 0, 0, tiled=True)]
where the time goes in v4:
time: 56.2 us; the launch traced here: 55.9 us
  Pallas kernels  23.8 us (42%)
  starting transfers between devices  17.3 us (31%)
  waiting for transfers between devices  13.5 us (24%)
  between operations  0.7 us (1%)
  local copies, waits for them, and re-layouts  0.69 us (1%)
    pallas_call x1, Pallas kernels, shards(): pl.pallas_call(far_kernel, out_shape=jax.ShapeDtypeStruct((half, 528, 128...  10.1 us
    all_to_all x1, starting transfers between devices, shards(): lax.all_to_all(total.reshape(groups, 264, 128), 'vector', 0, 0, tiled=True)  6.43 us
    all_to_all x1, waiting for transfers between devices, shards(): lax.all_to_all(total.reshape(groups, 264, 128), 'vector', 0, 0, tiled=True)  6.24 us
    ppermute x1, starting transfers between devices, shards(): outer = lax.ppermute(coeff, HOPS, swaps(range(1, peers - 1, 2)))  6.04 us
    pallas_call x1, Pallas kernels, shards(): pl.pallas_call(basis_kernel, out_shape=(jax.ShapeDtypeStruct((64, 32, 128...  5.72 us
    pallas_call x1, Pallas kernels, shards(): pl.pallas_call(coeff_kernel, out_shape=jax.ShapeDtypeStruct((768, 128), B...  4.69 us
    pallas_call x1, Pallas kernels, shards(): pl.pallas_call(product_kernel, out_shape=jax.ShapeDtypeStruct((16, 8192),...  3.27 us
    ppermute x1, waiting for transfers between devices, shards(): outer = lax.ppermute(coeff, HOPS, swaps(range(1, peers - 1, 2)))  3.23 us
  transfers between devices with their start and end apart: 4, of which 4 were waited for; matrix products, arithmetic and copies ran while one was open for 0% of the time, Pallas kernels for 6%

profile of v4, /device:TPU:385, one launch (start us, length us, event | category | flops | bytes accessed | tf_op | source)
XLA Modules:
  0.0 55.9 jit_solution(9859099423729945410)
XLA Ops:
  0.6 4.7 %coeff.1.own_at = bf16[768,128]{1,0:T(8,128)(2,1)} custom-call(bf16[16,8192]{1,0:T(8,128)(2,1)} %samples_at.1, bf16[2048,128]{1,0:T(8,128)(2,1)} %bitcast.6, bf16[1024,128]{1,0:T(8,128)(2,1)} %bitcast.11), custom_call_target="tpu_custom_call" | custom-call | tf_op jit(solution)/shard_map/coeff/pallas_call | solution.py:319
  5.3 6.0 %collective-permute-start.1 = (bf16[768,128]{1,0:T(8,128)(2,1)}, bf16[768,128]{1,0:T(8,128)(2,1)S(1)}, u32[]{:S(2)}, u32[]{:S(2)}) collective-permute-start(bf16[768,128]{1,0:T(8,128)(2,1)} %coeff.1.own_at), channel_id=1, source_target_pairs={{1,2},{2,1},{3,32},{32,3},{33,34},{34,33},{35,64},{64,35},{65,66},... | collective-permute-start | bytes 589832 | tf_op jit(solution)/shard_map/ppermute | solution.py:341
  11.4 1.9 %collective-permute-start = (bf16[768,128]{1,0:T(8,128)(2,1)}, bf16[768,128]{1,0:T(8,128)(2,1)S(1)}, u32[]{:S(2)}, u32[]{:S(2)}) collective-permute-start(bf16[768,128]{1,0:T(8,128)(2,1)} %coeff.1.own_at), channel_id=1, source_target_pairs={{0,1},{1,0},{2,3},{3,2},{32,33},{33,32},{34,35},{35,34},{64,65},{6... | collective-permute-start | bytes 589832 | tf_op jit(solution)/shard_map/ppermute | solution.py:342
  13.3 3.2 %collective-permute-done.1.outer_at = bf16[768,128]{1,0:T(8,128)(2,1)S(1)} collective-permute-done((bf16[768,128]{1,0:T(8,128)(2,1)}, bf16[768,128]{1,0:T(8,128)(2,1)S(1)}, u32[]{:S(2)}, u32[]{:S(2)}) %collective-permute-start.1) | collective-permute-done | bytes 196640 | tf_op jit(solution)/shard_map/ppermute | solution.py:341
  16.5 0.0 copy-start.2
  16.5 2.4 %collective-permute-done.inner_at = bf16[768,128]{1,0:T(8,128)(2,1)S(1)} collective-permute-done((bf16[768,128]{1,0:T(8,128)(2,1)}, bf16[768,128]{1,0:T(8,128)(2,1)S(1)}, u32[]{:S(2)}, u32[]{:S(2)}) %collective-permute-start) | collective-permute-done | bytes 196640 | tf_op jit(solution)/shard_map/ppermute | solution.py:342
  19.0 0.0 copy-start.3
  19.0 0.0 copy-done.2
  19.0 0.7 %copy-done.3 = bf16[768,128]{1,0:T(8,128)(2,1)} copy-done((bf16[768,128]{1,0:T(8,128)(2,1)}, bf16[768,128]{1,0:T(8,128)(2,1)S(1)}, u32[]{:S(2)}) %copy-start.3) | copy-done | bytes 196632
  19.7 10.1 %far.1.total_at = bf16[4,528,128]{2,1,0:T(8,128)(2,1)} custom-call(bf16[768,128]{1,0:T(8,128)(2,1)} %coeff.1.own_at, bf16[768,128]{1,0:T(8,128)(2,1)} %copy-done.3, bf16[768,128]{1,0:T(8,128)(2,1)} %copy-done.2, bf16[1024,128]{1,0:T(8,128)(2,1)} %bitcast.12, bf16[4096,128]{1,0:T(8,128)(2,1)} %bitcast.9, bf16[4096,64]{1,0:T(8,128)(2,1)} %bitcast.10, ...), custom_call_target="tpu_custom_call" | custom-call | tf_op jit(solution)/shard_map/far/pallas_call | solution.py:346
  29.8 0.0 copy-start
  29.8 0.0 copy-start.1
  29.8 6.4 %all-to-all-start = ((bf16[8,264,128]{2,1,0:T(8,128)(2,1)}), bf16[8,264,128]{2,1,0:T(8,128)(2,1)S(1)}, u32[]{:S(2)}, u32[]{:S(2)}) async-start(bf16[8,264,128]{2,1,0:T(8,128)(2,1)} %bitcast.5), calls=%async_computation | async-start | bytes 1081344 | tf_op jit(solution)/shard_map/all_to_all | solution.py:372
  36.2 0.0 copy-done
  36.2 0.0 copy-done.1
  36.2 3.3 %product.1 = bf16[16,8192]{1,0:T(8,128)(2,1)} custom-call(bf16[4,528,128]{2,1,0:T(8,128)(2,1)S(1)} %copy-done, bf16[2048,128]{1,0:T(8,128)(2,1)S(1)} %bitcast.7), custom_call_target="tpu_custom_call" | custom-call | flops 10000000 | bytes 1000000 | tf_op jit(solution)/shard_map/product/pallas_call | solution.py:373
  39.5 6.2 %all-to-all-done.mine_at = bf16[8,264,128]{2,1,0:T(8,128)(2,1)S(1)} async-done(((bf16[8,264,128]{2,1,0:T(8,128)(2,1)}), bf16[8,264,128]{2,1,0:T(8,128)(2,1)S(1)}, u32[]{:S(2)}, u32[]{:S(2)}) %all-to-all-start) | async-done | bytes 540704 | tf_op jit(solution)/shard_map/all_to_all | solution.py:372
  45.8 2.9 %collective-permute-start.2 = (bf16[8,264,128]{2,1,0:T(8,128)(2,1)S(1)}, bf16[8,264,128]{2,1,0:T(8,128)(2,1)S(1)}, u32[]{:S(2)}, u32[]{:S(2)}) collective-permute-start(bf16[8,264,128]{2,1,0:T(8,128)(2,1)S(1)} %all-to-all-done.mine_at), channel_id=1, source_target_pairs={{0,4},{4,0},{8,12},{12,8},{16,20},{20,16},{24,28},{28,24},{1,5},{5... | collective-permute-start | bytes 1622024 | tf_op jit(solution)/shard_map/ppermute | solution.py:393
  48.6 1.5 %collective-permute-done.2.theirs_at = bf16[8,264,128]{2,1,0:T(8,128)(2,1)S(1)} collective-permute-done((bf16[8,264,128]{2,1,0:T(8,128)(2,1)S(1)}, bf16[8,264,128]{2,1,0:T(8,128)(2,1)S(1)}, u32[]{:S(2)}, u32[]{:S(2)}) %collective-permute-start.2) | collective-permute-done | bytes 540704 | tf_op jit(solution)/shard_map/ppermute | solution.py:393
  50.2 5.7 %basis.1 = (f32[64,32,128]{2,1,0:T(8,128)}, f32[32,32,128]{2,1,0:T(8,128)}) custom-call(bf16[8,264,128]{2,1,0:T(8,128)(2,1)S(1)} %all-to-all-done.mine_at, bf16[8,264,128]{2,1,0:T(8,128)(2,1)S(1)} %collective-permute-done.2.theirs_at, bf16[2048,128]{1,0:T(8,128)(2,1)S(1)} %bitcast.8), custom_call_target="tpu_custom_call" | custom-call | tf_op jit(solution)/shard_map/basis/pallas_call | solution.py:395
Async XLA Ops:
  5.3 11.2 %collective-permute-start.1 = (bf16[768,128]{1,0:T(8,128)(2,1)}, bf16[768,128]{1,0:T(8,128)(2,1)S(1)}, u32[]{:S(2)}, u32[]{:S(2)}) collective-permute-start(bf16[768,128]{1,0:T(8,128)(2,1)} %coeff.1.own_at), channel_id=1, source_target_pairs={{1,2},{2,1},{3,32},{32,3},{33,34},{34,33},{35,64},{64,35},{65,66},... | collective-permute-start | bytes 589832 | tf_op jit(solution)/shard_map/ppermute | solution.py:341
  11.4 7.6 %collective-permute-start = (bf16[768,128]{1,0:T(8,128)(2,1)}, bf16[768,128]{1,0:T(8,128)(2,1)S(1)}, u32[]{:S(2)}, u32[]{:S(2)}) collective-permute-start(bf16[768,128]{1,0:T(8,128)(2,1)} %coeff.1.own_at), channel_id=1, source_target_pairs={{0,1},{1,0},{2,3},{3,2},{32,33},{33,32},{34,35},{35,34},{64,65},{6... | collective-permute-start | bytes 589832 | tf_op jit(solution)/shard_map/ppermute | solution.py:342
  16.5 2.5 %copy-start.2 = (bf16[768,128]{1,0:T(8,128)(2,1)}, bf16[768,128]{1,0:T(8,128)(2,1)S(1)}, u32[]{:S(2)}) copy-start(bf16[768,128]{1,0:T(8,128)(2,1)S(1)} %collective-permute-done.1.outer_at) | copy-start | bytes 589828
  19.0 0.7 %copy-start.3 = (bf16[768,128]{1,0:T(8,128)(2,1)}, bf16[768,128]{1,0:T(8,128)(2,1)S(1)}, u32[]{:S(2)}) copy-start(bf16[768,128]{1,0:T(8,128)(2,1)S(1)} %collective-permute-done.inner_at) | copy-start | bytes 589828
  29.8 6.5 %copy-start = (bf16[4,528,128]{2,1,0:T(8,128)(2,1)S(1)}, bf16[4,528,128]{2,1,0:T(8,128)(2,1)}, u32[]{:S(2)}) copy-start(bf16[4,528,128]{2,1,0:T(8,128)(2,1)} %far.1.total_at) | copy-start | bytes 1622020
  29.8 6.4 %copy-start.1 = (bf16[32,64,128]{2,1,0:T(8,128)(2,1)S(1)}, bf16[32,64,128]{2,1,0:T(8,128)(2,1)}, u32[]{:S(2)}) copy-start(bf16[32,64,128]{2,1,0:T(8,128)(2,1)} %param.9) | copy-start | bytes 1572868
  29.8 16.0 %all-to-all-start = ((bf16[8,264,128]{2,1,0:T(8,128)(2,1)}), bf16[8,264,128]{2,1,0:T(8,128)(2,1)S(1)}, u32[]{:S(2)}, u32[]{:S(2)}) async-start(bf16[8,264,128]{2,1,0:T(8,128)(2,1)} %bitcast.5), calls=%async_computation | async-start | bytes 1081344 | tf_op jit(solution)/shard_map/all_to_all | solution.py:372
  45.8 4.4 %collective-permute-start.2 = (bf16[8,264,128]{2,1,0:T(8,128)(2,1)S(1)}, bf16[8,264,128]{2,1,0:T(8,128)(2,1)S(1)}, u32[]{:S(2)}, u32[]{:S(2)}) collective-permute-start(bf16[8,264,128]{2,1,0:T(8,128)(2,1)S(1)} %all-to-all-done.mine_at), channel_id=1, source_target_pairs={{0,4},{4,0},{8,12},{12,8},{16,20},{20,16},{24,28},{28,24},{1,5},{5... | collective-permute-start | bytes 1622024 | tf_op jit(solution)/shard_map/ppermute | solution.py:393

commit v5 on v4

--- a/solution.py
+++ b/solution.py
@@ -44,11 +44,11 @@
     return lax.fori_loop(0, steps // unroll, body, tuple(init))
 
 
-def lane_product(out, left, right_of, blocks, chunks, per, tile_of, start=None, block=8):
+def lane_product(out, left, right_of, blocks, chunks, per, tile_of, start=None, block=8, at=0):
     rows, wide = out.shape[1:]
 
     def outer(blk, _):
-        first = [blk * block + i for i in range(block)]
+        first = [at + blk * block + i for i in range(block)]
         init = [jnp.zeros((rows, wide), F32) if start is None else start[o] for o in first]
 
         def weight(i, group, u):
@@ -85,19 +85,26 @@
         [(samples_at, samples), (basis_at, basis), (transfer_at, transfer)], sem
     )
     vecs = samples.shape[0]
-    even = picked(iota((64, 128), 1) == 2 * iota((64, 128), 0))
-    odd = picked(iota((64, 128), 1) == 2 * iota((64, 128), 0) + 1)
+    row, col = iota((256, 256), 0), iota((256, 256), 1)
+    spread = picked(
+        (row // 64 % 2 == col // 128) & (col % 128 == 2 * (row % 64) + row // 128)
+    )
     copies[0].wait()
     for j in range(64):
         xj[pl.ds(j * vecs, vecs), :] = samples[:, 128 * j : 128 * (j + 1)].astype(F32)
-    for v in range(vecs):
-        turned = xj[pl.ds(v, 64, stride=vecs), :].T
-        both = dot(turned[:64].astype(BF16), even) + dot(turned[64:].astype(BF16), odd)
-        points[:, v, :] = both
+    for v in range(0, vecs, 2):
+        pair = [xj[pl.ds(v + i, 64, stride=vecs), :] for i in range(2)]
+        turned = jnp.concatenate(pair, axis=0).T
+        both = dot(
+            jnp.concatenate([turned[:64], turned[64:]], axis=1).astype(BF16), spread
+        )
+        for i in range(2):
+            points[pl.ds(v + i, 64, stride=vecs), :] = both[:, 128 * i : 128 * (i + 1)]
     copies[1].wait()
     widen(basis, basis_w)
     lane_product(
-        leaf, basis_w, lambda chunk, c: points[chunk * 8 + c], 4, 8, 4,
+        leaf, basis_w,
+        lambda chunk, c: points[pl.ds(pl.multiple_of((chunk * 8 + c) * vecs, 16), vecs), :], 4, 8, 4,
         lambda r, chunk: r * 8 + chunk,
     )
     rounded = leaf[...].astype(BF16)
@@ -141,20 +148,21 @@
     )
 
     first = place * 64 - 64
-    twice = picked(iota((64, 128), 0) == iota((64, 128), 1) % 64)
     none = jnp.zeros((64, 128), BF16)
+    lists = jnp.concatenate([parent_lists[...], parent_lists[...]], axis=1) - first
     for copy in copies[:3]:
         copy.wait()
     packed = jnp.concatenate([before[512:768], own[512:768], after[512:768]], axis=1)
     for k in range(4):
-        index = jnp.broadcast_to(parent_lists[k : k + 1, :] - first, (64, 64))
-        hits = [
-            dot(picked(iota((64, 64), 0) + 64 * m == index), twice).astype(BF16) for m in range(3)
-        ]
+        index = jnp.broadcast_to(lists[k : k + 1, :], (64, 128))
+        parts = []
+        for m in range(3):
+            hit = picked(iota((64, 128), 0) + 64 * m == index)
+            parts += [jnp.concatenate(two, axis=1) for two in ((hit, none), (none, hit))]
+        got = dot(packed, jnp.concatenate(parts, axis=0))
         for h in range(2):
-            parts = [part for hit in hits for part in ((hit, none) if h == 0 else (none, hit))]
-            got = dot(packed, jnp.concatenate(parts, axis=0))
-            source[k, 16 * h : 16 * (h + 1)] = got.reshape(16, 16, 128)
+            part = got[:, 128 * h : 128 * (h + 1)]
+            source[k, 16 * h : 16 * (h + 1)] = part.reshape(16, 16, 128)
 
     copies[3].wait()
 
@@ -177,9 +185,17 @@
 
     first = place * 128 - 128
     rows = jnp.concatenate([before[0:512], own[0:512], after[0:512]], axis=1)
-    for k in range(4):
-        index = jnp.broadcast_to(leaf_lists[k : k + 1, :] - first, (384, 128))
-        source[k] = dot(rows, picked(iota((384, 128), 0) == index)).reshape(32, 16, 128)
+    for k in range(0, 4, 2):
+        hits = [
+            picked(
+                iota((384, 128), 0)
+                == jnp.broadcast_to(leaf_lists[k + i : k + i + 1, :] - first, (384, 128))
+            )
+            for i in range(2)
+        ]
+        got = dot(rows, jnp.concatenate(hits, axis=1))
+        for i in range(2):
+            source[k + i] = got[:, 128 * i : 128 * (i + 1)].reshape(32, 16, 128)
     copies[4].wait()
     widen(leaf_b, coupling_w)
     lane_product(
@@ -188,26 +204,30 @@
     )
     copies[5].wait()
     widen(transfer, transfer_w)
-    lane_product(
-        far, transfer_w, lambda chunk, c: wide[chunk * 8 + c], 4, 4, 4,
-        lambda a, chunk: a * 4 + chunk, start=far,
-    )
-    total = far[...].reshape(512, 128).astype(BF16)
     rows = jnp.concatenate([test[...].astype(F32), jnp.zeros((16, 128 - 32), F32)], axis=1)
+    copies = []
     for h in range(2):
-        payload[264 * h : 264 * h + 256, :] = total[256 * h : 256 * (h + 1)]
-        payload[264 * h + 256 : 264 * h + 264, :] = rows[8 * h : 8 * (h + 1)].astype(BF16)
-    for copy in fetched([(payload, out.at[i]) for i in range(out.shape[0])], sent):
+        lane_product(
+            far, transfer_w, lambda chunk, c: wide[chunk * 8 + c], 2, 4, 4,
+            lambda a, chunk: a * 4 + chunk, start=far, at=16 * h,
+        )
+        payload[h, 0:256, :] = far[16 * h : 16 * (h + 1)].reshape(256, 128).astype(BF16)
+        payload[h, 256:272, :] = rows.astype(BF16)
+        for y in range(out.shape[0] // 2):
+            copy = pltpu.make_async_copy(payload.at[h], out.at[2 * y + h], sent.at[2 * y + h])
+            copy.start()
+            copies.append(copy)
+    for copy in copies:
         copy.wait()
 
 
 def product_kernel(total_at, basis_at, out, total, basis, basis_w, total_w, grid, turned, sem):
-    copies = fetched([(total_at.at[0], total), (basis_at, basis)], sem)
+    copies = fetched([(total_at.at[0:2], total), (basis_at, basis)], sem)
     for copy in copies:
         copy.wait()
     widen(basis, basis_w)
     for h in range(2):
-        rows = total[264 * h : 264 * h + 256, :].astype(F32)
+        rows = total[h, 0:256, :].astype(F32)
         total_w[16 * h : 16 * (h + 1)] = rows.reshape(16, 16, 128)
 
     def outer(blk, _):
@@ -218,7 +238,7 @@
             [jnp.zeros((16, 128), F32)] * 8,
         )
         for i in range(8):
-            grid[blk * 8 + i] = acc[i]
+            grid[pl.ds(pl.multiple_of((blk * 8 + i) * 16, 16), 16), :] = acc[i]
         return 0
 
     lax.fori_loop(0, 8, outer, 0)
@@ -226,43 +246,70 @@
     odd = picked(iota((64, 128), 1) == 2 * iota((64, 128), 0) + 1)
     none = jnp.zeros((64, 128), BF16)
     for v in range(16):
-        mine = grid[:, v, :].astype(BF16)
-        turned[:, v, :] = dot(even, jnp.concatenate([mine, none], axis=0), ((1,), (1,))) + dot(
+        mine = grid[pl.ds(v, 64, stride=16), :].astype(BF16)
+        turned[pl.ds(v, 64, stride=16), :] = dot(even, jnp.concatenate([mine, none], axis=0), ((1,), (1,))) + dot(
             odd, jnp.concatenate([none, mine], axis=0), ((1,), (1,))
         )
     for j in range(64):
-        out[:, 128 * j : 128 * (j + 1)] = turned[j].astype(BF16)
-
-
-def basis_kernel(
-    mine_at, theirs_at, basis_at, new_at, fresh_at,
-    totals, basis, basis_w, compressed, sketch, scale_w, gram, new_basis, fresh, sem, sent,
-):
-    groups = totals.shape[1]
+        out[:, 128 * j : 128 * (j + 1)] = turned[16 * j : 16 * (j + 1), :].astype(BF16)
+
+
+def compress(halves, compressed):
+    groups = range(halves.shape[0])
+    tests = jnp.concatenate([halves[g, 256:272, :] for g in groups], axis=0)
+    across = tests.astype(F32).T[0:32].astype(BF16)
+    for a in range(16):
+        rows = jnp.concatenate([halves[g, 16 * a : 16 * (a + 1), :] for g in groups], axis=0)
+        compressed[a] = dot(across, rows)
+
+
+def part_kernel(mine_at, basis_at, out, halves, basis, basis_w, compressed, partial, sem, sent):
     core = lax.rem(lax.axis_index("vector"), 2)
-    copies = fetched(
-        [(basis_at, basis), (mine_at, totals.at[core]), (theirs_at, totals.at[1 - core])], sem
-    )
+    ranks = pl.ds(pl.multiple_of(core * 1024, 1024), 1024)
+    copies = fetched([(basis_at.at[ranks], basis), (mine_at, halves)], sem)
     copies[0].wait()
     widen(basis, basis_w)
-    for copy in copies[1:]:
-        copy.wait()
-    pairs = [(g, h) for g in range(groups) for h in range(2)]
-    tests = jnp.concatenate([totals[h, g, 256:264, :].astype(F32) for g, h in pairs], axis=0)
-    across = tests.T[0:32].astype(BF16)
-    for a in range(32):
-        at = 16 * (a % 16)
-        rows = jnp.concatenate([totals[a // 16, g, at : at + 16, :] for g in range(groups)], axis=0)
-        compressed[a] = dot(across, rows)
-
-    scale_w[...] = jnp.zeros((32, 128), F32)
+    copies[1].wait()
+    compress(halves, compressed)
 
     def outer(blk, _):
         acc = weighted(
-            8, 32, 16,
-            lambda i, group, u: basis_w[(group * 16 + u) * 8 + blk, i : i + 1, :],
-            lambda group, u: compressed[group * 16 + u],
+            8, 16, 16,
+            lambda i, group, u: basis_w[u * 8 + blk, i : i + 1, :],
+            lambda group, u: compressed[u],
             [jnp.zeros((32, 128), F32)] * 8,
+        )
+        for i in range(8):
+            partial[blk * 8 + i] = acc[i]
+        return 0
+
+    lax.fori_loop(0, 8, outer, 0)
+    for copy in fetched([(partial, out)], sent):
+        copy.wait()
+
+
+def basis_kernel(
+    theirs_at, partial_at, basis_at, new_at, fresh_at,
+    halves, basis, basis_w, compressed, sketch, scale_w, gram, new_basis, fresh, sem, sent,
+):
+    core = 1 - lax.rem(lax.axis_index("vector"), 2)
+    ranks = pl.ds(pl.multiple_of(core * 1024, 1024), 1024)
+    copies = fetched(
+        [(basis_at.at[ranks], basis), (theirs_at, halves), (partial_at, sketch)], sem
+    )
+    copies[0].wait()
+    widen(basis, basis_w)
+    copies[1].wait()
+    compress(halves, compressed)
+    copies[2].wait()
+    scale_w[...] = jnp.zeros((32, 128), F32)
+
+    def outer(blk, _):
+        acc = weighted(
+            8, 16, 16,
+            lambda i, group, u: basis_w[u * 8 + blk, i : i + 1, :],
+            lambda group, u: compressed[u],
+            [sketch[blk * 8 + i] for i in range(8)],
         )
         square = scale_w[...]
         for i in range(8):
@@ -328,7 +375,7 @@
             pltpu.VMEM((256, 8, 128), F32),
             pltpu.VMEM((128, 8, 128), F32),
             pltpu.VMEM((1024, 128), F32),
-            pltpu.VMEM((64, 16, 128), F32),
+            pltpu.VMEM((1024, 128), F32),
             pltpu.VMEM((32, 16, 128), F32),
             pltpu.VMEM((32, 16, 128), F32),
             pltpu.SemaphoreType.DMA((3,)),
@@ -342,10 +389,9 @@
     inner = lax.ppermute(coeff, HOPS, swaps(range(0, peers - 1, 2)))
 
     groups = lax.axis_size("vector")
-    half = groups // 2
     total = pl.pallas_call(
         far_kernel,
-        out_shape=jax.ShapeDtypeStruct((half, 528, 128), BF16),
+        out_shape=jax.ShapeDtypeStruct((groups, 272, 128), BF16),
         in_specs=[anywhere] * 3 + [anywhere] * 3 + [vmem] * 3,
         out_specs=anywhere,
         scratch_shapes=[
@@ -361,27 +407,27 @@
             pltpu.VMEM((32, 16, 128), F32),
             pltpu.VMEM((16, 16, 128), F32),
             pltpu.VMEM((32, 16, 128), F32),
-            pltpu.VMEM((528, 128), BF16),
+            pltpu.VMEM((2, 272, 128), BF16),
             pltpu.SemaphoreType.DMA((6,)),
-            pltpu.SemaphoreType.DMA((half,)),
+            pltpu.SemaphoreType.DMA((groups,)),
         ],
         compiler_params=pltpu.CompilerParams(vmem_limit_bytes=62 << 20),
         name="far",
     )(coeff, inner, outer, moves, near, above, leaf_lists, parent_lists, test_matrix)
 
-    mine = lax.all_to_all(total.reshape(groups, 264, 128), "vector", 0, 0, tiled=True)
+    mine = lax.all_to_all(total, "vector", 0, 0, tiled=True)
     product = pl.pallas_call(
         product_kernel,
         out_shape=jax.ShapeDtypeStruct((16, 8192), BF16),
         in_specs=[anywhere] * 2,
         out_specs=vmem,
         scratch_shapes=[
-            pltpu.VMEM((528, 128), BF16),
+            pltpu.VMEM((2, 272, 128), BF16),
             pltpu.VMEM((2048, 128), BF16),
             pltpu.VMEM((256, 8, 128), F32),
             pltpu.VMEM((32, 16, 128), F32),
-            pltpu.VMEM((64, 16, 128), F32),
-            pltpu.VMEM((64, 16, 128), F32),
+            pltpu.VMEM((1024, 128), F32),
+            pltpu.VMEM((1024, 128), F32),
             pltpu.SemaphoreType.DMA((2,)),
         ],
         cost_estimate=pl.CostEstimate(flops=10**7, bytes_accessed=10**6, transcendentals=0),
@@ -391,6 +437,25 @@
 
     mine, product = lax.optimization_barrier((mine, product))
     theirs = lax.ppermute(mine, "vector", [(i, i ^ 1) for i in range(groups)])
+
+    partial = pl.pallas_call(
+        part_kernel,
+        out_shape=jax.ShapeDtypeStruct((64, 32, 128), F32),
+        in_specs=[anywhere] * 2,
+        out_specs=anywhere,
+        scratch_shapes=[
+            pltpu.VMEM((groups, 272, 128), BF16),
+            pltpu.VMEM((1024, 128), BF16),
+            pltpu.VMEM((128, 8, 128), F32),
+            pltpu.VMEM((16, 32, 128), F32),
+            pltpu.VMEM((64, 32, 128), F32),
+            pltpu.SemaphoreType.DMA((2,)),
+            pltpu.SemaphoreType.DMA((1,)),
+        ],
+        cost_estimate=pl.CostEstimate(flops=10**7, bytes_accessed=10**6, transcendentals=0),
+        compiler_params=pltpu.CompilerParams(vmem_limit_bytes=24 << 20),
+        name="part",
+    )(mine, basis)
 
     new_basis, fresh = pl.pallas_call(
         basis_kernel,
@@ -401,10 +466,10 @@
         in_specs=[anywhere] * 3,
         out_specs=(anywhere, anywhere),
         scratch_shapes=[
-            pltpu.VMEM((2, groups, 264, 128), BF16),
-            pltpu.VMEM((2048, 128), BF16),
-            pltpu.VMEM((256, 8, 128), F32),
-            pltpu.VMEM((32, 32, 128), F32),
+            pltpu.VMEM((groups, 272, 128), BF16),
+            pltpu.VMEM((1024, 128), BF16),
+            pltpu.VMEM((128, 8, 128), F32),
+            pltpu.VMEM((16, 32, 128), F32),
             pltpu.VMEM((64, 32, 128), F32),
             pltpu.VMEM((32, 128), F32),
             pltpu.VMEM((1024, 128), F32),
@@ -415,7 +480,7 @@
         ],
         compiler_params=pltpu.CompilerParams(vmem_limit_bytes=24 << 20),
         name="basis",
-    )(mine, theirs, basis)
+    )(theirs, partial, basis)
     return product, new_basis, fresh
 
 

time: 56.2 us -> 54.8 us (0.975)
  waiting for transfers between devices: 13.5 us -> 12.4 us
    ppermute x1, waiting for transfers between devices: 1.54 us -> 0.01 us  [shards(): theirs = lax.ppermute(mine, 'vector', [(i, i ^ 1) for i in range(groups)])]
    pallas_call x1 -> x2, Pallas kernels: 10.1 us -> 11.2 us  [the longest x1 9.27 us: shards(): pl.pallas_call(far_kernel, out_shape=jax.ShapeDtypeStruct((groups, 272, 1...]
    pallas_call x1, Pallas kernels: 5.72 us -> 4.7 us  [shards(): pl.pallas_call(basis_kernel, out_shape=(jax.ShapeDtypeStruct((64, 32, 128...]
  transfers between devices with their start and end apart: 4 -> 4, of which waited for: 4 -> 3; matrix products, arithmetic and copies ran while one was open for 0% -> 0% of each run, Pallas kernels for 6% -> 9%
where the time goes in v5:
time: 54.8 us; the launch traced here: 54.5 us
  Pallas kernels  23.5 us (43%)
  starting transfers between devices  17.3 us (32%)
  waiting for transfers between devices  12.4 us (23%)
  between operations  0.72 us (1%)
  local copies, waits for them, and re-layouts  0.69 us (1%)
    pallas_call x1, Pallas kernels, shards(): pl.pallas_call(far_kernel, out_shape=jax.ShapeDtypeStruct((groups, 272, 1...  9.27 us
    all_to_all x1, waiting for transfers between devices, shards(): mine = lax.all_to_all(total, 'vector', 0, 0, tiled=True)  6.7 us
    all_to_all x1, starting transfers between devices, shards(): mine = lax.all_to_all(total, 'vector', 0, 0, tiled=True)  6.42 us
    ppermute x1, starting transfers between devices, shards(): outer = lax.ppermute(coeff, HOPS, swaps(range(1, peers - 1, 2)))  6.04 us
    pallas_call x1, Pallas kernels, shards(): pl.pallas_call(basis_kernel, out_shape=(jax.ShapeDtypeStruct((64, 32, 128...  4.7 us
    pallas_call x1, Pallas kernels, shards(): pl.pallas_call(coeff_kernel, out_shape=jax.ShapeDtypeStruct((768, 128), B...  4.58 us
    ppermute x1, waiting for transfers between devices, shards(): outer = lax.ppermute(coeff, HOPS, swaps(range(1, peers - 1, 2)))  3.23 us
    pallas_call x1, Pallas kernels, shards(): pl.pallas_call(product_kernel, out_shape=jax.ShapeDtypeStruct((16, 8192),...  2.99 us
  transfers between devices with their start and end apart: 4, of which 3 were waited for; matrix products, arithmetic and copies ran while one was open for 0% of the time, Pallas kernels for 9%

profile of v5, /device:TPU:385, one launch (start us, length us, event | category | flops | bytes accessed | tf_op | source)
XLA Modules:
  0.0 54.5 jit_solution(13247992984356892630)
XLA Ops:
  0.6 4.6 %coeff.1.own_at = bf16[768,128]{1,0:T(8,128)(2,1)} custom-call(bf16[16,8192]{1,0:T(8,128)(2,1)} %samples_at.1, bf16[2048,128]{1,0:T(8,128)(2,1)} %bitcast.4, bf16[1024,128]{1,0:T(8,128)(2,1)} %bitcast.10), custom_call_target="tpu_custom_call" | custom-call | tf_op jit(solution)/shard_map/coeff/pallas_call | solution.py:366
  5.2 6.0 %collective-permute-start.1 = (bf16[768,128]{1,0:T(8,128)(2,1)}, bf16[768,128]{1,0:T(8,128)(2,1)S(1)}, u32[]{:S(2)}, u32[]{:S(2)}) collective-permute-start(bf16[768,128]{1,0:T(8,128)(2,1)} %coeff.1.own_at), channel_id=1, source_target_pairs={{1,2},{2,1},{3,32},{32,3},{33,34},{34,33},{35,64},{64,35},{65,66},... | collective-permute-start | bytes 589832 | tf_op jit(solution)/shard_map/ppermute | solution.py:388
  11.3 1.9 %collective-permute-start = (bf16[768,128]{1,0:T(8,128)(2,1)}, bf16[768,128]{1,0:T(8,128)(2,1)S(1)}, u32[]{:S(2)}, u32[]{:S(2)}) collective-permute-start(bf16[768,128]{1,0:T(8,128)(2,1)} %coeff.1.own_at), channel_id=1, source_target_pairs={{0,1},{1,0},{2,3},{3,2},{32,33},{33,32},{34,35},{35,34},{64,65},{6... | collective-permute-start | bytes 589832 | tf_op jit(solution)/shard_map/ppermute | solution.py:389
  13.2 3.2 %collective-permute-done.1.outer_at = bf16[768,128]{1,0:T(8,128)(2,1)S(1)} collective-permute-done((bf16[768,128]{1,0:T(8,128)(2,1)}, bf16[768,128]{1,0:T(8,128)(2,1)S(1)}, u32[]{:S(2)}, u32[]{:S(2)}) %collective-permute-start.1) | collective-permute-done | bytes 196640 | tf_op jit(solution)/shard_map/ppermute | solution.py:388
  16.4 0.0 copy-start.2
  16.4 2.5 %collective-permute-done.inner_at = bf16[768,128]{1,0:T(8,128)(2,1)S(1)} collective-permute-done((bf16[768,128]{1,0:T(8,128)(2,1)}, bf16[768,128]{1,0:T(8,128)(2,1)S(1)}, u32[]{:S(2)}, u32[]{:S(2)}) %collective-permute-start) | collective-permute-done | bytes 196640 | tf_op jit(solution)/shard_map/ppermute | solution.py:389
  18.9 0.0 copy-start.3
  18.9 0.0 copy-done.2
  18.9 0.7 %copy-done.3 = bf16[768,128]{1,0:T(8,128)(2,1)} copy-done((bf16[768,128]{1,0:T(8,128)(2,1)}, bf16[768,128]{1,0:T(8,128)(2,1)S(1)}, u32[]{:S(2)}) %copy-start.3) | copy-done | bytes 196632
  19.6 9.3 %far.1.total_at = bf16[8,272,128]{2,1,0:T(8,128)(2,1)} custom-call(bf16[768,128]{1,0:T(8,128)(2,1)} %coeff.1.own_at, bf16[768,128]{1,0:T(8,128)(2,1)} %copy-done.3, bf16[768,128]{1,0:T(8,128)(2,1)} %copy-done.2, bf16[1024,128]{1,0:T(8,128)(2,1)} %bitcast.11, bf16[4096,128]{1,0:T(8,128)(2,1)} %bitcast.8, bf16[4096,64]{1,0:T(8,128)(2,1)} %bitcast.9, ...), custom_call_target="tpu_custom_call" | custom-call | tf_op jit(solution)/shard_map/far/pallas_call | solution.py:392
  28.8 0.0 copy-start
  28.8 0.0 copy-start.1
  28.9 6.4 %all-to-all-start = ((bf16[8,272,128]{2,1,0:T(8,128)(2,1)}), bf16[8,272,128]{2,1,0:T(8,128)(2,1)S(1)}, u32[]{:S(2)}, u32[]{:S(2)}) async-start(bf16[8,272,128]{2,1,0:T(8,128)(2,1)} %far.1.total_at), calls=%async_computation | async-start | bytes 1114112 | tf_op jit(solution)/shard_map/all_to_all | solution.py:418
  35.3 0.0 copy-done
  35.3 0.0 copy-done.1
  35.3 3.0 %product.1 = bf16[16,8192]{1,0:T(8,128)(2,1)} custom-call(bf16[8,272,128]{2,1,0:T(8,128)(2,1)S(1)} %copy-done.1, bf16[2048,128]{1,0:T(8,128)(2,1)S(1)} %bitcast.5), custom_call_target="tpu_custom_call" | custom-call | flops 10000000 | bytes 1000000 | tf_op jit(solution)/shard_map/product/pallas_call | solution.py:419
  38.3 6.7 %all-to-all-done.mine_at = bf16[8,272,128]{2,1,0:T(8,128)(2,1)S(1)} async-done(((bf16[8,272,128]{2,1,0:T(8,128)(2,1)}), bf16[8,272,128]{2,1,0:T(8,128)(2,1)S(1)}, u32[]{:S(2)}, u32[]{:S(2)}) %all-to-all-start) | async-done | bytes 557088 | tf_op jit(solution)/shard_map/all_to_all | solution.py:418
  45.0 2.9 %collective-permute-start.2 = (bf16[8,272,128]{2,1,0:T(8,128)(2,1)S(1)}, bf16[8,272,128]{2,1,0:T(8,128)(2,1)S(1)}, u32[]{:S(2)}, u32[]{:S(2)}) collective-permute-start(bf16[8,272,128]{2,1,0:T(8,128)(2,1)S(1)} %all-to-all-done.mine_at), channel_id=1, source_target_pairs={{0,4},{4,0},{8,12},{12,8},{16,20},{20,16},{24,28},{28,24},{1,5},{5... | collective-permute-start | bytes 1671176 | tf_op jit(solution)/shard_map/ppermute | solution.py:439
  47.9 1.9 %part.1.partial_at = f32[64,32,128]{2,1,0:T(8,128)S(1)} custom-call(bf16[8,272,128]{2,1,0:T(8,128)(2,1)S(1)} %all-to-all-done.mine_at, bf16[2048,128]{1,0:T(8,128)(2,1)S(1)} %bitcast.6), custom_call_target="tpu_custom_call" | custom-call | flops 10000000 | bytes 1000000 | tf_op jit(solution)/shard_map/part/pallas_call | solution.py:441
  49.8 0.0 collective-permute-done.2.theirs_at
  49.8 4.7 %basis.1 = (f32[64,32,128]{2,1,0:T(8,128)}, f32[32,32,128]{2,1,0:T(8,128)}) custom-call(bf16[8,272,128]{2,1,0:T(8,128)(2,1)S(1)} %collective-permute-done.2.theirs_at, f32[64,32,128]{2,1,0:T(8,128)S(1)} %part.1.partial_at, bf16[2048,128]{1,0:T(8,128)(2,1)S(1)} %bitcast.7), custom_call_target="tpu_custom_call" | custom-call | tf_op jit(solution)/shard_map/basis/pallas_call | solution.py:460
Async XLA Ops:
  5.2 11.2 %collective-permute-start.1 = (bf16[768,128]{1,0:T(8,128)(2,1)}, bf16[768,128]{1,0:T(8,128)(2,1)S(1)}, u32[]{:S(2)}, u32[]{:S(2)}) collective-permute-start(bf16[768,128]{1,0:T(8,128)(2,1)} %coeff.1.own_at), channel_id=1, source_target_pairs={{1,2},{2,1},{3,32},{32,3},{33,34},{34,33},{35,64},{64,35},{65,66},... | collective-permute-start | bytes 589832 | tf_op jit(solution)/shard_map/ppermute | solution.py:388
  11.3 7.6 %collective-permute-start = (bf16[768,128]{1,0:T(8,128)(2,1)}, bf16[768,128]{1,0:T(8,128)(2,1)S(1)}, u32[]{:S(2)}, u32[]{:S(2)}) collective-permute-start(bf16[768,128]{1,0:T(8,128)(2,1)} %coeff.1.own_at), channel_id=1, source_target_pairs={{0,1},{1,0},{2,3},{3,2},{32,33},{33,32},{34,35},{35,34},{64,65},{6... | collective-permute-start | bytes 589832 | tf_op jit(solution)/shard_map/ppermute | solution.py:389
  16.4 2.5 %copy-start.2 = (bf16[768,128]{1,0:T(8,128)(2,1)}, bf16[768,128]{1,0:T(8,128)(2,1)S(1)}, u32[]{:S(2)}) copy-start(bf16[768,128]{1,0:T(8,128)(2,1)S(1)} %collective-permute-done.1.outer_at) | copy-start | bytes 589828
  18.9 0.7 %copy-start.3 = (bf16[768,128]{1,0:T(8,128)(2,1)}, bf16[768,128]{1,0:T(8,128)(2,1)S(1)}, u32[]{:S(2)}) copy-start(bf16[768,128]{1,0:T(8,128)(2,1)S(1)} %collective-permute-done.inner_at) | copy-start | bytes 589828
  28.8 6.4 %copy-start = (bf16[32,64,128]{2,1,0:T(8,128)(2,1)S(1)}, bf16[32,64,128]{2,1,0:T(8,128)(2,1)}, u32[]{:S(2)}) copy-start(bf16[32,64,128]{2,1,0:T(8,128)(2,1)} %param.9) | copy-start | bytes 1572868
  28.8 6.4 %copy-start.1 = (bf16[8,272,128]{2,1,0:T(8,128)(2,1)S(1)}, bf16[8,272,128]{2,1,0:T(8,128)(2,1)}, u32[]{:S(2)}) copy-start(bf16[8,272,128]{2,1,0:T(8,128)(2,1)} %far.1.total_at) | copy-start | bytes 1671172
  28.9 16.1 %all-to-all-start = ((bf16[8,272,128]{2,1,0:T(8,128)(2,1)}), bf16[8,272,128]{2,1,0:T(8,128)(2,1)S(1)}, u32[]{:S(2)}, u32[]{:S(2)}) async-start(bf16[8,272,128]{2,1,0:T(8,128)(2,1)} %far.1.total_at), calls=%async_computation | async-start | bytes 1114112 | tf_op jit(solution)/shard_map/all_to_all | solution.py:418
  45.0 4.8 %collective-permute-start.2 = (bf16[8,272,128]{2,1,0:T(8,128)(2,1)S(1)}, bf16[8,272,128]{2,1,0:T(8,128)(2,1)S(1)}, u32[]{:S(2)}, u32[]{:S(2)}) collective-permute-start(bf16[8,272,128]{2,1,0:T(8,128)(2,1)S(1)} %all-to-all-done.mine_at), channel_id=1, source_target_pairs={{0,4},{4,0},{8,12},{12,8},{16,20},{20,16},{24,28},{28,24},{1,5},{5... | collective-permute-start | bytes 1671176 | tf_op jit(solution)/shard_map/ppermute | solution.py:439

commit v6 on v5

--- a/solution.py
+++ b/solution.py
@@ -131,28 +131,37 @@
     out[512:768, :] = (dot(sums[0:256], low) + dot(sums[256:512], high)).astype(BF16)
 
 
+def wide_kernel(coeff, transfer, leaf_b, parent_b, own, transfer_w, coupling_w, parent_w):
+    own[...] = coeff[...]
+    widen(transfer, transfer_w)
+
+    def pack(i, _):
+        low = parent_b[pl.ds(pl.multiple_of(i * 128, 128), 128), :].astype(F32)
+        high = parent_b[pl.ds(pl.multiple_of(2048 + i * 128, 128), 128), :].astype(F32)
+        both = jnp.concatenate([low, high], axis=1)
+        parent_w[pl.ds(i * 16, 16)] = both.reshape(16, 8, 128)
+        return 0
+
+    lax.fori_loop(0, 16, pack, 0)
+    widen(leaf_b, coupling_w)
+
+
 def far_kernel(
-    own_at, inner_at, outer_at, transfer_at, leaf_at, parent_at, leaf_lists, parent_lists, test,
-    out, own, sides, transfer, leaf_b, parent_b,
-    coupling_w, parent_w, transfer_w, source, far, pfar, wide, payload, sem, sent,
+    own, inner, outer, transfer_w, coupling_w, parent_w, leaf_lists, parent_lists, test,
+    out, source, far, pfar, wide, payload, sent,
 ):
     place = lax.axis_index("cluster") * lax.axis_size("replica") + lax.axis_index("replica")
-    odd = lax.rem(place, 2)
-    before, after = sides.at[0], sides.at[1]
-    copies = fetched(
-        [
-            (own_at, own), (inner_at, sides.at[1 - odd]), (outer_at, sides.at[odd]),
-            (parent_at, parent_b), (leaf_at, leaf_b), (transfer_at, transfer),
-        ],
-        sem,
-    )
+    odd = lax.rem(place, 2) == 1
+
+    def three(low, high):
+        one, other = inner[low:high], outer[low:high]
+        before, after = jnp.where(odd, one, other), jnp.where(odd, other, one)
+        return jnp.concatenate([before, own[low:high], after], axis=1)
 
     first = place * 64 - 64
     none = jnp.zeros((64, 128), BF16)
     lists = jnp.concatenate([parent_lists[...], parent_lists[...]], axis=1) - first
-    for copy in copies[:3]:
-        copy.wait()
-    packed = jnp.concatenate([before[512:768], own[512:768], after[512:768]], axis=1)
+    packed = three(512, 768)
     for k in range(4):
         index = jnp.broadcast_to(lists[k : k + 1, :], (64, 128))
         parts = []
@@ -164,16 +173,6 @@
             part = got[:, 128 * h : 128 * (h + 1)]
             source[k, 16 * h : 16 * (h + 1)] = part.reshape(16, 16, 128)
 
-    copies[3].wait()
-
-    def pack(i, _):
-        low = parent_b[pl.ds(pl.multiple_of(i * 128, 128), 128), :].astype(F32)
-        high = parent_b[pl.ds(pl.multiple_of(2048 + i * 128, 128), 128), :].astype(F32)
-        both = jnp.concatenate([low, high], axis=1)
-        parent_w[pl.ds(i * 16, 16)] = both.reshape(16, 8, 128)
-        return 0
-
-    lax.fori_loop(0, 16, pack, 0)
     lane_product(
         pfar, parent_w, lambda chunk, c: source[c % 4, chunk * 2 + c // 4], 2, 16, 4,
         lambda r, chunk: r * 16 + chunk,
@@ -184,7 +183,7 @@
     wide[16:32] = jnp.take_along_axis(flat, lane + 64, axis=1).reshape(16, 16, 128)
 
     first = place * 128 - 128
-    rows = jnp.concatenate([before[0:512], own[0:512], after[0:512]], axis=1)
+    rows = three(0, 512)
     for k in range(0, 4, 2):
         hits = [
             picked(
@@ -196,14 +195,10 @@
         got = dot(rows, jnp.concatenate(hits, axis=1))
         for i in range(2):
             source[k + i] = got[:, 128 * i : 128 * (i + 1)].reshape(32, 16, 128)
-    copies[4].wait()
-    widen(leaf_b, coupling_w)
     lane_product(
         far, coupling_w, lambda chunk, c: source[c % 4, chunk * 2 + c // 4], 4, 16, 4,
         lambda r, chunk: r * 16 + chunk,
     )
-    copies[5].wait()
-    widen(transfer, transfer_w)
     rows = jnp.concatenate([test[...].astype(F32), jnp.zeros((16, 128 - 32), F32)], axis=1)
     copies = []
     for h in range(2):
@@ -221,10 +216,7 @@
         copy.wait()
 
 
-def product_kernel(total_at, basis_at, out, total, basis, basis_w, total_w, grid, turned, sem):
-    copies = fetched([(total_at.at[0:2], total), (basis_at, basis)], sem)
-    for copy in copies:
-        copy.wait()
+def product_kernel(total, basis, out, basis_w, total_w, grid, turned):
     widen(basis, basis_w)
     for h in range(2):
         rows = total[h, 0:256, :].astype(F32)
@@ -263,13 +255,9 @@
         compressed[a] = dot(across, rows)
 
 
-def part_kernel(mine_at, basis_at, out, halves, basis, basis_w, compressed, partial, sem, sent):
+def part_kernel(halves, basis, partial, basis_w, compressed):
     core = lax.rem(lax.axis_index("vector"), 2)
-    ranks = pl.ds(pl.multiple_of(core * 1024, 1024), 1024)
-    copies = fetched([(basis_at.at[ranks], basis), (mine_at, halves)], sem)
-    copies[0].wait()
-    widen(basis, basis_w)
-    copies[1].wait()
+    widen(basis.at[pl.ds(pl.multiple_of(core * 1024, 1024), 1024)], basis_w)
     compress(halves, compressed)
 
     def outer(blk, _):
@@ -284,24 +272,15 @@
         return 0
 
     lax.fori_loop(0, 8, outer, 0)
-    for copy in fetched([(partial, out)], sent):
-        copy.wait()
 
 
 def basis_kernel(
-    theirs_at, partial_at, basis_at, new_at, fresh_at,
-    halves, basis, basis_w, compressed, sketch, scale_w, gram, new_basis, fresh, sem, sent,
+    halves, partial, basis, new_at, fresh_at,
+    basis_w, compressed, sketch, scale_w, gram, new_basis, fresh, sent,
 ):
     core = 1 - lax.rem(lax.axis_index("vector"), 2)
-    ranks = pl.ds(pl.multiple_of(core * 1024, 1024), 1024)
-    copies = fetched(
-        [(basis_at.at[ranks], basis), (theirs_at, halves), (partial_at, sketch)], sem
-    )
-    copies[0].wait()
-    widen(basis, basis_w)
-    copies[1].wait()
+    widen(basis.at[pl.ds(pl.multiple_of(core * 1024, 1024), 1024)], basis_w)
     compress(halves, compressed)
-    copies[2].wait()
     scale_w[...] = jnp.zeros((32, 128), F32)
 
     def outer(blk, _):
@@ -309,7 +288,7 @@
             8, 16, 16,
             lambda i, group, u: basis_w[u * 8 + blk, i : i + 1, :],
             lambda group, u: compressed[u],
-            [sketch[blk * 8 + i] for i in range(8)],
+            [partial[blk * 8 + i] for i in range(8)],
         )
         square = scale_w[...]
         for i in range(8):
@@ -389,46 +368,49 @@
     inner = lax.ppermute(coeff, HOPS, swaps(range(0, peers - 1, 2)))
 
     groups = lax.axis_size("vector")
+    own, transfer_w, coupling_w, parent_w = pl.pallas_call(
+        wide_kernel,
+        out_shape=(
+            jax.ShapeDtypeStruct((768, 128), BF16),
+            jax.ShapeDtypeStruct((128, 8, 128), F32),
+            jax.ShapeDtypeStruct((512, 8, 128), F32),
+            jax.ShapeDtypeStruct((256, 8, 128), F32),
+        ),
+        in_specs=[vmem] * 4,
+        out_specs=(vmem,) * 4,
+        cost_estimate=pl.CostEstimate(flops=10**7, bytes_accessed=10**6, transcendentals=0),
+        compiler_params=pltpu.CompilerParams(vmem_limit_bytes=24 << 20),
+        name="wide",
+    )(coeff, moves, near, above)
+
     total = pl.pallas_call(
         far_kernel,
         out_shape=jax.ShapeDtypeStruct((groups, 272, 128), BF16),
-        in_specs=[anywhere] * 3 + [anywhere] * 3 + [vmem] * 3,
+        in_specs=[vmem] * 9,
         out_specs=anywhere,
         scratch_shapes=[
-            pltpu.VMEM((768, 128), BF16),
-            pltpu.VMEM((2, 768, 128), BF16),
-            pltpu.VMEM((1024, 128), BF16),
-            pltpu.VMEM((4096, 128), BF16),
-            pltpu.VMEM((4096, 64), BF16),
-            pltpu.VMEM((512, 8, 128), F32),
-            pltpu.VMEM((256, 8, 128), F32),
-            pltpu.VMEM((128, 8, 128), F32),
             pltpu.VMEM((4, 32, 16, 128), F32),
             pltpu.VMEM((32, 16, 128), F32),
             pltpu.VMEM((16, 16, 128), F32),
             pltpu.VMEM((32, 16, 128), F32),
             pltpu.VMEM((2, 272, 128), BF16),
-            pltpu.SemaphoreType.DMA((6,)),
             pltpu.SemaphoreType.DMA((groups,)),
         ],
-        compiler_params=pltpu.CompilerParams(vmem_limit_bytes=62 << 20),
+        compiler_params=pltpu.CompilerParams(vmem_limit_bytes=24 << 20),
         name="far",
-    )(coeff, inner, outer, moves, near, above, leaf_lists, parent_lists, test_matrix)
+    )(own, inner, outer, transfer_w, coupling_w, parent_w, leaf_lists, parent_lists, test_matrix)
 
     mine = lax.all_to_all(total, "vector", 0, 0, tiled=True)
     product = pl.pallas_call(
         product_kernel,
         out_shape=jax.ShapeDtypeStruct((16, 8192), BF16),
-        in_specs=[anywhere] * 2,
+        in_specs=[vmem] * 2,
         out_specs=vmem,
         scratch_shapes=[
-            pltpu.VMEM((2, 272, 128), BF16),
-            pltpu.VMEM((2048, 128), BF16),
             pltpu.VMEM((256, 8, 128), F32),
             pltpu.VMEM((32, 16, 128), F32),
             pltpu.VMEM((1024, 128), F32),
             pltpu.VMEM((1024, 128), F32),
-            pltpu.SemaphoreType.DMA((2,)),
         ],
         cost_estimate=pl.CostEstimate(flops=10**7, bytes_accessed=10**6, transcendentals=0),
         compiler_params=pltpu.CompilerParams(vmem_limit_bytes=24 << 20),
@@ -441,16 +423,11 @@
     partial = pl.pallas_call(
         part_kernel,
         out_shape=jax.ShapeDtypeStruct((64, 32, 128), F32),
-        in_specs=[anywhere] * 2,
-        out_specs=anywhere,
+        in_specs=[vmem] * 2,
+        out_specs=vmem,
         scratch_shapes=[
-            pltpu.VMEM((groups, 272, 128), BF16),
-            pltpu.VMEM((1024, 128), BF16),
             pltpu.VMEM((128, 8, 128), F32),
             pltpu.VMEM((16, 32, 128), F32),
-            pltpu.VMEM((64, 32, 128), F32),
-            pltpu.SemaphoreType.DMA((2,)),
-            pltpu.SemaphoreType.DMA((1,)),
         ],
         cost_estimate=pl.CostEstimate(flops=10**7, bytes_accessed=10**6, transcendentals=0),
         compiler_params=pltpu.CompilerParams(vmem_limit_bytes=24 << 20),
@@ -463,11 +440,9 @@
             jax.ShapeDtypeStruct((64, 32, 128), F32),
             jax.ShapeDtypeStruct((32, 32, 128), F32),
         ),
-        in_specs=[anywhere] * 3,
+        in_specs=[vmem] * 3,
         out_specs=(anywhere, anywhere),
         scratch_shapes=[
-            pltpu.VMEM((groups, 272, 128), BF16),
-            pltpu.VMEM((1024, 128), BF16),
             pltpu.VMEM((128, 8, 128), F32),
             pltpu.VMEM((16, 32, 128), F32),
             pltpu.VMEM((64, 32, 128), F32),
@@ -475,7 +450,6 @@
             pltpu.VMEM((1024, 128), F32),
             pltpu.VMEM((64, 32, 128), F32),
             pltpu.VMEM((32, 32, 128), F32),
-            pltpu.SemaphoreType.DMA((3,)),
             pltpu.SemaphoreType.DMA((2,)),
         ],
         compiler_params=pltpu.CompilerParams(vmem_limit_bytes=24 << 20),

time: 54.8 us -> 50.3 us (0.918)
  waiting for transfers between devices: 12.4 us -> 5.88 us
  local copies, waits for them, and re-layouts: 0.69 us -> 4.34 us
  Pallas kernels: 23.5 us -> 22 us
    unnamed x8 -> x16, local copies, waits for them, and re-layouts: 0.69 us -> 4.34 us
    pallas_call x1, Pallas kernels: 9.27 us -> 5.81 us  [shards(): pl.pallas_call(far_kernel, out_shape=jax.ShapeDtypeStruct((groups, 272, 1...]
    ppermute x1, waiting for transfers between devices: 3.23 us -> 0.01 us  [shards(): outer = lax.ppermute(coeff, HOPS, swaps(range(1, peers - 1, 2)))]
    ppermute x1, waiting for transfers between devices: 2.45 us -> 0.01 us  [shards(): inner = lax.ppermute(coeff, HOPS, swaps(range(0, peers - 1, 2)))]
    pallas_call x0 -> x1, Pallas kernels: none -> 1.6 us  [shards(): pl.pallas_call(wide_kernel, out_shape=(jax.ShapeDtypeStruct((768, 128), B...]
    pallas_call x1, Pallas kernels: 2.99 us -> 3.82 us  [shards(): pl.pallas_call(product_kernel, out_shape=jax.ShapeDtypeStruct((16, 8192),...]
    all_to_all x1, waiting for transfers between devices: 6.7 us -> 5.88 us  [shards(): mine = lax.all_to_all(total, 'vector', 0, 0, tiled=True)]
  transfers between devices with their start and end apart: 4 -> 4, of which waited for: 3 -> 1; matrix products, arithmetic and copies ran while one was open for 0% -> 0% of each run, Pallas kernels for 9% -> 14%
where the time goes in v6:
time: 50.3 us; the launch traced here: 49.8 us
  Pallas kernels  22 us (44%)
  starting transfers between devices  16.8 us (33%)
  waiting for transfers between devices  5.88 us (12%)
  local copies, waits for them, and re-layouts  4.34 us (9%)
  between operations  0.78 us (2%)
    ppermute x1, starting transfers between devices, shards(): outer = lax.ppermute(coeff, HOPS, swaps(range(1, peers - 1, 2)))  6.04 us
    all_to_all x1, starting transfers between devices, shards(): mine = lax.all_to_all(total, 'vector', 0, 0, tiled=True)  5.99 us
    all_to_all x1, waiting for transfers between devices, shards(): mine = lax.all_to_all(total, 'vector', 0, 0, tiled=True)  5.88 us
    pallas_call x1, Pallas kernels, shards(): pl.pallas_call(far_kernel, out_shape=jax.ShapeDtypeStruct((groups, 272, 1...  5.81 us
    pallas_call x1, Pallas kernels, shards(): pl.pallas_call(coeff_kernel, out_shape=jax.ShapeDtypeStruct((768, 128), B...  4.6 us
    pallas_call x1, Pallas kernels, shards(): pl.pallas_call(basis_kernel, out_shape=(jax.ShapeDtypeStruct((64, 32, 128...  4.44 us
    unnamed x16, local copies, waits for them, and re-layouts  4.34 us
    pallas_call x1, Pallas kernels, shards(): pl.pallas_call(product_kernel, out_shape=jax.ShapeDtypeStruct((16, 8192),...  3.82 us
  transfers between devices with their start and end apart: 4, of which 1 were waited for; matrix products, arithmetic and copies ran while one was open for 0% of the time, Pallas kernels for 14%

profile of v6, /device:TPU:385, one launch (start us, length us, event | category | flops | bytes accessed | tf_op | source)
XLA Modules:
  0.0 49.8 jit_solution(1642644935475141522)
XLA Ops:
  0.6 0.0 copy-start.5
  0.6 0.0 copy-start.7
  0.7 0.0 copy-start.6
  0.7 4.6 %coeff.1 = bf16[768,128]{1,0:T(8,128)(2,1)} custom-call(bf16[16,8192]{1,0:T(8,128)(2,1)} %samples_at.1, bf16[2048,128]{1,0:T(8,128)(2,1)} %bitcast.4, bf16[1024,128]{1,0:T(8,128)(2,1)} %bitcast.8), custom_call_target="tpu_custom_call" | custom-call | tf_op jit(solution)/shard_map/coeff/pallas_call | solution.py:345
  5.3 6.0 %collective-permute-start.1 = (bf16[768,128]{1,0:T(8,128)(2,1)}, bf16[768,128]{1,0:T(8,128)(2,1)S(1)}, u32[]{:S(2)}, u32[]{:S(2)}) collective-permute-start(bf16[768,128]{1,0:T(8,128)(2,1)} %coeff.1), channel_id=1, source_target_pairs={{1,2},{2,1},{3,32},{32,3},{33,34},{34,33},{35,64},{64,35},{65,66},... | collective-permute-start | bytes 589832 | tf_op jit(solution)/shard_map/ppermute | solution.py:367
  11.3 1.9 %collective-permute-start = (bf16[768,128]{1,0:T(8,128)(2,1)}, bf16[768,128]{1,0:T(8,128)(2,1)S(1)}, u32[]{:S(2)}, u32[]{:S(2)}) collective-permute-start(bf16[768,128]{1,0:T(8,128)(2,1)} %coeff.1), channel_id=1, source_target_pairs={{0,1},{1,0},{2,3},{3,2},{32,33},{33,32},{34,35},{35,34},{64,65},{6... | collective-permute-start | bytes 589832 | tf_op jit(solution)/shard_map/ppermute | solution.py:368
  13.2 0.0 copy-start.1
  13.3 0.9 %copy-done.1 = bf16[32,32,128]{2,1,0:T(8,128)(2,1)S(1)} copy-done((bf16[32,32,128]{2,1,0:T(8,128)(2,1)S(1)}, bf16[32,32,128]{2,1,0:T(8,128)(2,1)}, u32[]{:S(2)}) %copy-start.1) | copy-done | bytes 262168
  14.2 0.0 copy-start.2
  14.2 1.2 %copy-done.2 = bf16[32,32,4,128]{3,2,1,0:T(4,128)(2,1)S(1)} copy-done((bf16[32,32,4,128]{3,2,1,0:T(4,128)(2,1)S(1)}, bf16[32,32,4,128]{3,2,1,0:T(4,128)(2,1)}, u32[]{:S(2)}) %copy-start.2) | copy-done | bytes 1048600
  15.4 0.0 copy-start.3
  15.4 1.2 %copy-done.3 = bf16[32,32,4,64]{3,2,1,0:T(4,128)(2,1)S(1)} copy-done((bf16[32,32,4,64]{3,2,1,0:T(4,128)(2,1)S(1)}, bf16[32,32,4,64]{3,2,1,0:T(4,128)(2,1)}, u32[]{:S(2)}) %copy-start.3) | copy-done | bytes 524312
  16.6 0.0 copy-start.4
  16.6 0.9 %copy-done.4 = bf16[768,128]{1,0:T(8,128)(2,1)S(1)} copy-done((bf16[768,128]{1,0:T(8,128)(2,1)S(1)}, bf16[768,128]{1,0:T(8,128)(2,1)}, u32[]{:S(2)}) %copy-start.4) | copy-done | bytes 196632
  17.6 1.6 %wide.1 = (bf16[768,128]{1,0:T(8,128)(2,1)S(1)}, f32[128,8,128]{2,1,0:T(8,128)S(1)}, f32[512,8,128]{2,1,0:T(8,128)S(1)}, f32[256,8,128]{2,1,0:T(8,128)S(1)}) custom-call(bf16[768,128]{1,0:T(8,128)(2,1)S(1)} %copy-done.4, bf16[1024,128]{1,0:T(8,128)(2,1)S(1)} %bitcast.9, bf16[4096,128]{1,0:T(8,128)(2,1)S(1)} %bitcast.10, bf16[4096,64]{1,0:T(8,128)(2,1)S(1)} %bitcast.11), custom_call_target="tpu_custom_call" | custom-call | flops 10000000 | bytes 1000000 | tf_op jit(solution)/shard_map/wide/pallas_call | solution.py:371
  19.2 0.0 collective-permute-done.1.outer
  19.2 0.0 collective-permute-done.inner
  19.2 0.0 copy-done.5
  19.2 0.0 copy-done.7
  19.2 0.0 copy-done.6
  19.2 0.0 copy-start
  19.2 5.8 %far.1.total = bf16[8,272,128]{2,1,0:T(8,128)(2,1)} custom-call(bf16[768,128]{1,0:T(8,128)(2,1)S(1)} %get-tuple-element.11.own, bf16[768,128]{1,0:T(8,128)(2,1)S(1)} %collective-permute-done.inner, bf16[768,128]{1,0:T(8,128)(2,1)S(1)} %collective-permute-done.1.outer, f32[128,8,128]{2,1,0:T(8,128)S(1)} %get-tuple-element.12.transfer_w, ...), custom_call_target="tpu_custom_call" | custom-call | tf_op jit(solution)/shard_map/far/pallas_call | solution.py:386
  25.1 6.0 %all-to-all-start = ((bf16[8,272,128]{2,1,0:T(8,128)(2,1)}), bf16[8,272,128]{2,1,0:T(8,128)(2,1)S(1)}, u32[]{:S(2)}, u32[]{:S(2)}) async-start(bf16[8,272,128]{2,1,0:T(8,128)(2,1)} %far.1.total), calls=%async_computation | async-start | bytes 1114112 | tf_op jit(solution)/shard_map/all_to_all | solution.py:403
  31.1 0.0 copy-done
  31.1 3.8 %product.1 = bf16[16,8192]{1,0:T(8,128)(2,1)} custom-call(bf16[8,272,128]{2,1,0:T(8,128)(2,1)} %far.1.total, bf16[2048,128]{1,0:T(8,128)(2,1)S(1)} %bitcast.5), custom_call_target="tpu_custom_call" | custom-call | flops 10000000 | bytes 1000000 | tf_op jit(solution)/shard_map/product/pallas_call | solution.py:404
  34.9 5.9 %all-to-all-done.halves = bf16[8,272,128]{2,1,0:T(8,128)(2,1)S(1)} async-done(((bf16[8,272,128]{2,1,0:T(8,128)(2,1)}), bf16[8,272,128]{2,1,0:T(8,128)(2,1)S(1)}, u32[]{:S(2)}, u32[]{:S(2)}) %all-to-all-start) | async-done | bytes 557088 | tf_op jit(solution)/shard_map/all_to_all | solution.py:403
  40.8 2.9 %collective-permute-start.2 = (bf16[8,272,128]{2,1,0:T(8,128)(2,1)S(1)}, bf16[8,272,128]{2,1,0:T(8,128)(2,1)S(1)}, u32[]{:S(2)}, u32[]{:S(2)}) collective-permute-start(bf16[8,272,128]{2,1,0:T(8,128)(2,1)S(1)} %all-to-all-done.halves), channel_id=1, source_target_pairs={{0,4},{4,0},{8,12},{12,8},{16,20},{20,16},{24,28},{28,24},{1,5},{5... | collective-permute-start | bytes 1671176 | tf_op jit(solution)/shard_map/ppermute | solution.py:421
  43.6 1.7 %part.1.partial = f32[64,32,128]{2,1,0:T(8,128)S(1)} custom-call(bf16[8,272,128]{2,1,0:T(8,128)(2,1)S(1)} %all-to-all-done.halves, bf16[2048,128]{1,0:T(8,128)(2,1)S(1)} %bitcast.6), custom_call_target="tpu_custom_call" | custom-call | flops 10000000 | bytes 1000000 | tf_op jit(solution)/shard_map/part/pallas_call | solution.py:423
  45.4 0.0 collective-permute-done.2.halves
  45.4 4.4 %basis.1 = (f32[64,32,128]{2,1,0:T(8,128)}, f32[32,32,128]{2,1,0:T(8,128)}) custom-call(bf16[8,272,128]{2,1,0:T(8,128)(2,1)S(1)} %collective-permute-done.2.halves, f32[64,32,128]{2,1,0:T(8,128)S(1)} %part.1.partial, bf16[2048,128]{1,0:T(8,128)(2,1)S(1)} %bitcast.7), custom_call_target="tpu_custom_call" | custom-call | tf_op jit(solution)/shard_map/basis/pallas_call | solution.py:437
Async XLA Ops:
  0.6 18.6 %copy-start.5 = (bf16[16,32]{1,0:T(8,128)(2,1)S(1)}, bf16[16,32]{1,0:T(8,128)(2,1)}, u32[]{:S(2)}) copy-start(bf16[16,32]{1,0:T(8,128)(2,1)} %test.1) | copy-start | bytes 3076
  0.6 18.6 %copy-start.7 = (s32[4,64]{1,0:T(4,128)S(1)}, s32[4,64]{1,0:T(4,128)}, u32[]{:S(2)}) copy-start(s32[4,64]{1,0:T(4,128)} %parent_lists.1) | copy-start | bytes 3076
  0.7 18.6 %copy-start.6 = (s32[4,128]{1,0:T(4,128)S(1)}, s32[4,128]{1,0:T(4,128)}, u32[]{:S(2)}) copy-start(s32[4,128]{1,0:T(4,128)} %leaf_lists.1) | copy-start | bytes 6148
  5.3 13.9 %collective-permute-start.1 = (bf16[768,128]{1,0:T(8,128)(2,1)}, bf16[768,128]{1,0:T(8,128)(2,1)S(1)}, u32[]{:S(2)}, u32[]{:S(2)}) collective-permute-start(bf16[768,128]{1,0:T(8,128)(2,1)} %coeff.1), channel_id=1, source_target_pairs={{1,2},{2,1},{3,32},{32,3},{33,34},{34,33},{35,64},{64,35},{65,66},... | collective-permute-start | bytes 589832 | tf_op jit(solution)/shard_map/ppermute | solution.py:367
  11.3 7.9 %collective-permute-start = (bf16[768,128]{1,0:T(8,128)(2,1)}, bf16[768,128]{1,0:T(8,128)(2,1)S(1)}, u32[]{:S(2)}, u32[]{:S(2)}) collective-permute-start(bf16[768,128]{1,0:T(8,128)(2,1)} %coeff.1), channel_id=1, source_target_pairs={{0,1},{1,0},{2,3},{3,2},{32,33},{33,32},{34,35},{35,34},{64,65},{6... | collective-permute-start | bytes 589832 | tf_op jit(solution)/shard_map/ppermute | solution.py:368
  13.2 1.0 %copy-start.1 = (bf16[32,32,128]{2,1,0:T(8,128)(2,1)S(1)}, bf16[32,32,128]{2,1,0:T(8,128)(2,1)}, u32[]{:S(2)}) copy-start(bf16[32,32,128]{2,1,0:T(8,128)(2,1)} %param.10) | copy-start | bytes 786436
  14.2 1.2 %copy-start.2 = (bf16[32,32,4,128]{3,2,1,0:T(4,128)(2,1)S(1)}, bf16[32,32,4,128]{3,2,1,0:T(4,128)(2,1)}, u32[]{:S(2)}) copy-start(bf16[32,32,4,128]{3,2,1,0:T(4,128)(2,1)} %param.12) | copy-start | bytes 3145732
  15.4 1.2 %copy-start.3 = (bf16[32,32,4,64]{3,2,1,0:T(4,128)(2,1)S(1)}, bf16[32,32,4,64]{3,2,1,0:T(4,128)(2,1)}, u32[]{:S(2)}) copy-start(bf16[32,32,4,64]{3,2,1,0:T(4,128)(2,1)} %param.14) | copy-start | bytes 1572868
  16.6 0.9 %copy-start.4 = (bf16[768,128]{1,0:T(8,128)(2,1)S(1)}, bf16[768,128]{1,0:T(8,128)(2,1)}, u32[]{:S(2)}) copy-start(bf16[768,128]{1,0:T(8,128)(2,1)} %coeff.1) | copy-start | bytes 589828
  19.2 11.8 %copy-start = (bf16[32,64,128]{2,1,0:T(8,128)(2,1)S(1)}, bf16[32,64,128]{2,1,0:T(8,128)(2,1)}, u32[]{:S(2)}) copy-start(bf16[32,64,128]{2,1,0:T(8,128)(2,1)} %param.9) | copy-start | bytes 1572868
  25.1 15.7 %all-to-all-start = ((bf16[8,272,128]{2,1,0:T(8,128)(2,1)}), bf16[8,272,128]{2,1,0:T(8,128)(2,1)S(1)}, u32[]{:S(2)}, u32[]{:S(2)}) async-start(bf16[8,272,128]{2,1,0:T(8,128)(2,1)} %far.1.total), calls=%async_computation | async-start | bytes 1114112 | tf_op jit(solution)/shard_map/all_to_all | solution.py:403
  40.8 4.6 %collective-permute-start.2 = (bf16[8,272,128]{2,1,0:T(8,128)(2,1)S(1)}, bf16[8,272,128]{2,1,0:T(8,128)(2,1)S(1)}, u32[]{:S(2)}, u32[]{:S(2)}) collective-permute-start(bf16[8,272,128]{2,1,0:T(8,128)(2,1)S(1)} %all-to-all-done.halves), channel_id=1, source_target_pairs={{0,4},{4,0},{8,12},{12,8},{16,20},{20,16},{24,28},{28,24},{1,5},{5... | collective-permute-start | bytes 1671176 | tf_op jit(solution)/shard_map/ppermute | solution.py:421

commit v7 on v6

--- a/solution.py
+++ b/solution.py
@@ -200,16 +200,21 @@
         lambda r, chunk: r * 16 + chunk,
     )
     rows = jnp.concatenate([test[...].astype(F32), jnp.zeros((16, 128 - 32), F32)], axis=1)
+    payload[512:528, :] = rows.astype(BF16)
     copies = []
+    peers = out.shape[0]
     for h in range(2):
         lane_product(
             far, transfer_w, lambda chunk, c: wide[chunk * 8 + c], 2, 4, 4,
             lambda a, chunk: a * 4 + chunk, start=far, at=16 * h,
         )
-        payload[h, 0:256, :] = far[16 * h : 16 * (h + 1)].reshape(256, 128).astype(BF16)
-        payload[h, 256:272, :] = rows.astype(BF16)
-        for y in range(out.shape[0] // 2):
-            copy = pltpu.make_async_copy(payload.at[h], out.at[2 * y + h], sent.at[2 * y + h])
+        low = 256 * h
+        payload[low : low + 256, :] = far[16 * h : 16 * (h + 1)].reshape(256, 128).astype(BF16)
+        sent_rows = pl.ds(low, 256 if h == 0 else 272)
+        for y in range(peers):
+            copy = pltpu.make_async_copy(
+                payload.at[sent_rows], out.at[y, sent_rows], sent.at[peers * h + y]
+            )
             copy.start()
             copies.append(copy)
     for copy in copies:
@@ -218,9 +223,7 @@
 
 def product_kernel(total, basis, out, basis_w, total_w, grid, turned):
     widen(basis, basis_w)
-    for h in range(2):
-        rows = total[h, 0:256, :].astype(F32)
-        total_w[16 * h : 16 * (h + 1)] = rows.reshape(16, 16, 128)
+    total_w[...] = total[0, 0:512, :].astype(F32).reshape(32, 16, 128)
 
     def outer(blk, _):
         acc = weighted(
@@ -246,49 +249,35 @@
         out[:, 128 * j : 128 * (j + 1)] = turned[16 * j : 16 * (j + 1), :].astype(BF16)
 
 
-def compress(halves, compressed):
-    groups = range(halves.shape[0])
-    tests = jnp.concatenate([halves[g, 256:272, :] for g in groups], axis=0)
+def compressed_ranks(totals):
+    groups = range(totals.shape[0])
+    tests = jnp.concatenate([totals[g, 512:528, :] for g in groups], axis=0)
     across = tests.astype(F32).T[0:32].astype(BF16)
-    for a in range(16):
-        rows = jnp.concatenate([halves[g, 16 * a : 16 * (a + 1), :] for g in groups], axis=0)
-        compressed[a] = dot(across, rows)
-
-
-def part_kernel(halves, basis, partial, basis_w, compressed):
-    core = lax.rem(lax.axis_index("vector"), 2)
-    widen(basis.at[pl.ds(pl.multiple_of(core * 1024, 1024), 1024)], basis_w)
-    compress(halves, compressed)
+    for a in range(32):
+        rows = jnp.concatenate([totals[g, 16 * a : 16 * (a + 1), :] for g in groups], axis=0)
+        yield a, dot(across, rows)
+
+
+def part_kernel(mine, partial):
+    for a, part in compressed_ranks(mine):
+        partial[a] = part
+
+
+def basis_kernel(
+    theirs, partial, basis, new_at, fresh_at,
+    basis_w, compressed, sketch, scale_w, gram, new_basis, fresh, sent,
+):
+    widen(basis, basis_w)
+    for a, part in compressed_ranks(theirs):
+        compressed[a] = partial[a] + part
+    scale_w[...] = jnp.zeros((32, 128), F32)
 
     def outer(blk, _):
         acc = weighted(
-            8, 16, 16,
-            lambda i, group, u: basis_w[u * 8 + blk, i : i + 1, :],
-            lambda group, u: compressed[u],
+            8, 32, 16,
+            lambda i, group, u: basis_w[(group * 16 + u) * 8 + blk, i : i + 1, :],
+            lambda group, u: compressed[group * 16 + u],
             [jnp.zeros((32, 128), F32)] * 8,
-        )
-        for i in range(8):
-            partial[blk * 8 + i] = acc[i]
-        return 0
-
-    lax.fori_loop(0, 8, outer, 0)
-
-
-def basis_kernel(
-    halves, partial, basis, new_at, fresh_at,
-    basis_w, compressed, sketch, scale_w, gram, new_basis, fresh, sent,
-):
-    core = 1 - lax.rem(lax.axis_index("vector"), 2)
-    widen(basis.at[pl.ds(pl.multiple_of(core * 1024, 1024), 1024)], basis_w)
-    compress(halves, compressed)
-    scale_w[...] = jnp.zeros((32, 128), F32)
-
-    def outer(blk, _):
-        acc = weighted(
-            8, 16, 16,
-            lambda i, group, u: basis_w[u * 8 + blk, i : i + 1, :],
-            lambda group, u: compressed[u],
-            [partial[blk * 8 + i] for i in range(8)],
         )
         square = scale_w[...]
         for i in range(8):
@@ -307,7 +296,7 @@
         return 0
 
     lax.fori_loop(0, 8, scaled, 0)
-    first = fetched([(new_basis, new_at)], sent)
+    copies = fetched([(new_basis, new_at)], sent)
 
     for tile in range(4):
         low = 8 * tile
@@ -318,17 +307,18 @@
             [jnp.zeros((32 - low, 128), F32)] * 8,
         )
         for i in range(8):
-            gram[(low + i) * 32 + low : (low + i) * 32 + 32, :] = acc[i]
-    for a in range(32):
-        row = scale_w[a : a + 1, :] * (1.0 / 64)
-        low = a // 8 * 8
-        fresh[a, low:32, :] = gram[a * 32 + low : a * 32 + 32, :] * row
-        for b in range(0, low, 8):
-            fresh[a, b : b + 8, :] = gram[pl.ds(b * 32 + a, 8, stride=32), :] * row
-    second = pltpu.make_async_copy(fresh, fresh_at, sent.at[1])
-    second.start()
-    first[0].wait()
-    second.wait()
+            a = low + i
+            row = scale_w[a : a + 1, :] * (1.0 / 64)
+            gram[a * 32 + low : a * 32 + 32, :] = acc[i]
+            fresh[a, low:32, :] = acc[i] * row
+            for b in range(0, low, 8):
+                fresh[a, b : b + 8, :] = gram[pl.ds(b * 32 + a, 8, stride=32), :] * row
+        ranks = pl.ds(low, 8)
+        copy = pltpu.make_async_copy(fresh.at[ranks], fresh_at.at[ranks], sent.at[1 + tile])
+        copy.start()
+        copies.append(copy)
+    for copy in copies:
+        copy.wait()
 
 
 def shards(
@@ -368,6 +358,7 @@
     inner = lax.ppermute(coeff, HOPS, swaps(range(0, peers - 1, 2)))
 
     groups = lax.axis_size("vector")
+    half = groups // 2
     own, transfer_w, coupling_w, parent_w = pl.pallas_call(
         wide_kernel,
         out_shape=(
@@ -385,7 +376,7 @@
 
     total = pl.pallas_call(
         far_kernel,
-        out_shape=jax.ShapeDtypeStruct((groups, 272, 128), BF16),
+        out_shape=jax.ShapeDtypeStruct((half, 528, 128), BF16),
         in_specs=[vmem] * 9,
         out_specs=anywhere,
         scratch_shapes=[
@@ -393,14 +384,16 @@
             pltpu.VMEM((32, 16, 128), F32),
             pltpu.VMEM((16, 16, 128), F32),
             pltpu.VMEM((32, 16, 128), F32),
-            pltpu.VMEM((2, 272, 128), BF16),
+            pltpu.VMEM((528, 128), BF16),
             pltpu.SemaphoreType.DMA((groups,)),
         ],
         compiler_params=pltpu.CompilerParams(vmem_limit_bytes=24 << 20),
         name="far",
     )(own, inner, outer, transfer_w, coupling_w, parent_w, leaf_lists, parent_lists, test_matrix)
 
-    mine = lax.all_to_all(total, "vector", 0, 0, tiled=True)
+    cores = [[2 * y + core for y in range(half)] for core in range(2)]
+    mine = lax.all_to_all(total, "vector", 0, 0, tiled=True, axis_index_groups=cores)
+
     product = pl.pallas_call(
         product_kernel,
         out_shape=jax.ShapeDtypeStruct((16, 8192), BF16),
@@ -422,17 +415,13 @@
 
     partial = pl.pallas_call(
         part_kernel,
-        out_shape=jax.ShapeDtypeStruct((64, 32, 128), F32),
-        in_specs=[vmem] * 2,
+        out_shape=jax.ShapeDtypeStruct((32, 32, 128), F32),
+        in_specs=[vmem],
         out_specs=vmem,
-        scratch_shapes=[
-            pltpu.VMEM((128, 8, 128), F32),
-            pltpu.VMEM((16, 32, 128), F32),
-        ],
         cost_estimate=pl.CostEstimate(flops=10**7, bytes_accessed=10**6, transcendentals=0),
         compiler_params=pltpu.CompilerParams(vmem_limit_bytes=24 << 20),
         name="part",
-    )(mine, basis)
+    )(mine)
 
     new_basis, fresh = pl.pallas_call(
         basis_kernel,
@@ -443,14 +432,14 @@
         in_specs=[vmem] * 3,
         out_specs=(anywhere, anywhere),
         scratch_shapes=[
-            pltpu.VMEM((128, 8, 128), F32),
-            pltpu.VMEM((16, 32, 128), F32),
+            pltpu.VMEM((256, 8, 128), F32),
+            pltpu.VMEM((32, 32, 128), F32),
             pltpu.VMEM((64, 32, 128), F32),
             pltpu.VMEM((32, 128), F32),
             pltpu.VMEM((1024, 128), F32),
             pltpu.VMEM((64, 32, 128), F32),
             pltpu.VMEM((32, 32, 128), F32),
-            pltpu.SemaphoreType.DMA((2,)),
+            pltpu.SemaphoreType.DMA((5,)),
         ],
         compiler_params=pltpu.CompilerParams(vmem_limit_bytes=24 << 20),
         name="basis",

time: 50.3 us -> 49.3 us (0.980)
  the two profiles are of different devices: /device:TPU:385 before, /device:TPU:387 now
where the time goes in v7:
time: 49.3 us; the launch traced here: 48.9 us
  Pallas kernels  21.5 us (44%)
  starting transfers between devices  17 us (34%)
  waiting for transfers between devices  5.34 us (11%)
  local copies, waits for them, and re-layouts  4.34 us (9%)
  between operations  0.76 us (2%)
    pallas_call x1, Pallas kernels, shards(): pl.pallas_call(far_kernel, out_shape=jax.ShapeDtypeStruct((half, 528, 128...  5.81 us
    pallas_call x1, Pallas kernels, shards(): pl.pallas_call(basis_kernel, out_shape=(jax.ShapeDtypeStruct((64, 32, 128...  5.3 us
    ppermute x1, starting transfers between devices, shards(): inner = lax.ppermute(coeff, HOPS, swaps(range(0, peers - 1, 2)))  5.08 us
    pallas_call x1, Pallas kernels, shards(): pl.pallas_call(coeff_kernel, out_shape=jax.ShapeDtypeStruct((768, 128), B...  4.59 us
    ppermute x1, starting transfers between devices, shards(): theirs = lax.ppermute(mine, 'vector', [(i, i ^ 1) for i in range(groups)])  4.56 us
    unnamed x16, local copies, waits for them, and re-layouts  4.34 us
    all_to_all x1, starting transfers between devices, shards(): lax.all_to_all(total, 'vector', 0, 0, tiled=True, axis_index_groups=cores)  4.2 us
    all_to_all x1, waiting for transfers between devices, shards(): lax.all_to_all(total, 'vector', 0, 0, tiled=True, axis_index_groups=cores)  4.12 us
  transfers between devices with their start and end apart: 4, of which 2 were waited for; matrix products, arithmetic and copies ran while one was open for 0% of the time, Pallas kernels for 12%

profile of v7, /device:TPU:387, one launch (start us, length us, event | category | flops | bytes accessed | tf_op | source)
XLA Modules:
  0.0 48.9 jit_solution(8311345360495147594)
XLA Ops:
  0.6 0.0 copy-start.5
  0.6 0.0 copy-start.7
  0.7 0.0 copy-start.6
  0.7 4.6 %coeff.1 = bf16[768,128]{1,0:T(8,128)(2,1)} custom-call(bf16[16,8192]{1,0:T(8,128)(2,1)} %samples_at.1, bf16[2048,128]{1,0:T(8,128)(2,1)} %bitcast.4, bf16[1024,128]{1,0:T(8,128)(2,1)} %bitcast.7), custom_call_target="tpu_custom_call" | custom-call | tf_op jit(solution)/shard_map/coeff/pallas_call | solution.py:335
  5.3 3.1 %collective-permute-start.1 = (bf16[768,128]{1,0:T(8,128)(2,1)}, bf16[768,128]{1,0:T(8,128)(2,1)S(1)}, u32[]{:S(2)}, u32[]{:S(2)}) collective-permute-start(bf16[768,128]{1,0:T(8,128)(2,1)} %coeff.1), channel_id=1, source_target_pairs={{1,2},{2,1},{3,32},{32,3},{33,34},{34,33},{35,64},{64,35},{65,66},... | collective-permute-start | bytes 589832 | tf_op jit(solution)/shard_map/ppermute | solution.py:357
  8.4 5.1 %collective-permute-start = (bf16[768,128]{1,0:T(8,128)(2,1)}, bf16[768,128]{1,0:T(8,128)(2,1)S(1)}, u32[]{:S(2)}, u32[]{:S(2)}) collective-permute-start(bf16[768,128]{1,0:T(8,128)(2,1)} %coeff.1), channel_id=1, source_target_pairs={{0,1},{1,0},{2,3},{3,2},{32,33},{33,32},{34,35},{35,34},{64,65},{6... | collective-permute-start | bytes 589832 | tf_op jit(solution)/shard_map/ppermute | solution.py:358
  13.5 0.0 copy-start.1
  13.5 0.9 %copy-done.1 = bf16[32,32,128]{2,1,0:T(8,128)(2,1)S(1)} copy-done((bf16[32,32,128]{2,1,0:T(8,128)(2,1)S(1)}, bf16[32,32,128]{2,1,0:T(8,128)(2,1)}, u32[]{:S(2)}) %copy-start.1) | copy-done | bytes 262168
  14.4 0.0 copy-start.2
  14.4 1.2 %copy-done.2 = bf16[32,32,4,128]{3,2,1,0:T(4,128)(2,1)S(1)} copy-done((bf16[32,32,4,128]{3,2,1,0:T(4,128)(2,1)S(1)}, bf16[32,32,4,128]{3,2,1,0:T(4,128)(2,1)}, u32[]{:S(2)}) %copy-start.2) | copy-done | bytes 1048600
  15.7 0.0 copy-start.3
  15.7 1.2 %copy-done.3 = bf16[32,32,4,64]{3,2,1,0:T(4,128)(2,1)S(1)} copy-done((bf16[32,32,4,64]{3,2,1,0:T(4,128)(2,1)S(1)}, bf16[32,32,4,64]{3,2,1,0:T(4,128)(2,1)}, u32[]{:S(2)}) %copy-start.3) | copy-done | bytes 524312
  16.9 0.0 copy-start.4
  16.9 0.9 %copy-done.4 = bf16[768,128]{1,0:T(8,128)(2,1)S(1)} copy-done((bf16[768,128]{1,0:T(8,128)(2,1)S(1)}, bf16[768,128]{1,0:T(8,128)(2,1)}, u32[]{:S(2)}) %copy-start.4) | copy-done | bytes 196632
  17.8 1.6 %wide.1 = (bf16[768,128]{1,0:T(8,128)(2,1)S(1)}, f32[128,8,128]{2,1,0:T(8,128)S(1)}, f32[512,8,128]{2,1,0:T(8,128)S(1)}, f32[256,8,128]{2,1,0:T(8,128)S(1)}) custom-call(bf16[768,128]{1,0:T(8,128)(2,1)S(1)} %copy-done.4, bf16[1024,128]{1,0:T(8,128)(2,1)S(1)} %bitcast.8, bf16[4096,128]{1,0:T(8,128)(2,1)S(1)} %bitcast.9, bf16[4096,64]{1,0:T(8,128)(2,1)S(1)} %bitcast.10), custom_call_target="tpu_custom_call" | custom-call | flops 10000000 | bytes 1000000 | tf_op jit(solution)/shard_map/wide/pallas_call | solution.py:362
  19.4 0.0 collective-permute-done.1.outer
  19.4 0.0 collective-permute-done.inner
  19.4 0.0 copy-done.5
  19.5 0.0 copy-done.7
  19.5 0.0 copy-done.6
  19.5 0.0 copy-start
  19.5 5.8 %far.1.total = bf16[4,528,128]{2,1,0:T(8,128)(2,1)} custom-call(bf16[768,128]{1,0:T(8,128)(2,1)S(1)} %get-tuple-element.11.own, bf16[768,128]{1,0:T(8,128)(2,1)S(1)} %collective-permute-done.inner, bf16[768,128]{1,0:T(8,128)(2,1)S(1)} %collective-permute-done.1.outer, f32[128,8,128]{2,1,0:T(8,128)S(1)} %get-tuple-element.12.transfer_w, ...), custom_call_target="tpu_custom_call" | custom-call | tf_op jit(solution)/shard_map/far/pallas_call | solution.py:377
  25.3 4.2 %all-to-all-start = ((bf16[4,528,128]{2,1,0:T(8,128)(2,1)}), bf16[4,528,128]{2,1,0:T(8,128)(2,1)S(1)}, u32[]{:S(2)}, u32[]{:S(2)}) async-start(bf16[4,528,128]{2,1,0:T(8,128)(2,1)} %far.1.total), calls=%async_computation | async-start | bytes 1081344 | tf_op jit(solution)/shard_map/all_to_all | solution.py:395
  29.5 0.0 copy-done
  29.5 3.8 %product.1 = bf16[16,8192]{1,0:T(8,128)(2,1)} custom-call(bf16[4,528,128]{2,1,0:T(8,128)(2,1)} %far.1.total, bf16[2048,128]{1,0:T(8,128)(2,1)S(1)} %bitcast.5), custom_call_target="tpu_custom_call" | custom-call | flops 10000000 | bytes 1000000 | tf_op jit(solution)/shard_map/product/pallas_call | solution.py:397
  33.3 4.1 %all-to-all-done.mine = bf16[4,528,128]{2,1,0:T(8,128)(2,1)S(1)} async-done(((bf16[4,528,128]{2,1,0:T(8,128)(2,1)}), bf16[4,528,128]{2,1,0:T(8,128)(2,1)S(1)}, u32[]{:S(2)}, u32[]{:S(2)}) %all-to-all-start) | async-done | bytes 540704 | tf_op jit(solution)/shard_map/all_to_all | solution.py:395
  37.5 4.6 %collective-permute-start.2 = (bf16[4,528,128]{2,1,0:T(8,128)(2,1)S(1)}, bf16[4,528,128]{2,1,0:T(8,128)(2,1)S(1)}, u32[]{:S(2)}, u32[]{:S(2)}) collective-permute-start(bf16[4,528,128]{2,1,0:T(8,128)(2,1)S(1)} %all-to-all-done.mine), channel_id=1, source_target_pairs={{0,4},{4,0},{8,12},{12,8},{16,20},{20,16},{24,28},{28,24},{1,5},{5... | collective-permute-start | bytes 1622024 | tf_op jit(solution)/shard_map/ppermute | solution.py:414
  42.0 0.3 part.1.partial
  42.3 1.2 %collective-permute-done.2.theirs = bf16[4,528,128]{2,1,0:T(8,128)(2,1)S(1)} collective-permute-done((bf16[4,528,128]{2,1,0:T(8,128)(2,1)S(1)}, bf16[4,528,128]{2,1,0:T(8,128)(2,1)S(1)}, u32[]{:S(2)}, u32[]{:S(2)}) %collective-permute-start.2) | collective-permute-done | bytes 540704 | tf_op jit(solution)/shard_map/ppermute | solution.py:414
  43.6 5.3 %basis.1 = (f32[64,32,128]{2,1,0:T(8,128)}, f32[32,32,128]{2,1,0:T(8,128)}) custom-call(bf16[4,528,128]{2,1,0:T(8,128)(2,1)S(1)} %collective-permute-done.2.theirs, f32[32,32,128]{2,1,0:T(8,128)S(1)} %part.1.partial, bf16[2048,128]{1,0:T(8,128)(2,1)S(1)} %bitcast.6), custom_call_target="tpu_custom_call" | custom-call | tf_op jit(solution)/shard_map/basis/pallas_call | solution.py:426
Async XLA Ops:
  0.6 18.8 %copy-start.5 = (bf16[16,32]{1,0:T(8,128)(2,1)S(1)}, bf16[16,32]{1,0:T(8,128)(2,1)}, u32[]{:S(2)}) copy-start(bf16[16,32]{1,0:T(8,128)(2,1)} %test.1) | copy-start | bytes 3076
  0.6 18.8 %copy-start.7 = (s32[4,64]{1,0:T(4,128)S(1)}, s32[4,64]{1,0:T(4,128)}, u32[]{:S(2)}) copy-start(s32[4,64]{1,0:T(4,128)} %parent_lists.1) | copy-start | bytes 3076
  0.7 18.8 %copy-start.6 = (s32[4,128]{1,0:T(4,128)S(1)}, s32[4,128]{1,0:T(4,128)}, u32[]{:S(2)}) copy-start(s32[4,128]{1,0:T(4,128)} %leaf_lists.1) | copy-start | bytes 6148
  5.3 14.2 %collective-permute-start.1 = (bf16[768,128]{1,0:T(8,128)(2,1)}, bf16[768,128]{1,0:T(8,128)(2,1)S(1)}, u32[]{:S(2)}, u32[]{:S(2)}) collective-permute-start(bf16[768,128]{1,0:T(8,128)(2,1)} %coeff.1), channel_id=1, source_target_pairs={{1,2},{2,1},{3,32},{32,3},{33,34},{34,33},{35,64},{64,35},{65,66},... | collective-permute-start | bytes 589832 | tf_op jit(solution)/shard_map/ppermute | solution.py:357
  8.4 11.0 %collective-permute-start = (bf16[768,128]{1,0:T(8,128)(2,1)}, bf16[768,128]{1,0:T(8,128)(2,1)S(1)}, u32[]{:S(2)}, u32[]{:S(2)}) collective-permute-start(bf16[768,128]{1,0:T(8,128)(2,1)} %coeff.1), channel_id=1, source_target_pairs={{0,1},{1,0},{2,3},{3,2},{32,33},{33,32},{34,35},{35,34},{64,65},{6... | collective-permute-start | bytes 589832 | tf_op jit(solution)/shard_map/ppermute | solution.py:358
  13.5 1.0 %copy-start.1 = (bf16[32,32,128]{2,1,0:T(8,128)(2,1)S(1)}, bf16[32,32,128]{2,1,0:T(8,128)(2,1)}, u32[]{:S(2)}) copy-start(bf16[32,32,128]{2,1,0:T(8,128)(2,1)} %param.10) | copy-start | bytes 786436
  14.4 1.2 %copy-start.2 = (bf16[32,32,4,128]{3,2,1,0:T(4,128)(2,1)S(1)}, bf16[32,32,4,128]{3,2,1,0:T(4,128)(2,1)}, u32[]{:S(2)}) copy-start(bf16[32,32,4,128]{3,2,1,0:T(4,128)(2,1)} %param.12) | copy-start | bytes 3145732
  15.7 1.2 %copy-start.3 = (bf16[32,32,4,64]{3,2,1,0:T(4,128)(2,1)S(1)}, bf16[32,32,4,64]{3,2,1,0:T(4,128)(2,1)}, u32[]{:S(2)}) copy-start(bf16[32,32,4,64]{3,2,1,0:T(4,128)(2,1)} %param.14) | copy-start | bytes 1572868
  16.9 0.9 %copy-start.4 = (bf16[768,128]{1,0:T(8,128)(2,1)S(1)}, bf16[768,128]{1,0:T(8,128)(2,1)}, u32[]{:S(2)}) copy-start(bf16[768,128]{1,0:T(8,128)(2,1)} %coeff.1) | copy-start | bytes 589828
  19.5 10.0 %copy-start = (bf16[32,64,128]{2,1,0:T(8,128)(2,1)S(1)}, bf16[32,64,128]{2,1,0:T(8,128)(2,1)}, u32[]{:S(2)}) copy-start(bf16[32,64,128]{2,1,0:T(8,128)(2,1)} %param.9) | copy-start | bytes 1572868
  25.3 12.1 %all-to-all-start = ((bf16[4,528,128]{2,1,0:T(8,128)(2,1)}), bf16[4,528,128]{2,1,0:T(8,128)(2,1)S(1)}, u32[]{:S(2)}, u32[]{:S(2)}) async-start(bf16[4,528,128]{2,1,0:T(8,128)(2,1)} %far.1.total), calls=%async_computation | async-start | bytes 1081344 | tf_op jit(solution)/shard_map/all_to_all | solution.py:395
  37.5 6.1 %collective-permute-start.2 = (bf16[4,528,128]{2,1,0:T(8,128)(2,1)S(1)}, bf16[4,528,128]{2,1,0:T(8,128)(2,1)S(1)}, u32[]{:S(2)}, u32[]{:S(2)}) collective-permute-start(bf16[4,528,128]{2,1,0:T(8,128)(2,1)S(1)} %all-to-all-done.mine), channel_id=1, source_target_pairs={{0,4},{4,0},{8,12},{12,8},{16,20},{20,16},{24,28},{28,24},{1,5},{5... | collective-permute-start | bytes 1622024 | tf_op jit(solution)/shard_map/ppermute | solution.py:414

commit v8 on v7

--- a/solution.py
+++ b/solution.py
@@ -78,8 +78,8 @@
 
 
 def coeff_kernel(
-    samples_at, basis_at, transfer_at, out,
-    samples, basis, transfer, basis_w, transfer_w, xj, points, leaf, parent, sem,
+    samples_at, basis_at, transfer_at, out_at,
+    samples, basis, transfer, basis_w, transfer_w, xj, points, leaf, parent, out, sem, sent,
 ):
     copies = fetched(
         [(samples_at, samples), (basis_at, basis), (transfer_at, transfer)], sem
@@ -109,6 +109,8 @@
     )
     rounded = leaf[...].astype(BF16)
     out[0:512, :] = rounded.reshape(512, 128)
+    first = pltpu.make_async_copy(out.at[0:512], out_at.at[0:512], sent.at[0])
+    first.start()
     leaf[...] = rounded.astype(F32)
     copies[2].wait()
     widen(transfer, transfer_w)
@@ -129,6 +131,10 @@
     high = picked(iota((128, 128), 0) == 2 * iota((128, 128), 1) - 128)
     sums = parent[...].reshape(512, 128).astype(BF16)
     out[512:768, :] = (dot(sums[0:256], low) + dot(sums[256:512], high)).astype(BF16)
+    second = pltpu.make_async_copy(out.at[512:768], out_at.at[512:768], sent.at[1])
+    second.start()
+    first.wait()
+    second.wait()
 
 
 def wide_kernel(coeff, transfer, leaf_b, parent_b, own, transfer_w, coupling_w, parent_w):
@@ -249,27 +255,23 @@
         out[:, 128 * j : 128 * (j + 1)] = turned[16 * j : 16 * (j + 1), :].astype(BF16)
 
 
-def compressed_ranks(totals):
+def part_kernel(totals, partial):
     groups = range(totals.shape[0])
     tests = jnp.concatenate([totals[g, 512:528, :] for g in groups], axis=0)
     across = tests.astype(F32).T[0:32].astype(BF16)
     for a in range(32):
         rows = jnp.concatenate([totals[g, 16 * a : 16 * (a + 1), :] for g in groups], axis=0)
-        yield a, dot(across, rows)
-
-
-def part_kernel(mine, partial):
-    for a, part in compressed_ranks(mine):
-        partial[a] = part
+        partial[32 * a : 32 * (a + 1), :] = dot(across, rows).astype(BF16)
 
 
 def basis_kernel(
-    theirs, partial, basis, new_at, fresh_at,
+    mine, theirs, basis, new_at, fresh_at,
     basis_w, compressed, sketch, scale_w, gram, new_basis, fresh, sent,
 ):
     widen(basis, basis_w)
-    for a, part in compressed_ranks(theirs):
-        compressed[a] = partial[a] + part
+    for a in range(0, 1024, 128):
+        both = mine[a : a + 128, :].astype(F32) + theirs[a : a + 128, :].astype(F32)
+        compressed[a // 32 : a // 32 + 4] = both.reshape(4, 32, 128)
     scale_w[...] = jnp.zeros((32, 128), F32)
 
     def outer(blk, _):
@@ -336,7 +338,7 @@
         coeff_kernel,
         out_shape=jax.ShapeDtypeStruct((768, 128), BF16),
         in_specs=[anywhere] * 3,
-        out_specs=vmem,
+        out_specs=anywhere,
         scratch_shapes=[
             pltpu.VMEM((16, 8192), BF16),
             pltpu.VMEM((2048, 128), BF16),
@@ -347,7 +349,9 @@
             pltpu.VMEM((1024, 128), F32),
             pltpu.VMEM((32, 16, 128), F32),
             pltpu.VMEM((32, 16, 128), F32),
+            pltpu.VMEM((768, 128), BF16),
             pltpu.SemaphoreType.DMA((3,)),
+            pltpu.SemaphoreType.DMA((2,)),
         ],
         compiler_params=pltpu.CompilerParams(vmem_limit_bytes=62 << 20),
         name="coeff",
@@ -411,17 +415,16 @@
     )(total, basis)
 
     mine, product = lax.optimization_barrier((mine, product))
-    theirs = lax.ppermute(mine, "vector", [(i, i ^ 1) for i in range(groups)])
-
     partial = pl.pallas_call(
         part_kernel,
-        out_shape=jax.ShapeDtypeStruct((32, 32, 128), F32),
+        out_shape=jax.ShapeDtypeStruct((1024, 128), BF16),
         in_specs=[vmem],
         out_specs=vmem,
         cost_estimate=pl.CostEstimate(flops=10**7, bytes_accessed=10**6, transcendentals=0),
         compiler_params=pltpu.CompilerParams(vmem_limit_bytes=24 << 20),
         name="part",
     )(mine)
+    theirs = lax.ppermute(partial, "vector", [(i, i ^ 1) for i in range(groups)])
 
     new_basis, fresh = pl.pallas_call(
         basis_kernel,
@@ -443,7 +446,7 @@
         ],
         compiler_params=pltpu.CompilerParams(vmem_limit_bytes=24 << 20),
         name="basis",
-    )(theirs, partial, basis)
+    )(partial, theirs, basis)
     return product, new_basis, fresh
 
 

time: 49.3 us -> 48.9 us (level)
  transfers between devices with their start and end apart: 4 -> 4, of which waited for: 2 -> 2; matrix products, arithmetic and copies ran while one was open for 0% -> 0% of each run, Pallas kernels for 12% -> 11%
where the time goes in v8:
time: 48.9 us; the launch traced here: 48.5 us
  Pallas kernels  21.1 us (43%)
  starting transfers between devices  17 us (35%)
  waiting for transfers between devices  5.26 us (11%)
  local copies, waits for them, and re-layouts  4.34 us (9%)
  between operations  0.77 us (2%)
    pallas_call x1, Pallas kernels, shards(): pl.pallas_call(far_kernel, out_shape=jax.ShapeDtypeStruct((half, 528, 128...  5.81 us
    ppermute x1, starting transfers between devices, shards(): inner = lax.ppermute(coeff, HOPS, swaps(range(0, peers - 1, 2)))  5.08 us
    pallas_call x1, Pallas kernels, shards(): pl.pallas_call(basis_kernel, out_shape=(jax.ShapeDtypeStruct((64, 32, 128...  5.03 us
    ppermute x1, starting transfers between devices, shards(): lax.ppermute(partial, 'vector', [(i, i ^ 1) for i in range(groups)])  4.58 us
    pallas_call x1, Pallas kernels, shards(): pl.pallas_call(coeff_kernel, out_shape=jax.ShapeDtypeStruct((768, 128), B...  4.56 us
    unnamed x16, local copies, waits for them, and re-layouts  4.34 us
    all_to_all x1, starting transfers between devices, shards(): lax.all_to_all(total, 'vector', 0, 0, tiled=True, axis_index_groups=cores)  4.2 us
    all_to_all x1, waiting for transfers between devices, shards(): lax.all_to_all(total, 'vector', 0, 0, tiled=True, axis_index_groups=cores)  4.12 us
  transfers between devices with their start and end apart: 4, of which 2 were waited for; matrix products, arithmetic and copies ran while one was open for 0% of the time, Pallas kernels for 11%

profile of v8, /device:TPU:387, one launch (start us, length us, event | category | flops | bytes accessed | tf_op | source)
XLA Modules:
  0.0 48.5 jit_solution(2386654271029737420)
XLA Ops:
  0.6 0.0 copy-start.5
  0.6 0.0 copy-start.7
  0.7 0.0 copy-start.6
  0.7 4.6 %coeff.1 = bf16[768,128]{1,0:T(8,128)(2,1)} custom-call(bf16[16,8192]{1,0:T(8,128)(2,1)} %samples_at.1, bf16[2048,128]{1,0:T(8,128)(2,1)} %bitcast.4, bf16[1024,128]{1,0:T(8,128)(2,1)} %bitcast.7), custom_call_target="tpu_custom_call" | custom-call | tf_op jit(solution)/shard_map/coeff/pallas_call | solution.py:337
  5.2 3.1 %collective-permute-start.1 = (bf16[768,128]{1,0:T(8,128)(2,1)}, bf16[768,128]{1,0:T(8,128)(2,1)S(1)}, u32[]{:S(2)}, u32[]{:S(2)}) collective-permute-start(bf16[768,128]{1,0:T(8,128)(2,1)} %coeff.1), channel_id=1, source_target_pairs={{1,2},{2,1},{3,32},{32,3},{33,34},{34,33},{35,64},{64,35},{65,66},... | collective-permute-start | bytes 589832 | tf_op jit(solution)/shard_map/ppermute | solution.py:361
  8.4 5.1 %collective-permute-start = (bf16[768,128]{1,0:T(8,128)(2,1)}, bf16[768,128]{1,0:T(8,128)(2,1)S(1)}, u32[]{:S(2)}, u32[]{:S(2)}) collective-permute-start(bf16[768,128]{1,0:T(8,128)(2,1)} %coeff.1), channel_id=1, source_target_pairs={{0,1},{1,0},{2,3},{3,2},{32,33},{33,32},{34,35},{35,34},{64,65},{6... | collective-permute-start | bytes 589832 | tf_op jit(solution)/shard_map/ppermute | solution.py:362
  13.5 0.0 copy-start.1
  13.5 0.9 %copy-done.1 = bf16[32,32,128]{2,1,0:T(8,128)(2,1)S(1)} copy-done((bf16[32,32,128]{2,1,0:T(8,128)(2,1)S(1)}, bf16[32,32,128]{2,1,0:T(8,128)(2,1)}, u32[]{:S(2)}) %copy-start.1) | copy-done | bytes 262168
  14.4 0.0 copy-start.2
  14.4 1.2 %copy-done.2 = bf16[32,32,4,128]{3,2,1,0:T(4,128)(2,1)S(1)} copy-done((bf16[32,32,4,128]{3,2,1,0:T(4,128)(2,1)S(1)}, bf16[32,32,4,128]{3,2,1,0:T(4,128)(2,1)}, u32[]{:S(2)}) %copy-start.2) | copy-done | bytes 1048600
  15.6 0.0 copy-start.3
  15.6 1.2 %copy-done.3 = bf16[32,32,4,64]{3,2,1,0:T(4,128)(2,1)S(1)} copy-done((bf16[32,32,4,64]{3,2,1,0:T(4,128)(2,1)S(1)}, bf16[32,32,4,64]{3,2,1,0:T(4,128)(2,1)}, u32[]{:S(2)}) %copy-start.3) | copy-done | bytes 524312
  16.9 0.0 copy-start.4
  16.9 0.9 %copy-done.4 = bf16[768,128]{1,0:T(8,128)(2,1)S(1)} copy-done((bf16[768,128]{1,0:T(8,128)(2,1)S(1)}, bf16[768,128]{1,0:T(8,128)(2,1)}, u32[]{:S(2)}) %copy-start.4) | copy-done | bytes 196632
  17.8 1.6 %wide.1 = (bf16[768,128]{1,0:T(8,128)(2,1)S(1)}, f32[128,8,128]{2,1,0:T(8,128)S(1)}, f32[512,8,128]{2,1,0:T(8,128)S(1)}, f32[256,8,128]{2,1,0:T(8,128)S(1)}) custom-call(bf16[768,128]{1,0:T(8,128)(2,1)S(1)} %copy-done.4, bf16[1024,128]{1,0:T(8,128)(2,1)S(1)} %bitcast.8, bf16[4096,128]{1,0:T(8,128)(2,1)S(1)} %bitcast.9, bf16[4096,64]{1,0:T(8,128)(2,1)S(1)} %bitcast.10), custom_call_target="tpu_custom_call" | custom-call | flops 10000000 | bytes 1000000 | tf_op jit(solution)/shard_map/wide/pallas_call | solution.py:366
  19.4 0.0 collective-permute-done.1.outer
  19.4 0.0 collective-permute-done.inner
  19.4 0.0 copy-done.5
  19.4 0.0 copy-done.7
  19.4 0.0 copy-done.6
  19.4 0.0 copy-start
  19.5 5.8 %far.1.total = bf16[4,528,128]{2,1,0:T(8,128)(2,1)} custom-call(bf16[768,128]{1,0:T(8,128)(2,1)S(1)} %get-tuple-element.11.own, bf16[768,128]{1,0:T(8,128)(2,1)S(1)} %collective-permute-done.inner, bf16[768,128]{1,0:T(8,128)(2,1)S(1)} %collective-permute-done.1.outer, f32[128,8,128]{2,1,0:T(8,128)S(1)} %get-tuple-element.12.transfer_w, ...), custom_call_target="tpu_custom_call" | custom-call | tf_op jit(solution)/shard_map/far/pallas_call | solution.py:381
  25.3 4.2 %all-to-all-start = ((bf16[4,528,128]{2,1,0:T(8,128)(2,1)}), bf16[4,528,128]{2,1,0:T(8,128)(2,1)S(1)}, u32[]{:S(2)}, u32[]{:S(2)}) async-start(bf16[4,528,128]{2,1,0:T(8,128)(2,1)} %far.1.total), calls=%async_computation | async-start | bytes 1081344 | tf_op jit(solution)/shard_map/all_to_all | solution.py:399
  29.5 0.0 copy-done
  29.5 3.8 %product.1 = bf16[16,8192]{1,0:T(8,128)(2,1)} custom-call(bf16[4,528,128]{2,1,0:T(8,128)(2,1)} %far.1.total, bf16[2048,128]{1,0:T(8,128)(2,1)S(1)} %bitcast.5), custom_call_target="tpu_custom_call" | custom-call | flops 10000000 | bytes 1000000 | tf_op jit(solution)/shard_map/product/pallas_call | solution.py:401
  33.3 4.1 %all-to-all-done.totals = bf16[4,528,128]{2,1,0:T(8,128)(2,1)S(1)} async-done(((bf16[4,528,128]{2,1,0:T(8,128)(2,1)}), bf16[4,528,128]{2,1,0:T(8,128)(2,1)S(1)}, u32[]{:S(2)}, u32[]{:S(2)}) %all-to-all-start) | async-done | bytes 540704 | tf_op jit(solution)/shard_map/all_to_all | solution.py:399
  37.4 0.3 part.1.mine
  37.7 4.6 %collective-permute-start.2 = (bf16[1024,128]{1,0:T(8,128)(2,1)S(1)}, bf16[1024,128]{1,0:T(8,128)(2,1)S(1)}, u32[]{:S(2)}, u32[]{:S(2)}) collective-permute-start(bf16[1024,128]{1,0:T(8,128)(2,1)S(1)} %part.1.mine), channel_id=1, source_target_pairs={{0,4},{4,0},{8,12},{12,8},{16,20},{20,16},{24,28},{28,24},{1,5},{5... | collective-permute-start | bytes 786440 | tf_op jit(solution)/shard_map/ppermute | solution.py:427
  42.3 1.1 %collective-permute-done.2.theirs = bf16[1024,128]{1,0:T(8,128)(2,1)S(1)} collective-permute-done((bf16[1024,128]{1,0:T(8,128)(2,1)S(1)}, bf16[1024,128]{1,0:T(8,128)(2,1)S(1)}, u32[]{:S(2)}, u32[]{:S(2)}) %collective-permute-start.2) | collective-permute-done | bytes 262176 | tf_op jit(solution)/shard_map/ppermute | solution.py:427
  43.5 5.0 %basis.1 = (f32[64,32,128]{2,1,0:T(8,128)}, f32[32,32,128]{2,1,0:T(8,128)}) custom-call(bf16[1024,128]{1,0:T(8,128)(2,1)S(1)} %part.1.mine, bf16[1024,128]{1,0:T(8,128)(2,1)S(1)} %collective-permute-done.2.theirs, bf16[2048,128]{1,0:T(8,128)(2,1)S(1)} %bitcast.6), custom_call_target="tpu_custom_call" | custom-call | tf_op jit(solution)/shard_map/basis/pallas_call | solution.py:429
Async XLA Ops:
  0.6 18.8 %copy-start.5 = (bf16[16,32]{1,0:T(8,128)(2,1)S(1)}, bf16[16,32]{1,0:T(8,128)(2,1)}, u32[]{:S(2)}) copy-start(bf16[16,32]{1,0:T(8,128)(2,1)} %test.1) | copy-start | bytes 3076
  0.6 18.8 %copy-start.7 = (s32[4,64]{1,0:T(4,128)S(1)}, s32[4,64]{1,0:T(4,128)}, u32[]{:S(2)}) copy-start(s32[4,64]{1,0:T(4,128)} %parent_lists.1) | copy-start | bytes 3076
  0.7 18.8 %copy-start.6 = (s32[4,128]{1,0:T(4,128)S(1)}, s32[4,128]{1,0:T(4,128)}, u32[]{:S(2)}) copy-start(s32[4,128]{1,0:T(4,128)} %leaf_lists.1) | copy-start | bytes 6148
  5.2 14.2 %collective-permute-start.1 = (bf16[768,128]{1,0:T(8,128)(2,1)}, bf16[768,128]{1,0:T(8,128)(2,1)S(1)}, u32[]{:S(2)}, u32[]{:S(2)}) collective-permute-start(bf16[768,128]{1,0:T(8,128)(2,1)} %coeff.1), channel_id=1, source_target_pairs={{1,2},{2,1},{3,32},{32,3},{33,34},{34,33},{35,64},{64,35},{65,66},... | collective-permute-start | bytes 589832 | tf_op jit(solution)/shard_map/ppermute | solution.py:361
  8.4 11.0 %collective-permute-start = (bf16[768,128]{1,0:T(8,128)(2,1)}, bf16[768,128]{1,0:T(8,128)(2,1)S(1)}, u32[]{:S(2)}, u32[]{:S(2)}) collective-permute-start(bf16[768,128]{1,0:T(8,128)(2,1)} %coeff.1), channel_id=1, source_target_pairs={{0,1},{1,0},{2,3},{3,2},{32,33},{33,32},{34,35},{35,34},{64,65},{6... | collective-permute-start | bytes 589832 | tf_op jit(solution)/shard_map/ppermute | solution.py:362
  13.5 1.0 %copy-start.1 = (bf16[32,32,128]{2,1,0:T(8,128)(2,1)S(1)}, bf16[32,32,128]{2,1,0:T(8,128)(2,1)}, u32[]{:S(2)}) copy-start(bf16[32,32,128]{2,1,0:T(8,128)(2,1)} %param.10) | copy-start | bytes 786436
  14.4 1.2 %copy-start.2 = (bf16[32,32,4,128]{3,2,1,0:T(4,128)(2,1)S(1)}, bf16[32,32,4,128]{3,2,1,0:T(4,128)(2,1)}, u32[]{:S(2)}) copy-start(bf16[32,32,4,128]{3,2,1,0:T(4,128)(2,1)} %param.12) | copy-start | bytes 3145732
  15.6 1.2 %copy-start.3 = (bf16[32,32,4,64]{3,2,1,0:T(4,128)(2,1)S(1)}, bf16[32,32,4,64]{3,2,1,0:T(4,128)(2,1)}, u32[]{:S(2)}) copy-start(bf16[32,32,4,64]{3,2,1,0:T(4,128)(2,1)} %param.14) | copy-start | bytes 1572868
  16.9 0.9 %copy-start.4 = (bf16[768,128]{1,0:T(8,128)(2,1)S(1)}, bf16[768,128]{1,0:T(8,128)(2,1)}, u32[]{:S(2)}) copy-start(bf16[768,128]{1,0:T(8,128)(2,1)} %coeff.1) | copy-start | bytes 589828
  19.4 10.0 %copy-start = (bf16[32,64,128]{2,1,0:T(8,128)(2,1)S(1)}, bf16[32,64,128]{2,1,0:T(8,128)(2,1)}, u32[]{:S(2)}) copy-start(bf16[32,64,128]{2,1,0:T(8,128)(2,1)} %param.9) | copy-start | bytes 1572868
  25.3 12.1 %all-to-all-start = ((bf16[4,528,128]{2,1,0:T(8,128)(2,1)}), bf16[4,528,128]{2,1,0:T(8,128)(2,1)S(1)}, u32[]{:S(2)}, u32[]{:S(2)}) async-start(bf16[4,528,128]{2,1,0:T(8,128)(2,1)} %far.1.total), calls=%async_computation | async-start | bytes 1081344 | tf_op jit(solution)/shard_map/all_to_all | solution.py:399
  37.7 5.7 %collective-permute-start.2 = (bf16[1024,128]{1,0:T(8,128)(2,1)S(1)}, bf16[1024,128]{1,0:T(8,128)(2,1)S(1)}, u32[]{:S(2)}, u32[]{:S(2)}) collective-permute-start(bf16[1024,128]{1,0:T(8,128)(2,1)S(1)} %part.1.mine), channel_id=1, source_target_pairs={{0,4},{4,0},{8,12},{12,8},{16,20},{20,16},{24,28},{28,24},{1,5},{5... | collective-permute-start | bytes 786440 | tf_op jit(solution)/shard_map/ppermute | solution.py:427

commit v9 on v8

--- a/solution.py
+++ b/solution.py
@@ -104,7 +104,7 @@
     widen(basis, basis_w)
     lane_product(
         leaf, basis_w,
-        lambda chunk, c: points[pl.ds(pl.multiple_of((chunk * 8 + c) * vecs, 16), vecs), :], 4, 8, 4,
+        lambda chunk, c: points[pl.ds(pl.multiple_of((chunk * 8 + c) * vecs, 16), vecs), :], 4, 8, 8,
         lambda r, chunk: r * 8 + chunk,
     )
     rounded = leaf[...].astype(BF16)
@@ -117,9 +117,9 @@
 
     def outer(blk, _):
         acc = weighted(
-            8, 32, 16,
-            lambda i, group, u: transfer_w[(group * 16 + u) * 4 + blk, i : i + 1, :],
-            lambda group, u: leaf[group * 16 + u],
+            8, 32, 32,
+            lambda i, group, u: transfer_w[(group * 32 + u) * 4 + blk, i : i + 1, :],
+            lambda group, u: leaf[group * 32 + u],
             [jnp.zeros((vecs, 128), F32)] * 8,
         )
         for i in range(8):
@@ -180,7 +180,7 @@
             source[k, 16 * h : 16 * (h + 1)] = part.reshape(16, 16, 128)
 
     lane_product(
-        pfar, parent_w, lambda chunk, c: source[c % 4, chunk * 2 + c // 4], 2, 16, 4,
+        pfar, parent_w, lambda chunk, c: source[c % 4, chunk * 2 + c // 4], 2, 16, 8,
         lambda r, chunk: r * 16 + chunk,
     )
     lane = iota((256, 128), 1) // 2
@@ -202,7 +202,7 @@
         for i in range(2):
             source[k + i] = got[:, 128 * i : 128 * (i + 1)].reshape(32, 16, 128)
     lane_product(
-        far, coupling_w, lambda chunk, c: source[c % 4, chunk * 2 + c // 4], 4, 16, 4,
+        far, coupling_w, lambda chunk, c: source[c % 4, chunk * 2 + c // 4], 4, 16, 8,
         lambda r, chunk: r * 16 + chunk,
     )
     rows = jnp.concatenate([test[...].astype(F32), jnp.zeros((16, 128 - 32), F32)], axis=1)
@@ -233,9 +233,9 @@
 
     def outer(blk, _):
         acc = weighted(
-            8, 32, 16,
-            lambda i, group, u: basis_w[(group * 16 + u) * 8 + blk, i : i + 1, :],
-            lambda group, u: total_w[group * 16 + u],
+            8, 32, 32,
+            lambda i, group, u: basis_w[(group * 32 + u) * 8 + blk, i : i + 1, :],
+            lambda group, u: total_w[group * 32 + u],
             [jnp.zeros((16, 128), F32)] * 8,
         )
         for i in range(8):
@@ -276,9 +276,9 @@
 
     def outer(blk, _):
         acc = weighted(
-            8, 32, 16,
-            lambda i, group, u: basis_w[(group * 16 + u) * 8 + blk, i : i + 1, :],
-            lambda group, u: compressed[group * 16 + u],
+            8, 32, 32,
+            lambda i, group, u: basis_w[(group * 32 + u) * 8 + blk, i : i + 1, :],
+            lambda group, u: compressed[group * 32 + u],
             [jnp.zeros((32, 128), F32)] * 8,
         )
         square = scale_w[...]
@@ -303,9 +303,9 @@
     for tile in range(4):
         low = 8 * tile
         acc = weighted(
-            8, 64, 16,
-            lambda i, group, u: sketch[group * 16 + u, low + i : low + i + 1, :],
-            lambda group, u: sketch[group * 16 + u, low:32, :],
+            8, 64, 32,
+            lambda i, group, u: sketch[group * 32 + u, low + i : low + i + 1, :],
+            lambda group, u: sketch[group * 32 + u, low:32, :],
             [jnp.zeros((32 - low, 128), F32)] * 8,
         )
         for i in range(8):

time: 48.9 us -> 49.9 us (1.020)
  Pallas kernels: 21.1 us -> 22.4 us
    pallas_call x1, Pallas kernels: 5.03 us -> 5.74 us  [shards(): pl.pallas_call(basis_kernel, out_shape=(jax.ShapeDtypeStruct((64, 32, 128...]
  transfers between devices with their start and end apart: 4 -> 4, of which waited for: 2 -> 2; matrix products, arithmetic and copies ran while one was open for 0% -> 0% of each run, Pallas kernels for 11% -> 12%
where the time goes in v9:
time: 49.9 us; the launch traced here: 49.5 us
  Pallas kernels  22.4 us (45%)
  starting transfers between devices  17 us (34%)
  waiting for transfers between devices  4.98 us (10%)
  local copies, waits for them, and re-layouts  4.34 us (9%)
  between operations  0.77 us (2%)
    pallas_call x1, Pallas kernels, shards(): pl.pallas_call(basis_kernel, out_shape=(jax.ShapeDtypeStruct((64, 32, 128...  5.74 us
    pallas_call x1, Pallas kernels, shards(): pl.pallas_call(far_kernel, out_shape=jax.ShapeDtypeStruct((half, 528, 128...  5.74 us
    ppermute x1, starting transfers between devices, shards(): inner = lax.ppermute(coeff, HOPS, swaps(range(0, peers - 1, 2)))  5.08 us
    pallas_call x1, Pallas kernels, shards(): pl.pallas_call(coeff_kernel, out_shape=jax.ShapeDtypeStruct((768, 128), B...  4.89 us
    ppermute x1, starting transfers between devices, shards(): lax.ppermute(partial, 'vector', [(i, i ^ 1) for i in range(groups)])  4.57 us
    unnamed x16, local copies, waits for them, and re-layouts  4.34 us
    all_to_all x1, starting transfers between devices, shards(): lax.all_to_all(total, 'vector', 0, 0, tiled=True, axis_index_groups=cores)  4.2 us
    pallas_call x1, Pallas kernels, shards(): pl.pallas_call(product_kernel, out_shape=jax.ShapeDtypeStruct((16, 8192),...  4.1 us
  transfers between devices with their start and end apart: 4, of which 2 were waited for; matrix products, arithmetic and copies ran while one was open for 0% of the time, Pallas kernels for 12%

profile of v9, /device:TPU:387, one launch (start us, length us, event | category | flops | bytes accessed | tf_op | source)
XLA Modules:
  0.0 49.5 jit_solution(5842807417317924539)
XLA Ops:
  0.6 0.0 copy-start.5
  0.6 0.0 copy-start.7
  0.7 0.0 copy-start.6
  0.7 4.9 %coeff.1 = bf16[768,128]{1,0:T(8,128)(2,1)} custom-call(bf16[16,8192]{1,0:T(8,128)(2,1)} %samples_at.1, bf16[2048,128]{1,0:T(8,128)(2,1)} %bitcast.4, bf16[1024,128]{1,0:T(8,128)(2,1)} %bitcast.7), custom_call_target="tpu_custom_call" | custom-call | tf_op jit(solution)/shard_map/coeff/pallas_call | solution.py:337
  5.6 3.1 %collective-permute-start.1 = (bf16[768,128]{1,0:T(8,128)(2,1)}, bf16[768,128]{1,0:T(8,128)(2,1)S(1)}, u32[]{:S(2)}, u32[]{:S(2)}) collective-permute-start(bf16[768,128]{1,0:T(8,128)(2,1)} %coeff.1), channel_id=1, source_target_pairs={{1,2},{2,1},{3,32},{32,3},{33,34},{34,33},{35,64},{64,35},{65,66},... | collective-permute-start | bytes 589832 | tf_op jit(solution)/shard_map/ppermute | solution.py:361
  8.7 5.1 %collective-permute-start = (bf16[768,128]{1,0:T(8,128)(2,1)}, bf16[768,128]{1,0:T(8,128)(2,1)S(1)}, u32[]{:S(2)}, u32[]{:S(2)}) collective-permute-start(bf16[768,128]{1,0:T(8,128)(2,1)} %coeff.1), channel_id=1, source_target_pairs={{0,1},{1,0},{2,3},{3,2},{32,33},{33,32},{34,35},{35,34},{64,65},{6... | collective-permute-start | bytes 589832 | tf_op jit(solution)/shard_map/ppermute | solution.py:362
  13.8 0.0 copy-start.1
  13.8 0.9 %copy-done.1 = bf16[32,32,128]{2,1,0:T(8,128)(2,1)S(1)} copy-done((bf16[32,32,128]{2,1,0:T(8,128)(2,1)S(1)}, bf16[32,32,128]{2,1,0:T(8,128)(2,1)}, u32[]{:S(2)}) %copy-start.1) | copy-done | bytes 262168
  14.7 0.0 copy-start.2
  14.7 1.2 %copy-done.2 = bf16[32,32,4,128]{3,2,1,0:T(4,128)(2,1)S(1)} copy-done((bf16[32,32,4,128]{3,2,1,0:T(4,128)(2,1)S(1)}, bf16[32,32,4,128]{3,2,1,0:T(4,128)(2,1)}, u32[]{:S(2)}) %copy-start.2) | copy-done | bytes 1048600
  16.0 0.0 copy-start.3
  16.0 1.2 %copy-done.3 = bf16[32,32,4,64]{3,2,1,0:T(4,128)(2,1)S(1)} copy-done((bf16[32,32,4,64]{3,2,1,0:T(4,128)(2,1)S(1)}, bf16[32,32,4,64]{3,2,1,0:T(4,128)(2,1)}, u32[]{:S(2)}) %copy-start.3) | copy-done | bytes 524312
  17.2 0.0 copy-start.4
  17.2 0.9 %copy-done.4 = bf16[768,128]{1,0:T(8,128)(2,1)S(1)} copy-done((bf16[768,128]{1,0:T(8,128)(2,1)S(1)}, bf16[768,128]{1,0:T(8,128)(2,1)}, u32[]{:S(2)}) %copy-start.4) | copy-done | bytes 196632
  18.1 1.6 %wide.1 = (bf16[768,128]{1,0:T(8,128)(2,1)S(1)}, f32[128,8,128]{2,1,0:T(8,128)S(1)}, f32[512,8,128]{2,1,0:T(8,128)S(1)}, f32[256,8,128]{2,1,0:T(8,128)S(1)}) custom-call(bf16[768,128]{1,0:T(8,128)(2,1)S(1)} %copy-done.4, bf16[1024,128]{1,0:T(8,128)(2,1)S(1)} %bitcast.8, bf16[4096,128]{1,0:T(8,128)(2,1)S(1)} %bitcast.9, bf16[4096,64]{1,0:T(8,128)(2,1)S(1)} %bitcast.10), custom_call_target="tpu_custom_call" | custom-call | flops 10000000 | bytes 1000000 | tf_op jit(solution)/shard_map/wide/pallas_call | solution.py:366
  19.7 0.0 collective-permute-done.1.outer
  19.7 0.0 collective-permute-done.inner
  19.7 0.0 copy-done.5
  19.8 0.0 copy-done.7
  19.8 0.0 copy-done.6
  19.8 0.0 copy-start
  19.8 5.7 %far.1.total = bf16[4,528,128]{2,1,0:T(8,128)(2,1)} custom-call(bf16[768,128]{1,0:T(8,128)(2,1)S(1)} %get-tuple-element.11.own, bf16[768,128]{1,0:T(8,128)(2,1)S(1)} %collective-permute-done.inner, bf16[768,128]{1,0:T(8,128)(2,1)S(1)} %collective-permute-done.1.outer, f32[128,8,128]{2,1,0:T(8,128)S(1)} %get-tuple-element.12.transfer_w, ...), custom_call_target="tpu_custom_call" | custom-call | tf_op jit(solution)/shard_map/far/pallas_call | solution.py:381
  25.5 4.2 %all-to-all-start = ((bf16[4,528,128]{2,1,0:T(8,128)(2,1)}), bf16[4,528,128]{2,1,0:T(8,128)(2,1)S(1)}, u32[]{:S(2)}, u32[]{:S(2)}) async-start(bf16[4,528,128]{2,1,0:T(8,128)(2,1)} %far.1.total), calls=%async_computation | async-start | bytes 1081344 | tf_op jit(solution)/shard_map/all_to_all | solution.py:399
  29.7 0.0 copy-done
  29.7 4.1 %product.1 = bf16[16,8192]{1,0:T(8,128)(2,1)} custom-call(bf16[4,528,128]{2,1,0:T(8,128)(2,1)} %far.1.total, bf16[2048,128]{1,0:T(8,128)(2,1)S(1)} %bitcast.5), custom_call_target="tpu_custom_call" | custom-call | flops 10000000 | bytes 1000000 | tf_op jit(solution)/shard_map/product/pallas_call | solution.py:401
  33.8 3.8 %all-to-all-done.totals = bf16[4,528,128]{2,1,0:T(8,128)(2,1)S(1)} async-done(((bf16[4,528,128]{2,1,0:T(8,128)(2,1)}), bf16[4,528,128]{2,1,0:T(8,128)(2,1)S(1)}, u32[]{:S(2)}, u32[]{:S(2)}) %all-to-all-start) | async-done | bytes 540704 | tf_op jit(solution)/shard_map/all_to_all | solution.py:399
  37.7 0.3 part.1.mine
  38.0 4.6 %collective-permute-start.2 = (bf16[1024,128]{1,0:T(8,128)(2,1)S(1)}, bf16[1024,128]{1,0:T(8,128)(2,1)S(1)}, u32[]{:S(2)}, u32[]{:S(2)}) collective-permute-start(bf16[1024,128]{1,0:T(8,128)(2,1)S(1)} %part.1.mine), channel_id=1, source_target_pairs={{0,4},{4,0},{8,12},{12,8},{16,20},{20,16},{24,28},{28,24},{1,5},{5... | collective-permute-start | bytes 786440 | tf_op jit(solution)/shard_map/ppermute | solution.py:427
  42.6 1.1 %collective-permute-done.2.theirs = bf16[1024,128]{1,0:T(8,128)(2,1)S(1)} collective-permute-done((bf16[1024,128]{1,0:T(8,128)(2,1)S(1)}, bf16[1024,128]{1,0:T(8,128)(2,1)S(1)}, u32[]{:S(2)}, u32[]{:S(2)}) %collective-permute-start.2) | collective-permute-done | bytes 262176 | tf_op jit(solution)/shard_map/ppermute | solution.py:427
  43.7 5.7 %basis.1 = (f32[64,32,128]{2,1,0:T(8,128)}, f32[32,32,128]{2,1,0:T(8,128)}) custom-call(bf16[1024,128]{1,0:T(8,128)(2,1)S(1)} %part.1.mine, bf16[1024,128]{1,0:T(8,128)(2,1)S(1)} %collective-permute-done.2.theirs, bf16[2048,128]{1,0:T(8,128)(2,1)S(1)} %bitcast.6), custom_call_target="tpu_custom_call" | custom-call | tf_op jit(solution)/shard_map/basis/pallas_call | solution.py:429
Async XLA Ops:
  0.6 19.1 %copy-start.5 = (bf16[16,32]{1,0:T(8,128)(2,1)S(1)}, bf16[16,32]{1,0:T(8,128)(2,1)}, u32[]{:S(2)}) copy-start(bf16[16,32]{1,0:T(8,128)(2,1)} %test.1) | copy-start | bytes 3076
  0.6 19.1 %copy-start.7 = (s32[4,64]{1,0:T(4,128)S(1)}, s32[4,64]{1,0:T(4,128)}, u32[]{:S(2)}) copy-start(s32[4,64]{1,0:T(4,128)} %parent_lists.1) | copy-start | bytes 3076
  0.7 19.1 %copy-start.6 = (s32[4,128]{1,0:T(4,128)S(1)}, s32[4,128]{1,0:T(4,128)}, u32[]{:S(2)}) copy-start(s32[4,128]{1,0:T(4,128)} %leaf_lists.1) | copy-start | bytes 6148
  5.6 14.2 %collective-permute-start.1 = (bf16[768,128]{1,0:T(8,128)(2,1)}, bf16[768,128]{1,0:T(8,128)(2,1)S(1)}, u32[]{:S(2)}, u32[]{:S(2)}) collective-permute-start(bf16[768,128]{1,0:T(8,128)(2,1)} %coeff.1), channel_id=1, source_target_pairs={{1,2},{2,1},{3,32},{32,3},{33,34},{34,33},{35,64},{64,35},{65,66},... | collective-permute-start | bytes 589832 | tf_op jit(solution)/shard_map/ppermute | solution.py:361
  8.7 11.0 %collective-permute-start = (bf16[768,128]{1,0:T(8,128)(2,1)}, bf16[768,128]{1,0:T(8,128)(2,1)S(1)}, u32[]{:S(2)}, u32[]{:S(2)}) collective-permute-start(bf16[768,128]{1,0:T(8,128)(2,1)} %coeff.1), channel_id=1, source_target_pairs={{0,1},{1,0},{2,3},{3,2},{32,33},{33,32},{34,35},{35,34},{64,65},{6... | collective-permute-start | bytes 589832 | tf_op jit(solution)/shard_map/ppermute | solution.py:362
  13.8 1.0 %copy-start.1 = (bf16[32,32,128]{2,1,0:T(8,128)(2,1)S(1)}, bf16[32,32,128]{2,1,0:T(8,128)(2,1)}, u32[]{:S(2)}) copy-start(bf16[32,32,128]{2,1,0:T(8,128)(2,1)} %param.10) | copy-start | bytes 786436
  14.7 1.2 %copy-start.2 = (bf16[32,32,4,128]{3,2,1,0:T(4,128)(2,1)S(1)}, bf16[32,32,4,128]{3,2,1,0:T(4,128)(2,1)}, u32[]{:S(2)}) copy-start(bf16[32,32,4,128]{3,2,1,0:T(4,128)(2,1)} %param.12) | copy-start | bytes 3145732
  16.0 1.2 %copy-start.3 = (bf16[32,32,4,64]{3,2,1,0:T(4,128)(2,1)S(1)}, bf16[32,32,4,64]{3,2,1,0:T(4,128)(2,1)}, u32[]{:S(2)}) copy-start(bf16[32,32,4,64]{3,2,1,0:T(4,128)(2,1)} %param.14) | copy-start | bytes 1572868
  17.2 0.9 %copy-start.4 = (bf16[768,128]{1,0:T(8,128)(2,1)S(1)}, bf16[768,128]{1,0:T(8,128)(2,1)}, u32[]{:S(2)}) copy-start(bf16[768,128]{1,0:T(8,128)(2,1)} %coeff.1) | copy-start | bytes 589828
  19.8 10.0 %copy-start = (bf16[32,64,128]{2,1,0:T(8,128)(2,1)S(1)}, bf16[32,64,128]{2,1,0:T(8,128)(2,1)}, u32[]{:S(2)}) copy-start(bf16[32,64,128]{2,1,0:T(8,128)(2,1)} %param.9) | copy-start | bytes 1572868
  25.5 12.1 %all-to-all-start = ((bf16[4,528,128]{2,1,0:T(8,128)(2,1)}), bf16[4,528,128]{2,1,0:T(8,128)(2,1)S(1)}, u32[]{:S(2)}, u32[]{:S(2)}) async-start(bf16[4,528,128]{2,1,0:T(8,128)(2,1)} %far.1.total), calls=%async_computation | async-start | bytes 1081344 | tf_op jit(solution)/shard_map/all_to_all | solution.py:399
  38.0 5.7 %collective-permute-start.2 = (bf16[1024,128]{1,0:T(8,128)(2,1)S(1)}, bf16[1024,128]{1,0:T(8,128)(2,1)S(1)}, u32[]{:S(2)}, u32[]{:S(2)}) collective-permute-start(bf16[1024,128]{1,0:T(8,128)(2,1)S(1)} %part.1.mine), channel_id=1, source_target_pairs={{0,4},{4,0},{8,12},{12,8},{16,20},{20,16},{24,28},{28,24},{1,5},{5... | collective-permute-start | bytes 786440 | tf_op jit(solution)/shard_map/ppermute | solution.py:427
